TPU v7x, 32 devices: a whole 2x2x4 slice. The times are simulated.
32 devices in a mesh: dp: 8 (over z, y), tensor: 4 (over x, core).
Axes of the slice: x: 2, y: 2, z: 4, core: 2. Of those that a mesh axis runs over, the one named last changes fastest.
Arguments:
- tokens: bfloat16 [1024, 2048], P('dp'), may hold values from -6 to 6
- lengths: int32 [8], replicated, may hold values from 96 to 128, as said below
- request_adapter: int32 [8], replicated, may hold values from 0 to 63
- token_experts: int32 [1024, 8], P('dp'), may hold values from 0 to 63, as said below
- router_weight: float32 [1024, 8], P('dp'), may hold values from 0.05 to 1
- gate_weight: bfloat16 [128, 2048, 512], P('dp', None, 'tensor'), may hold values from -0.125 to 0.125
- up_weight: bfloat16 [128, 2048, 512], P('dp', None, 'tensor'), may hold values from -0.125 to 0.125
- down_weight: bfloat16 [128, 2048, 512], P('dp', None, 'tensor'), may hold values from -0.1875 to 0.1875
- adapter_input_maps: bfloat16 [2048, 2048], P('tensor', 'dp'), may hold values from -0.125 to 0.125
- adapter_output_maps: bfloat16 [2048, 2, 512], P('dp', None, 'tensor'), may hold values from -1.5 to 1.5
Outputs:
- moe_output: bfloat16 [1024, 2048], P('dp', 'tensor')
Inputs may be any that keep to these rules, and one draw needn't show every extreme that they name: `token_experts`: each row names 8 different experts. Among the rows of one request window, each expert is named by at most 28 rows, and one expert, the same in every window, is named by exactly 28 rows, all of live tokens. `lengths`: some request has all 128 tokens live.
All inputs are finite; a program needn't handle non-finite values.
Results may differ from a plain program's by a relative error of at most 0.0065.
Values may be sent and summed in bfloat16 or wider, within the bound.
No kernel may reach another device: no remote copies, remote signals or barrier semaphores. Data moves between devices by JAX's collectives and lax.ppermute only.
A program may use at most 320 MiB of HBM per device.

v0:
```python
import jax
import jax.numpy as jnp
from jax import lax
from jax.sharding import PartitionSpec as P

ADAPTER_RANK = 16
CAP = 28


def combine_routes(unit_table, lower_slot, shift_half, route_gain, tok_rows, topk):
    lower_slot = lower_slot.reshape(tok_rows, topk)
    route_gain = route_gain.reshape(tok_rows, topk)
    pair_slots = jnp.stack([lower_slot, lower_slot + shift_half], axis=2)
    pair_rows = unit_table[pair_slots].astype(jnp.float32)
    summed_pair = jnp.sum(pair_rows, axis=2)
    return jnp.sum(summed_pair * route_gain[:, :, None], axis=1)


def per_device(
    tokens,
    lengths,
    request_adapter,
    token_experts,
    router_weight,
    gate_weight,
    up_weight,
    down_weight,
    adapter_input_maps,
    adapter_output_maps,
):
    tok_rows, width = tokens.shape
    topk = token_experts.shape[1]
    dp_count = lax.axis_size("dp")
    tp_count = lax.axis_size("tensor")
    units_local = gate_weight.shape[0]
    experts_all = units_local * dp_count // 2
    quarter = CAP // tp_count
    double_rank = 2 * ADAPTER_RANK
    row_index = lax.axis_index("dp")
    part_index = lax.axis_index("tensor")
    live_mask = jnp.arange(tok_rows) < lengths[row_index]
    adapter = request_adapter[row_index]
    width_part = width // tp_count
    x_part = lax.dynamic_slice_in_dim(tokens, part_index * width_part, width_part, 1)
    device_portion = lax.all_gather(adapter_input_maps, "dp", axis=1, tiled=True)
    columns = jnp.arange(device_portion.shape[1])
    selector = (
        columns[:, None] == adapter * double_rank + jnp.arange(double_rank)[None, :]
    ).astype(jnp.bfloat16)
    chosen = jnp.dot(device_portion, selector, preferred_element_type=jnp.float32)
    partial_z = jnp.dot(x_part, chosen.astype(jnp.bfloat16), preferred_element_type=jnp.float32)
    low_rank = lax.psum(partial_z, "tensor").astype(jnp.bfloat16)
    entries = tok_rows * topk
    flat_ids = token_experts.reshape(entries)
    entry_token = jnp.arange(entries) // topk
    entry_live = live_mask[entry_token]
    expert_hits = (
        (flat_ids[:, None] == jnp.arange(experts_all)[None, :]) & entry_live[:, None]
    ).astype(jnp.int32)
    position = jnp.sum(jnp.cumsum(expert_hits, axis=0) * expert_hits, axis=1) - 1
    entry_mine = entry_live & (position // quarter == part_index)
    empty_slot = experts_all * quarter
    slot_part = jnp.where(entry_mine, flat_ids * quarter + position % quarter, empty_slot)
    slot_token = (
        jnp.full((empty_slot + 1,), tok_rows, jnp.int32).at[slot_part].set(entry_token)[:empty_slot]
    )
    padded_x = jnp.concatenate([tokens, jnp.zeros((1, width), jnp.bfloat16)], axis=0)
    padded_z = jnp.concatenate([low_rank, jnp.zeros((1, double_rank), jnp.bfloat16)], axis=0)
    slot_rows = padded_x[slot_token]
    slot_low = padded_z[slot_token]
    send_rows = jnp.concatenate([slot_rows, slot_rows], axis=0).reshape(
        dp_count, units_local, quarter, width
    )
    send_low = jnp.concatenate([slot_low, slot_low], axis=0).reshape(
        dp_count, units_local, quarter, double_rank
    )
    recv_rows, recv_low = (
        lax.all_to_all(send_rows, "dp", split_axis=0, concat_axis=0, tiled=True),
        lax.all_to_all(send_low, "dp", split_axis=0, concat_axis=0, tiled=True),
    )
    every_table = lax.all_gather(adapter_output_maps, "dp", axis=0, tiled=True)
    unit_half = (row_index * units_local + jnp.arange(units_local)) // experts_all
    half_tables = jnp.moveaxis(jnp.take(every_table, unit_half, axis=1), 1, 0)
    source_rows = (
        request_adapter[:, None] * double_rank + jnp.arange(double_rank)[None, :]
    ).reshape(dp_count * double_rank)
    source_tables = jnp.take(half_tables, source_rows, axis=1)
    gate_piece = lax.all_gather(gate_weight, "tensor", axis=2, tiled=True)
    up_piece = lax.all_gather(up_weight, "tensor", axis=2, tiled=True)
    table_piece = lax.all_gather(source_tables, "tensor", axis=2, tiled=True)
    table_split = table_piece.reshape(units_local, dp_count, double_rank, table_piece.shape[2])
    gate_term = jnp.einsum(
        "slcd,ldk->slck", recv_rows, gate_piece, preferred_element_type=jnp.float32
    )
    gate_term = gate_term + jnp.einsum(
        "slcj,lsjk->slck",
        recv_low[..., :ADAPTER_RANK],
        table_split[:, :, :ADAPTER_RANK],
        preferred_element_type=jnp.float32,
    )
    up_term = jnp.einsum("slcd,ldk->slck", recv_rows, up_piece, preferred_element_type=jnp.float32)
    up_term = up_term + jnp.einsum(
        "slcj,lsjk->slck",
        recv_low[..., ADAPTER_RANK:],
        table_split[:, :, ADAPTER_RANK:],
        preferred_element_type=jnp.float32,
    )
    hidden = (jax.nn.silu(gate_term) * up_term).astype(jnp.bfloat16)
    down_whole = lax.all_gather(down_weight, "tensor", axis=2, tiled=True)
    unit_output = jnp.einsum(
        "slck,ldk->slcd", hidden, down_whole, preferred_element_type=jnp.float32
    ).astype(jnp.bfloat16)
    weights_flat = router_weight.reshape(entries)
    returned = lax.all_to_all(unit_output, "dp", split_axis=0, concat_axis=0, tiled=True)
    unit_table = returned.reshape(2 * experts_all * quarter, width)
    lower_slot = jnp.where(entry_mine, slot_part, 0)
    route_gain = jnp.where(entry_mine, weights_flat, 0.0)
    combined = combine_routes(
        unit_table, lower_slot, experts_all * quarter, route_gain, tok_rows, topk
    )
    summed = lax.psum_scatter(combined, "tensor", scatter_dimension=1, tiled=True)
    return summed.astype(jnp.bfloat16)


def solution(mesh):
    in_specs = (
        P("dp", None),
        P(),
        P(),
        P("dp", None),
        P("dp", None),
        P("dp", None, "tensor"),
        P("dp", None, "tensor"),
        P("dp", None, "tensor"),
        P("tensor", "dp"),
        P("dp", None, "tensor"),
    )
    out_specs = P("dp", "tensor")
    return jax.shard_map(
        per_device, mesh=mesh, in_specs=in_specs, out_specs=out_specs, check_vma=False
    )
```

profile of v0, /device:TPU:0, one launch (start us, length us, event | category | flops | bytes accessed | tf_op | source)
XLA Modules:
  0.0 988.5 jit_solution(2396284120542666581)
XLA Ops:
  9.9 42.5 %all-gather.11.cloned.1.call-done = bf16[2048,2,128]{2,0,1:T(8,128)(2,1)} async-done(((bf16[256,2,128]{2,0,1:T(8,128)(2,1)}), bf16[2048,2,128]{2,0,1:T(8,128)(2,1)}) %all-gather.11.cloned.1.call-update) | async-done | bytes 1048592 | tf_op jit(solution)/shard_map/all_gather | solution.py:81
  52.5 5.7 gather_fusion.3
  58.2 7.6 broadcast_select_fusion
  65.8 10.3 %copy.137 = bf16[16,2048,128]{2,0,1:T(8,128)(2,1)} copy(bf16[16,2048,128]{2,1,0:T(8,128)(2,1)} %broadcast_select_fusion) | data formatting | bytes 16777216 | tf_op jit(solution)/shard_map/jit(_take)/select_n | solution.py:83
  76.1 4.2 gather_fusion.4
  86.1 6.5 gather_fusion
  92.8 18.0 %reduce-window.6 = s32[64,8,128]{2,1,0:T(8,128)S(1)} reduce-window(s32[64,8,128]{2,1,0:T(8,128)S(1)} %fusion.29, s32[]{:T(128)} %constant.103.clone.1), window={size=1x1x128 pad=0_0x0_0x127_0}, to_apply=%region_0.0 | reduce-window | flops 8323072 | bytes 524292 | tf_op jit(solution)/shard_map/reduce-window
  112.8 4.3 scatter_custom_fusion
  122.0 11.2 %psum.7 = bf16[128,32]{0,1:T(8,128)(2,1)S(1)} all-reduce(f32[128,32]{0,1:T(8,128)S(1)} %fusion.16), channel_id=1, replica_groups=mesh['dp'=8,'tensor'=4] {'tensor'}, use_global_device_ids=true, to_apply=%region_4.5 | all-reduce | flops 4096 | bytes 24576 | tf_op jit(solution)/shard_map/psum | solution.py:52
  135.9 3.5 all-to-all-start.1
  141.6 6.1 reshape.409
  147.7 8.0 copy.130
  155.8 6.0 all-to-all-start
  162.1 3.6 fusion.44
  170.8 72.0 %all-to-all-done = bf16[8,16,7,2048]{3,1,2,0:T(8,128)(2,1)} async-done(((bf16[8,16,7,2048]{3,1,2,0:T(8,128)(2,1)}), bf16[8,16,7,2048]{3,1,2,0:T(8,128)(2,1)}, u32[]{:S(2)}, u32[]{:S(2)}) %all-to-all-start) | async-done | bytes 3670048 | tf_op jit(solution)/shard_map/all_to_all | solution.py:78
  242.8 104.2 %all-gather.7.cloned.1.call-done = bf16[16,2048,512]{2,1,0:T(8,128)(2,1)} async-done(((bf16[16,2048,128]{2,1,0:T(8,128)(2,1)}), bf16[16,2048,512]{2,1,0:T(8,128)(2,1)}) %all-gather.7.cloned.1.call-update) | async-done | bytes 33554448 | tf_op jit(solution)/shard_map/all_gather | solution.py:88
  347.0 19.5 %fusion.4 = f32[16,8,7,512]{3,1,2,0:T(8,128)S(1)} fusion(bf16[16,2048,512]{2,1,0:T(8,128)(2,1)} %all-gather.7.cloned.1.call-done, bf16[8,16,7,2048]{3,1,2,0:T(8,128)(2,1)} %all-to-all-done), kind=kOutput, calls=%fused_computation.11 | convolution fusion | flops 1879048192 | bytes 39059456 | tf_op jit(solution)/shard_map/slcd,ldk->slck/dot_general | solution.py:92
  366.5 187.9 %all-gather.15.cloned.1.call-done = bf16[16,2048,512]{2,1,0:T(8,128)(2,1)} async-done(((bf16[16,2048,128]{2,1,0:T(8,128)(2,1)}), bf16[16,2048,512]{2,1,0:T(8,128)(2,1)}) %all-gather.15.cloned.1.call-update) | async-done | bytes 33554448 | tf_op jit(solution)/shard_map/all_gather | solution.py:89
  554.5 23.0 %fusion.2 = f32[16,8,7,512]{3,1,2,0:T(8,128)} fusion(bf16[16,2048,512]{2,1,0:T(8,128)(2,1)} %all-gather.15.cloned.1.call-done, bf16[8,16,7,2048]{3,1,2,0:T(8,128)(2,1)} %all-to-all-done), kind=kOutput, calls=%fused_computation.9 | convolution fusion | flops 1879048192 | bytes 39059456 | tf_op jit(solution)/shard_map/slcd,ldk->slck/dot_general | solution.py:101
  577.5 7.7 fusion.15
  585.2 176.8 %all-gather.17.cloned.1.call-done = bf16[16,2048,512]{2,1,0:T(8,128)(2,1)} async-done(((bf16[16,2048,128]{2,1,0:T(8,128)(2,1)}), bf16[16,2048,512]{2,1,0:T(8,128)(2,1)}) %all-gather.17.cloned.1.call-update) | async-done | bytes 33554448 | tf_op jit(solution)/shard_map/all_gather | solution.py:109
  762.0 17.3 %convert_bitcast_fusion = bf16[8,16,7,2048]{3,0,2,1:T(8,128)(2,1)} fusion(bf16[16,2048,512]{2,1,0:T(8,128)(2,1)} %all-gather.17.cloned.1.call-done, bf16[8,16,7,512]{3,1,2,0:T(8,128)(2,1)S(1)} %fusion.15), kind=kOutput, calls=%fused_computation.16 | convolution fusion | flops 1880883200 | bytes 38141952 | tf_op jit(solution)/shard_map/slck,ldk->slcd/dot_general | solution.py:110
  779.2 5.9 copy.147
  785.1 5.5 all-to-all-start.2
  791.3 81.7 %all-to-all-done.2 = bf16[8,16,7,2048]{3,1,2,0:T(8,128)(2,1)} async-done(((bf16[8,16,7,2048]{3,1,2,0:T(8,128)(2,1)}), bf16[8,16,7,2048]{3,1,2,0:T(8,128)(2,1)}, u32[]{:S(2)}, u32[]{:S(2)}) %all-to-all-start.2) | async-done | bytes 3670048 | tf_op jit(solution)/shard_map/all_to_all | solution.py:114
  873.1 6.4 copy.148
  879.5 6.3 reshape.412
  885.8 18.9 %gather_fusion.5 = bf16[2048,2048]{1,0:T(8,128)(2,1)} fusion(bf16[896,2048]{1,0:T(8,128)(2,1)} %reshape.412, s32[2048]{0:T(1024)S(1)} %broadcast_clamp_fusion), kind=kCustom, calls=%fused_computation.5 | custom fusion | bytes 16785408 | tf_op jit(solution)/shard_map/gather | solution.py:14
  904.7 18.1 %reshape.472 = f32[128,8,2,2048]{3,2,1,0:T(2,128)} reshape(bf16[2048,2048]{1,0:T(8,128)(2,1)} %gather_fusion.5) | data formatting | bytes 25165824 | tf_op jit(solution)/shard_map/convert_element_type | solution.py:14
  922.8 26.2 %reduce_sum.28 = f32[128,8,2048]{2,1,0:T(8,128)} reduce(f32[128,8,2,2048]{3,2,1,0:T(2,128)} %reshape.472, f32[]{:T(128)} %constant.125.clone.1), dimensions={2}, to_apply=%region_5.6 | reduce | flops 2097152 | bytes 25165828 | tf_op jit(solution)/shard_map/reduce_sum | solution.py:15
  949.0 7.4 multiply_reduce_fusion
  956.4 23.1 %reduce-scatter.2.cloned.1.call-done = f32[128,512]{1,0:T(8,128)} async-done(((f32[128,2048]{1,0:T(8,128)}), f32[128,512]{1,0:T(8,128)}) %reduce-scatter.2.cloned.1.call-update) | async-done | bytes 262160 | tf_op jit(solution)/shard_map/reduce_scatter | solution.py:121
  (92 shorter events, 28.0 us)
Async XLA Ops:
  6.5 45.9 %all-gather.11.cloned.1.call-start = ((), (), s32[]{:S(2)}) async-start(), calls=%async_computation.6 | async-start | bytes 1179648 | tf_op jit(solution)/shard_map/all_gather | solution.py:81
  8.1 111.5 %all-gather.9.cloned.1.call-start = ((), (), s32[]{:S(2)}) async-start(), calls=%async_computation.5 | async-start | bytes 2359296 | tf_op jit(solution)/shard_map/all_gather | solution.py:45
  8.9 153.2 %all-gather.13.cloned.1.call-start = ((), (), s32[]{:S(2)}) async-start(), calls=%async_computation.7 | async-start | bytes 5242880 | tf_op jit(solution)/shard_map/all_gather | solution.py:90
  82.1 264.9 %all-gather.7.cloned.1.call-start = ((), (), s32[]{:S(2)}) async-start(), calls=%async_computation.4 | async-start | bytes 41943040 | tf_op jit(solution)/shard_map/all_gather | solution.py:88
  82.7 471.8 %all-gather.15.cloned.1.call-start = ((), (), s32[]{:S(2)}) async-start(), calls=%async_computation.8 | async-start | bytes 41943040 | tf_op jit(solution)/shard_map/all_gather | solution.py:89
  83.3 0.7 copy-start.1
  83.3 1.0 copy-start.3
  83.3 1.6 copy-start.4
  83.3 678.7 %all-gather.17.cloned.1.call-start = ((), (), s32[]{:S(2)}) async-start(), calls=%async_computation.9 | async-start | bytes 41943040 | tf_op jit(solution)/shard_map/all_gather | solution.py:109
  84.0 27.8 %copy-start.2 = (f32[128,8]{0,1:T(8,128)S(1)}, f32[128,8]{0,1:T(8,128)}, u32[]{:S(2)}) copy-start(f32[128,8]{0,1:T(8,128)} %param.14) | copy-start | bytes 12292
  84.0 28.7 %copy-start = (bf16[128,2048]{1,0:T(8,128)(2,1)S(1)}, bf16[128,2048]{1,0:T(8,128)(2,1)}, u32[]{:S(2)}) copy-start(bf16[128,2048]{1,0:T(8,128)(2,1)} %param.10) | copy-start | bytes 1572868
  135.9 19.9 %all-to-all-start.1 = ((bf16[8,2,1792]{2,1,0:T(2,128)(2,1)}), bf16[8,2,1792]{2,1,0:T(2,128)(2,1)S(1)}, u32[]{:S(2)}, u32[]{:S(2)}) async-start(bf16[8,2,1792]{2,1,0:T(2,128)(2,1)} %reshape.478), calls=%async_computation.1 | async-start | bytes 114688 | tf_op jit(solution)/shard_map/all_to_all | solution.py:79
  155.8 87.1 %all-to-all-start = ((bf16[8,16,7,2048]{3,1,2,0:T(8,128)(2,1)}), bf16[8,16,7,2048]{3,1,2,0:T(8,128)(2,1)}, u32[]{:S(2)}, u32[]{:S(2)}) async-start(bf16[8,16,7,2048]{3,1,2,0:T(8,128)(2,1)} %copy.130), calls=%async_computation | async-start | bytes 7340032 | tf_op jit(solution)/shard_map/all_to_all | solution.py:78
  785.1 88.0 %all-to-all-start.2 = ((bf16[8,16,7,2048]{3,1,2,0:T(8,128)(2,1)}), bf16[8,16,7,2048]{3,1,2,0:T(8,128)(2,1)}, u32[]{:S(2)}, u32[]{:S(2)}) async-start(bf16[8,16,7,2048]{3,1,2,0:T(8,128)(2,1)} %copy.147), calls=%async_computation.2 | async-start | bytes 7340032 | tf_op jit(solution)/shard_map/all_to_all | solution.py:114
  790.6 189.0 %reduce-scatter.2.cloned.1.call-start = ((), (), s32[]{:S(2)}) async-start(), calls=%async_computation.10 | async-start | bytes 1310720 | tf_op jit(solution)/shard_map/reduce_scatter | solution.py:121
Sparse Core Ops, SparseCore 0:
  9.5 42.8 all-gather.10
  54.5 49.8 all-gather.8
  106.0 33.4 all-gather.12
  140.9 206.0 all-gather.6
  348.4 206.0 all-gather.14
  555.9 206.0 all-gather.16
  956.6 22.9 reduce-scatter.1
where the time goes:
time: 997 us; the launch traced here: 989 us
  waiting for transfers between devices  691 us (69%)
  local copies, waits for them, and re-layouts  115 us (12%)
  other arithmetic  74.5 us (7%)
  matrix products  67.3 us (7%)
  starting transfers between devices  15.3 us (2%)
  between operations  15 us (2%)
  blocking collectives  11.2 us (1%)
    all_gather x1, waiting for transfers between devices, per_device(): up_piece = lax.all_gather(up_weight, 'tensor', axis=2, tiled=True)  188 us
    all_gather x1, waiting for transfers between devices, per_device(): down_whole = lax.all_gather(down_weight, 'tensor', axis=2, tiled=True)  177 us
    all_gather x1, waiting for transfers between devices, per_device(): gate_piece = lax.all_gather(gate_weight, 'tensor', axis=2, tiled=True)  104 us
    all_to_all x1, waiting for transfers between devices, per_device(): lax.all_to_all(unit_output, 'dp', split_axis=0, concat_axis=0, tiled=True)  81.7 us
    all_to_all x1, waiting for transfers between devices, per_device(): lax.all_to_all(send_rows, 'dp', split_axis=0, concat_axis=0, tiled=True)  72 us
    all_gather x1, waiting for transfers between devices, per_device(): every_table = lax.all_gather(adapter_output_maps, 'dp', axis=0, tiled=True)  42.5 us
    reduce_sum x1, other arithmetic, combine_routes(): summed_pair = jnp.sum(pair_rows, axis=2)  26.2 us
    reduce_scatter x1, waiting for transfers between devices, per_device(): lax.psum_scatter(combined, 'tensor', scatter_dimension=1, tiled=True)  23.1 us
  transfers between devices with their start and end apart: 10, of which 7 were waited for; matrix products, arithmetic and copies ran while one was open for 15% of the time, Pallas kernels for 0%

commit v1 on v0

v1 whole, which is shorter than its diff:
```python
import functools

import jax
import jax.numpy as jnp
from jax import lax
from jax.experimental import pallas as pl
from jax.experimental.pallas import tpu as pltpu
from jax.sharding import PartitionSpec as P

ADAPTER_RANK = 16
DOUBLE_RANK = 2 * ADAPTER_RANK
CAP = 28
SLOT = 32
GROUP = 8
BF16 = jnp.bfloat16
F32 = jnp.float32
VMEM_BYTES = 56 * 1024 * 1024
ORDER = (0, 2, 4, 6, 1, 3, 5, 7)


def params(**more):
    return pltpu.CompilerParams(vmem_limit_bytes=VMEM_BYTES, **more)


def full_spec(shape):
    return pl.BlockSpec(shape, lambda *_: (0,) * len(shape))


def slots_kernel(units, scalar_ref, *refs):
    metas, (pick_ref, place_ref, gain_ref) = refs[:-3], refs[-3:]
    metas = [m.at[n] for m in metas for n in range(m.shape[0])]
    rows = max(units, 8)
    topk = metas[0].shape[0]
    tokens = metas[0].shape[1] // 4
    first = scalar_ref[0]
    expert = (lax.broadcasted_iota(jnp.int32, (rows, tokens), 0) + first).astype(F32)
    token = lax.broadcasted_iota(jnp.int32, (rows, tokens), 1)
    slot = lax.broadcasted_iota(jnp.int32, (units, SLOT, tokens), 1).astype(F32)
    before = (
        lax.broadcasted_iota(jnp.int32, (tokens, tokens), 0)
        < lax.broadcasted_iota(jnp.int32, (tokens, tokens), 1)
    ).astype(BF16)
    for r in range(GROUP):
        live = token < scalar_ref[1 + r]
        meta = metas[r][...].astype(F32)
        ids = meta[:, :tokens]
        weights = meta[:, tokens : 2 * tokens] + meta[:, 2 * tokens : 3 * tokens] + meta[:, 3 * tokens :]
        hit = jnp.zeros((rows, tokens), F32)
        gain = jnp.zeros((rows, tokens), F32)
        for k in range(topk):
            same = jnp.broadcast_to(ids[k : k + 1], (rows, tokens)) == expert
            hit = hit + jnp.where(same, 1.0, 0.0)
            gain = gain + jnp.where(same, jnp.broadcast_to(weights[k : k + 1], (rows, tokens)), 0.0)
        hit = jnp.where(live, hit, 0.0)
        position = jnp.dot(hit.astype(BF16), before, preferred_element_type=F32)
        position = jnp.where(hit > 0.5, position, -1.0)[:units]
        pick = jnp.where(jnp.broadcast_to(position[:, None, :], slot.shape) == slot, 1.0, 0.0)
        gains = jnp.sum(pick * gain[:units][:, None, :], axis=2, keepdims=True)
        gain_ref[:, r * SLOT : (r + 1) * SLOT, :] = jnp.broadcast_to(gains, (units, SLOT, 128))
        pick = pick.reshape(units * SLOT, tokens)
        pick_ref[r] = pick.astype(BF16)
        place_ref[r] = pick.T.astype(BF16)


def make_slots(metas, specs, tokens, first_expert, lengths_rel, units):
    scalars = jnp.concatenate([first_expert[None], lengths_rel]).astype(jnp.int32)
    slots = units * SLOT
    return pl.pallas_call(
        functools.partial(slots_kernel, units),
        grid_spec=pltpu.PrefetchScalarGridSpec(
            num_scalar_prefetch=1,
            grid=(1,),
            in_specs=specs,
            out_specs=[
                full_spec((GROUP, slots, tokens)),
                full_spec((GROUP, tokens, slots)),
                full_spec((units, GROUP * SLOT, 128)),
            ],
        ),
        out_shape=[
            jax.ShapeDtypeStruct((GROUP, slots, tokens), BF16),
            jax.ShapeDtypeStruct((GROUP, tokens, slots), BF16),
            jax.ShapeDtypeStruct((units, GROUP * SLOT, 128), F32),
        ],
        compiler_params=params(),
        cost_estimate=pl.CostEstimate(flops=100_000_000, bytes_accessed=4_500_000, transcendentals=0),
    )(scalars, *metas)


def expand_kernel(units, block, quarters, layout, final, scalar_ref, *refs):
    count = len(layout)
    groups, refs = refs[: quarters * count], refs[quarters * count :]
    if final:
        pick_ref, gate_ref, up_ref, start_ref, low_ref, table_ref = refs[:6]
        hidden_ref, gathered, total = refs[6:]
    else:
        pick_ref, gate_ref, up_ref = refs[:3]
        total, gathered = refs[3:]
    q, b = pl.program_id(0), pl.program_id(1)
    tokens, wide = pick_ref.shape[2], gathered.shape[2]
    for turn in range(quarters):

        @pl.when(jnp.logical_and(q == turn, b == 0))
        def _(turn=turn):
            for source, places in zip(groups[turn * count : (turn + 1) * count], layout, strict=True):
                for n, r in enumerate(places):
                    block_rows = source[n] if len(source.shape) == 3 else source[...]
                    rows = jnp.dot(pick_ref[r], block_rows[:tokens], preferred_element_type=F32)
                    gathered[:, r * SLOT : (r + 1) * SLOT, :] = rows.astype(BF16).reshape(units, SLOT, wide)

    if final:

        @pl.when(jnp.logical_and(q == 0, b == 0))
        def _():
            for r in range(GROUP):
                low = lax.dot_general(
                    pick_ref[r], low_ref[r], (((1,), (1,)), ((), ())), preferred_element_type=F32
                ).astype(BF16)
                table = table_ref[scalar_ref[1 + r]]
                added = jnp.dot(low, table, preferred_element_type=F32)
                part = slice(r * SLOT, (r + 1) * SLOT)
                total[:, part, :] = start_ref[:, part, :] + added.reshape(units, SLOT, added.shape[1])

    for e in range(block):
        unit = b * block + e
        both = jnp.concatenate([gate_ref[e], up_ref[e]], axis=1)
        product = jnp.dot(gathered[unit], both, preferred_element_type=F32)
        if not final:

            @pl.when(q == 0)
            def _():
                total[unit] = product

            @pl.when(q > 0)
            def _():
                total[unit] += product

        else:
            value = total[unit] + product

            @pl.when(q < quarters - 1)
            def _():
                total[unit] = value

            @pl.when(q == quarters - 1)
            def _():
                half = value.shape[1] // 2
                gate, up = value[:, :half], value[:, half:]
                hidden_ref[e] = (gate / (1.0 + jnp.exp(-gate)) * up).astype(BF16)


def expand(sources, specs, layout, first, scalars, pick, gate_weight, up_weight, final=None):
    units, width, share = gate_weight.shape
    wide = width // 4
    quarters = len(sources) // len(layout)
    block = min(units, 4)
    rows = GROUP * SLOT
    weight_spec = pl.BlockSpec((block, wide, share), lambda q, b, s: (b, s[0] ^ (q + first), 0))
    in_specs = list(specs) + [full_spec(pick.shape), weight_spec, weight_spec]
    args = list(sources) + [pick, gate_weight, up_weight]
    gathered = pltpu.VMEM((units, rows, wide), BF16)
    total = (units, rows, 2 * share)
    if final is None:
        out_specs = full_spec(total)
        out_shape = jax.ShapeDtypeStruct(total, F32)
        scratch = [gathered]
    else:
        args += list(final)
        in_specs += [full_spec(a.shape) for a in final]
        out_specs = pl.BlockSpec((block, rows, share), lambda q, b, s: (jnp.where(q == quarters - 1, b, 0), 0, 0))
        out_shape = jax.ShapeDtypeStruct((units, rows, share), BF16)
        scratch = [gathered, pltpu.VMEM(total, F32)]
    flops = 2 * quarters * units * rows * wide * (2 * share + 128)
    return pl.pallas_call(
        functools.partial(expand_kernel, units, block, quarters, layout, final is not None),
        grid_spec=pltpu.PrefetchScalarGridSpec(
            num_scalar_prefetch=1,
            grid=(quarters, units // block),
            in_specs=in_specs,
            out_specs=out_specs,
            scratch_shapes=scratch,
        ),
        out_shape=out_shape,
        compiler_params=params(),
        cost_estimate=pl.CostEstimate(
            flops=flops, bytes_accessed=quarters * (units * wide * share * 4 + 2**20) + 2**22, transcendentals=0
        ),
    )(scalars, *args)


def contract_kernel(units, scalar_ref, hidden_ref, down_ref, place_ref, gain_ref, send_ref, keep_ref, table):
    step = pl.program_id(0)
    wide = table.shape[2]
    for e in range(units):
        rows = lax.dot_general(
            hidden_ref[e], down_ref[e], (((1,), (1,)), ((), ())), preferred_element_type=F32
        )
        gain = jnp.concatenate([gain_ref[e]] * (wide // 128), axis=1)
        table[:, e * SLOT : (e + 1) * SLOT, :] = (rows * gain).astype(BF16).reshape(GROUP, SLOT, wide)

    @pl.when(step % 2 == 0)
    def _():
        for r in range(GROUP):
            send_ref[0, r] = jnp.dot(place_ref[r], table[r], preferred_element_type=F32).astype(BF16)

    @pl.when(step % 2 == 1)
    def _():
        for r in range(GROUP):
            keep_ref[0, r] = jnp.dot(place_ref[r], table[r], preferred_element_type=F32)


def contract(hidden, down_weight, place, gain, scalars, part, parts):
    units, width, share = down_weight.shape
    rows = GROUP * SLOT
    tokens = place.shape[1]
    wide = width // 4 // parts
    out = (2, GROUP, tokens, wide)
    out_spec = pl.BlockSpec((1, GROUP, tokens, wide), lambda q, s: (1 - q // 2, 0, 0, 0))
    return pl.pallas_call(
        functools.partial(contract_kernel, units),
        grid_spec=pltpu.PrefetchScalarGridSpec(
            num_scalar_prefetch=1,
            grid=(4,),
            in_specs=[
                full_spec(hidden.shape),
                pl.BlockSpec((units, wide, share), lambda q, s: (0, (s[0] ^ (3 - q)) * parts + part, 0)),
                full_spec(place.shape),
                full_spec(gain.shape),
            ],
            out_specs=[out_spec, out_spec],
            scratch_shapes=[pltpu.VMEM((GROUP, units * SLOT, wide), BF16)],
        ),
        out_shape=[jax.ShapeDtypeStruct(out, BF16), jax.ShapeDtypeStruct(out, F32)],
        compiler_params=params(),
        cost_estimate=pl.CostEstimate(
            flops=8 * units * wide * (rows * share + GROUP * SLOT * tokens),
            bytes_accessed=4 * wide * (units * share * 2 + GROUP * tokens * 3) + 2**21,
            transcendentals=0,
        ),
    )(scalars, hidden, down_weight, place, gain)


def xor_move(value, axis, bits):
    size = lax.axis_size(axis)
    return lax.ppermute(value, axis, [(i, i ^ bits) for i in range(size)])


def every_request(value, axis="dp"):
    blocks, found = value[None], [0]
    for bits in (4, 2, 1):
        blocks = jnp.concatenate([blocks, xor_move(blocks, axis, bits)], axis=0)
        found = found + [f ^ bits for f in found]
    return [blocks[found.index(n)] for n in range(8)]


def select_adapters(request_adapter, rows_local, row_index):
    wanted = request_adapter[:, None] * DOUBLE_RANK + jnp.arange(DOUBLE_RANK)[None, :]
    held = row_index * rows_local + jnp.arange(rows_local)
    return (wanted.reshape(-1)[:, None] == held[None, :]).astype(BF16)


def nt_dot(a, b):
    return lax.dot_general(a, b, (((1,), (1,)), ((), ())), preferred_element_type=F32)


def widen_tables(tables):
    is_gate = (jnp.arange(DOUBLE_RANK) < ADAPTER_RANK)[None, :, None]
    zero = jnp.zeros_like(tables)
    return jnp.concatenate([jnp.where(is_gate, tables, zero), jnp.where(is_gate, zero, tables)], axis=2)


def meta_of(token_experts, router_weight):
    left = router_weight.T
    terms = []
    for _ in range(3):
        term = lax.reduce_precision(left, 8, 7)
        terms.append(term.astype(BF16))
        left = left - term
    return jnp.concatenate([token_experts.T.astype(BF16)] + terms, axis=1)


def near_device(
    tokens,
    lengths,
    request_adapter,
    token_experts,
    router_weight,
    gate_weight,
    up_weight,
    down_weight,
    adapter_input_maps,
    adapter_output_maps,
):
    width = tokens.shape[1]
    units = gate_weight.shape[0]
    dp_count = lax.axis_size("dp")
    tp_count = lax.axis_size("tensor")
    i = lax.axis_index("dp")
    j = lax.axis_index("tensor")
    experts_all = units * dp_count // 2
    quarter = width // tp_count
    rel = i ^ jnp.array(ORDER, jnp.int32)
    tok_rows = tokens.shape[0]
    own = lax.dynamic_slice_in_dim(tokens, j * quarter, quarter, 1)

    block = jnp.concatenate([own, meta_of(token_experts, router_weight)], axis=0)
    ahead = [xor_move(block, "dp", n) for n in (1, 2, 4, 6)]
    behind = xor_move(jnp.stack(ahead[1:]), "dp", 1)
    ahead = jnp.stack(ahead)
    layout = ((0,), (4, 1, 2, 3), (5, 6, 7))

    natural = i ^ jnp.arange(dp_count)
    adapters = jnp.sum(
        jnp.where(natural[:, None] == jnp.arange(dp_count)[None, :], request_adapter[None, :], 0), axis=1
    )
    columns = nt_dot(select_adapters(adapters, adapter_input_maps.shape[1], i), adapter_input_maps)
    columns = columns.astype(BF16)
    for bits in (4, 2, 1):
        mine, theirs = columns[: bits * DOUBLE_RANK], columns[bits * DOUBLE_RANK :]
        columns = mine + xor_move(theirs, "dp", bits)
    low = nt_dot(columns, own)
    low = low + xor_move(low, "tensor", 1)
    low = low + xor_move(low, "tensor", 2)
    low = every_request(low.astype(BF16))
    low = jnp.stack([low[n] for n in ORDER])

    halves = adapter_output_maps.reshape(adapter_output_maps.shape[0], -1)
    tables = jnp.dot(
        select_adapters(request_adapter, halves.shape[0], i), halves, preferred_element_type=F32
    ).astype(BF16)
    share = halves.shape[1] // 2
    upper = i >= dp_count // 2
    low_half, high_half = tables[:, :share], tables[:, share:]
    tables = jnp.where(upper, high_half, low_half) + xor_move(
        jnp.where(upper, low_half, high_half), "dp", 4
    )
    for bits in (2, 1):
        tables = tables + xor_move(tables, "dp", bits)
    tables = widen_tables(tables.reshape(dp_count, DOUBLE_RANK, share))

    core_ahead, core_behind = xor_move(ahead, "tensor", 1), xor_move(behind, "tensor", 1)
    side_ahead, side_behind = xor_move(ahead, "tensor", 2), xor_move(behind, "tensor", 2)
    both_ahead, both_behind = xor_move(side_ahead, "tensor", 1), xor_move(side_behind, "tensor", 1)

    is_rel = rel[:, None] == jnp.arange(dp_count)[None, :]
    lengths_rel = jnp.sum(jnp.where(is_rel, lengths[None, :], 0), axis=1)
    first_expert = (i * units) % experts_all
    routes = block.shape[0] - tok_rows
    meta_specs = [
        pl.BlockSpec((n, routes, quarter), lambda *_: (0, tok_rows // routes, 0)) for n in (1, 3, 1, 3)
    ]
    meta_specs[2] = pl.BlockSpec((1, routes, quarter), lambda *_: (0, tok_rows // routes, 0))
    meta_specs[1] = pl.BlockSpec((3, routes, quarter), lambda *_: (0, tok_rows // routes, 0))
    pick, place, gain = make_slots(
        [block[None], ahead[1:], ahead[:1], behind], meta_specs, tok_rows, first_expert, lengths_rel, units
    )

    scalars = jnp.concatenate([j[None], rel]).astype(jnp.int32)

    def own_spec(q0):
        return pl.BlockSpec((tok_rows, quarter), lambda *a: (0, a[-1][0] ^ q0))

    def sources(*pairs):
        return [x for pair in pairs for x in (tokens,) + pair]

    def specs(first, *pairs):
        return [
            s
            for n, pair in enumerate(pairs)
            for s in [own_spec(first + n)] + [full_spec(x.shape) for x in pair]
        ]

    pairs = [(ahead, behind), (core_ahead, core_behind), (side_ahead, side_behind), (both_ahead, both_behind)]
    start = expand(
        sources(*pairs[:2]), specs(0, *pairs[:2]), layout, 0, scalars, pick, gate_weight, up_weight
    )
    hidden = expand(
        sources(*pairs[2:]),
        specs(2, *pairs[2:]),
        layout,
        2,
        scalars,
        pick,
        gate_weight,
        up_weight,
        (start, low, tables),
    )

    results = []
    parts = 2
    for part in range(parts):
        send, keep = contract(hidden, down_weight, place, gain, scalars, part, parts)
        sums = keep + xor_move(send, "tensor", 1).astype(F32)
        if part % 2 == 0:
            here = sums[0] + xor_move(sums[1].astype(BF16), "tensor", 2).astype(F32)
            here = here[:4] + xor_move(here[4:].astype(BF16), "dp", 1).astype(F32)
        else:
            sums = sums[:, :4] + xor_move(sums[:, 4:].astype(BF16), "dp", 1).astype(F32)
            here = sums[0] + xor_move(sums[1].astype(BF16), "tensor", 2).astype(F32)
        last = here[0]
        for k in (1, 2, 3):
            last = last + xor_move(here[k].astype(BF16), "dp", 2 * k).astype(F32)
        results.append(last.astype(BF16))
    return jnp.concatenate(results, axis=1)


def any_device(
    tokens,
    lengths,
    request_adapter,
    token_experts,
    router_weight,
    gate_weight,
    up_weight,
    down_weight,
    adapter_input_maps,
    adapter_output_maps,
):
    tok_rows, width = tokens.shape
    units = gate_weight.shape[0]
    dp_count = lax.axis_size("dp")
    tp_count = lax.axis_size("tensor")
    i = lax.axis_index("dp")
    j = lax.axis_index("tensor")
    experts_all = units * dp_count // 2
    quarter = width // tp_count
    meta = lax.all_gather(meta_of(token_experts, router_weight), "dp", axis=0)
    rows = lax.all_gather(tokens, "dp", axis=0)
    maps = lax.all_gather(adapter_input_maps, "dp", axis=1, tiled=True)
    adapter = jnp.sum(jnp.where(jnp.arange(dp_count) == i, request_adapter, 0))
    columns = nt_dot(select_adapters(adapter[None], maps.shape[1], 0), maps).astype(BF16)
    x_part = lax.dynamic_slice_in_dim(tokens, j * quarter, quarter, 1)
    low = lax.psum(nt_dot(columns, x_part), "tensor").astype(BF16)
    low = lax.all_gather(low, "dp", axis=0)
    every = lax.all_gather(adapter_output_maps, "dp", axis=0, tiled=True)
    half = jnp.where(i * units >= experts_all, every[:, 1], every[:, 0])
    tables = jnp.dot(
        select_adapters(request_adapter, half.shape[0], 0), half, preferred_element_type=F32
    ).astype(BF16)
    tables = widen_tables(tables.reshape(dp_count, DOUBLE_RANK, half.shape[1]))
    first_expert = (i * units) % experts_all
    natural = jnp.concatenate([j[None], jnp.arange(GROUP)]).astype(jnp.int32)

    def one_group(group):
        meta_g, rows_g, low_g, tables_g, lengths_g = group
        pick, place, gain = make_slots(
            [meta_g], [full_spec(meta_g.shape)], tok_rows, first_expert, lengths_g, units
        )
        layout = (tuple(range(GROUP)),)

        def spec(q0):
            return pl.BlockSpec((GROUP, tok_rows, quarter), lambda *a: (0, 0, a[-1][0] ^ q0))

        start = expand(
            [rows_g] * 2, [spec(0), spec(1)], layout, 0, natural, pick, gate_weight, up_weight
        )
        hidden = expand(
            [rows_g] * 2,
            [spec(2), spec(3)],
            layout,
            2,
            natural,
            pick,
            gate_weight,
            up_weight,
            (start, low_g, tables_g),
        )
        send, keep = contract(hidden, down_weight, place, gain, natural, 0, 1)
        return keep.astype(BF16), send

    groups = dp_count // GROUP
    grouped = [
        a.reshape((groups, GROUP) + a.shape[1:]) for a in (meta, rows, low, tables, lengths)
    ]
    keep, send = lax.map(one_group, tuple(grouped))
    sums = [keep[:, 0], send[:, 0], keep[:, 1], send[:, 1]]
    sums = [a.reshape(dp_count * tok_rows, quarter) for a in sums]
    here = sums[0].astype(F32)
    for q in range(1, 4):
        here = here + xor_move(sums[q], "tensor", q).astype(F32)
    return lax.psum_scatter(here, "dp", scatter_dimension=0, tiled=True).astype(BF16)


def solution(mesh):
    near = mesh.shape["dp"] == 8 and mesh.shape["tensor"] == 4
    in_specs = (
        P("dp", None),
        P(),
        P(),
        P("dp", None),
        P("dp", None),
        P("dp", None, "tensor"),
        P("dp", None, "tensor"),
        P("dp", None, "tensor"),
        P("tensor", "dp"),
        P("dp", None, "tensor"),
    )
    return jax.shard_map(
        near_device if near else any_device,
        mesh=mesh,
        in_specs=in_specs,
        out_specs=P("dp", "tensor"),
        check_vma=False,
    )
```

time: 997 us -> 168 us (0.17)
  waiting for transfers between devices: 691 us -> 57.1 us
  local copies, waits for them, and re-layouts: 115 us -> 3.88 us
  matrix products: 67.3 us -> 1.54 us
  other arithmetic: 74.5 us -> 9.23 us
  Pallas kernels: 0 us -> 60.7 us
  starting transfers between devices: 15.3 us -> 34.2 us
  between operations: 15 us -> 0.41 us
  blocking collectives: 11.2 us -> 0 us
    all_gather x6 -> x0, waiting for transfers between devices: 512 us -> none  [the longest x1 188 us: per_device(): up_piece = lax.all_gather(up_weight, 'tensor', axis=2, tiled=True)]
    all_to_all x3 -> x0, waiting for transfers between devices: 154 us -> none  [the longest x1 81.7 us: per_device(): lax.all_to_all(unit_output, 'dp', split_axis=0, concat_axis=0, tiled=True)]
    dot_general x6 -> x3, matrix products: 67.3 us -> 1.54 us  [the longest x1 1.13 us: near_device(): jnp.dot(select_adapters(request_adapter, halves.shape[0], i), halves, pre...]
    pallas_call x0 -> x5, Pallas kernels: none -> 60.7 us  [the longest x2 36.9 us: expand(): pl.pallas_call(functools.partial(expand_kernel, units, block, quarters, l...]
    ppermute x0 -> x34, waiting for transfers between devices: none -> 57.1 us  [xor_move(): return lax.ppermute(value, axis, [(i, i ^ bits) for i in range(size)])]
    gather x7 -> x0, local copies, waits for them, and re-layouts: 39.3 us -> none  [the longest x1 18.9 us: combine_routes(): pair_rows = unit_table[pair_slots].astype(jnp.float32)]
    ppermute x0 -> x34, starting transfers between devices: none -> 34.2 us  [xor_move(): return lax.ppermute(value, axis, [(i, i ^ bits) for i in range(size)])]
    reduce_sum x3 -> x2, other arithmetic: 33.7 us -> 1.67 us  [the longest x1 0.84 us: near_device(): jnp.sum(jnp.where(natural[:, None] == jnp.arange(dp_count)[None, :], requ...]
  transfers between devices with their start and end apart: 10 -> 34, of which waited for: 7 -> 18; matrix products, arithmetic and copies ran while one was open for 15% -> 5% of each run, Pallas kernels for 0% -> 19%
where the time goes in v1:
time: 168 us; the launch traced here: 167 us
  Pallas kernels  60.7 us (36%)
  waiting for transfers between devices  57.1 us (34%)
  starting transfers between devices  34.2 us (20%)
  other arithmetic  9.23 us (5%)
  local copies, waits for them, and re-layouts  3.88 us (2%)
    ppermute x34, waiting for transfers between devices, xor_move(): return lax.ppermute(value, axis, [(i, i ^ bits) for i in range(size)])  57.1 us
    pallas_call x2, Pallas kernels, expand(): pl.pallas_call(functools.partial(expand_kernel, units, block, quarters, l...  36.9 us
    ppermute x34, starting transfers between devices, xor_move(): return lax.ppermute(value, axis, [(i, i ^ bits) for i in range(size)])  34.2 us
    pallas_call x2, Pallas kernels, contract(): pl.pallas_call(functools.partial(contract_kernel, units), grid_spec=pltpu...  19.7 us
    pallas_call x1, Pallas kernels, make_slots(): pl.pallas_call(functools.partial(slots_kernel, units), grid_spec=pltpu.Pr...  4.19 us
  transfers between devices with their start and end apart: 34, of which 18 were waited for; matrix products, arithmetic and copies ran while one was open for 5% of the time, Pallas kernels for 19%

profile of v1, /device:TPU:0, one launch (start us, length us, event | category | flops | bytes accessed | tf_op | source)
XLA Modules:
  0.0 167.1 jit_solution(13655966426480783343)
XLA Ops:
  2.4 3.1 %collective-permute-start.1 = (bf16[136,512]{1,0:T(8,128)(2,1)S(1)}, bf16[136,512]{1,0:T(8,128)(2,1)S(1)}, u32[]{:S(2)}, u32[]{:S(2)}) collective-permute-start(bf16[136,512]{1,0:T(8,128)(2,1)S(1)} %maximum_maximum_fusion), channel_id=1, source_target_pairs={{0,8},{4,12},{8,0},{12,4},{16,24},{20,28},{24,16},{28,20},{1,9},{5... | collective-permute-start | bytes 417800 | tf_op jit(solution)/shard_map/ppermute | solution.py:245
  5.5 2.6 %collective-permute-start.2 = (bf16[136,512]{1,0:T(8,128)(2,1)S(1)}, bf16[136,512]{1,0:T(8,128)(2,1)S(1)}, u32[]{:S(2)}, u32[]{:S(2)}) collective-permute-start(bf16[136,512]{1,0:T(8,128)(2,1)S(1)} %maximum_maximum_fusion), channel_id=1, source_target_pairs={{0,16},{4,20},{8,24},{12,28},{16,0},{20,4},{24,8},{28,12},{1,17},{... | collective-permute-start | bytes 417800 | tf_op jit(solution)/shard_map/ppermute | solution.py:245
  9.4 2.0 %collective-permute-start.11 = (bf16[128,512]{1,0:T(8,128)(2,1)S(1)}, bf16[128,512]{1,0:T(8,128)(2,1)S(1)}, u32[]{:S(2)}, u32[]{:S(2)}) collective-permute-start(bf16[128,512]{1,0:T(8,128)(2,1)S(1)} %slice.133), channel_id=1, source_target_pairs={{0,16},{4,20},{8,24},{12,28},{16,0},{20,4},{24,8},{28,12},{1,17},{... | collective-permute-start | bytes 393224 | tf_op jit(solution)/shard_map/ppermute | solution.py:245
  12.1 1.1 convolution_convert_fusion.1
  17.2 11.0 %collective-permute-done.11 = bf16[128,512]{1,0:T(8,128)(2,1)S(1)} collective-permute-done((bf16[128,512]{1,0:T(8,128)(2,1)S(1)}, bf16[128,512]{1,0:T(8,128)(2,1)S(1)}, u32[]{:S(2)}, u32[]{:S(2)}) %collective-permute-start.11) | collective-permute-done | bytes 131104 | tf_op jit(solution)/shard_map/ppermute | solution.py:245
  29.0 1.5 collective-permute-start.20
  30.4 2.2 %collective-permute-done.12 = bf16[64,512]{1,0:T(8,128)(2,1)S(1)} collective-permute-done((bf16[64,512]{1,0:T(8,128)(2,1)S(1)}, bf16[64,512]{1,0:T(8,128)(2,1)S(1)}, u32[]{:S(2)}, u32[]{:S(2)}) %collective-permute-start.12) | collective-permute-done | bytes 65568 | tf_op jit(solution)/shard_map/ppermute | solution.py:245
  32.6 1.6 collective-permute-start.13
  35.3 1.3 collective-permute-done.13
  36.6 1.5 collective-permute-start.21
  38.3 1.5 collective-permute-done
  40.0 1.6 collective-permute-start.15
  44.9 3.4 %collective-permute-done.16 = bf16[1,32,128]{2,1,0:T(8,128)(2,1)S(1)} collective-permute-done((bf16[1,32,128]{2,1,0:T(8,128)(2,1)S(1)}, bf16[1,32,128]{2,1,0:T(8,128)(2,1)S(1)}, u32[]{:S(2)}, u32[]{:S(2)}) %collective-permute-start.16) | collective-permute-done | bytes 8224 | tf_op jit(solution)/shard_map/ppermute | solution.py:245
  49.1 3.0 %collective-permute-done.17 = bf16[2,32,128]{2,1,0:T(8,128)(2,1)S(1)} collective-permute-done((bf16[2,32,128]{2,1,0:T(8,128)(2,1)S(1)}, bf16[2,32,128]{2,1,0:T(8,128)(2,1)S(1)}, u32[]{:S(2)}, u32[]{:S(2)}) %collective-permute-start.17) | collective-permute-done | bytes 16416 | tf_op jit(solution)/shard_map/ppermute | solution.py:245
  52.7 3.3 %collective-permute-done.18 = bf16[4,32,128]{2,1,0:T(8,128)(2,1)S(1)} collective-permute-done((bf16[4,32,128]{2,1,0:T(8,128)(2,1)S(1)}, bf16[4,32,128]{2,1,0:T(8,128)(2,1)S(1)}, u32[]{:S(2)}, u32[]{:S(2)}) %collective-permute-start.18) | collective-permute-done | bytes 32800 | tf_op jit(solution)/shard_map/ppermute | solution.py:245
  56.0 1.6 collective-permute-start.6
  58.1 7.6 %collective-permute-done.6.refs_2_ = bf16[3,136,512]{2,1,0:T(8,128)(2,1)S(1)} collective-permute-done((bf16[3,136,512]{2,1,0:T(8,128)(2,1)S(1)}, bf16[3,136,512]{2,1,0:T(8,128)(2,1)S(1)}, u32[]{:S(2)}, u32[]{:S(2)}) %collective-permute-start.6) | collective-permute-done | bytes 417824 | tf_op jit(solution)/shard_map/ppermute | solution.py:245
  65.7 4.2 %shard_map.109 = (bf16[8,512,128]{2,1,0:T(8,128)(2,1)}, bf16[8,128,512]{2,1,0:T(8,128)(2,1)}, f32[16,256,128]{2,1,0:T(8,128)}) custom-call(s32[9]{0:T(128)} %pad_add_fusion.1.scalar_ref, bf16[1,136,512]{2,1,0:T(8,128)(2,1)} %fusion.30.refs_0_, bf16[3,136,512]{2,1,0:T(8,128)(2,1)} %copy-done.4, bf16[1,136,512]{2,1,0:T(8,128)(2,1)} %bitcast.79, ...), custom_call_target="tpu_custom_call" | custom-call | flops 100000000 | bytes 4500000 | tf_op jit(solution)/shard_map/pallas_call | solution.py:68
  70.9 17.5 %shard_map.110.refs_9_ = f32[16,256,256]{2,1,0:T(8,128)} custom-call(s32[9]{0:T(128)} %pad_add_fusion.scalar_ref, bf16[128,2048]{1,0:T(8,128)(2,1)} %refs_3_.3, bf16[4,136,512]{2,1,0:T(8,128)(2,1)} %copy-done.1, bf16[3,136,512]{2,1,0:T(8,128)(2,1)} %copy-done.5, bf16[128,2048]{1,0:T(8,128)(2,1)} %refs_3_.3, bf16[4,136,512]{2,1,0:T(8,128)(2,1)} %copy-done.7, ...), custom_call_target="tpu_custom_call" | custom-call | flops 3221225472 | bytes 14680064 | tf_op jit(solution)/shard_map/pallas_call | solution.py:174
  90.0 19.3 %shard_map.111.hidden_ref = bf16[16,256,128]{2,1,0:T(8,128)(2,1)} custom-call(s32[9]{0:T(128)} %pad_add_fusion.scalar_ref, bf16[128,2048]{1,0:T(8,128)(2,1)} %refs_3_.3, bf16[4,136,512]{2,1,0:T(8,128)(2,1)} %copy-done.6, bf16[3,136,512]{2,1,0:T(8,128)(2,1)} %copy-done.10, bf16[128,2048]{1,0:T(8,128)(2,1)} %refs_3_.3, bf16[4,136,512]{2,1,0:T(8,128)(2,1)} %copy-done.8, ...), custom_call_target="tpu_custom_call" | custom-call | flops 3221225472 | bytes 14680064 | tf_op jit(solution)/shard_map/pallas_call | solution.py:174
  109.3 9.8 %shard_map.112 = (bf16[2,8,128,256]{3,2,1,0:T(8,128)(2,1)}, f32[2,8,128,256]{3,2,1,0:T(8,128)}) custom-call(s32[9]{0:T(128)} %pad_add_fusion.scalar_ref, bf16[16,256,128]{2,1,0:T(8,128)(2,1)} %shard_map.111.hidden_ref, bf16[16,2048,128]{2,1,0:T(8,128)(2,1)} %down_ref.3, bf16[8,128,512]{2,1,0:T(8,128)(2,1)} %get-tuple-element.13.place_ref, ...), custom_call_target="tpu_custom_call" | custom-call | flops 2147483648 | bytes 9437184 | tf_op jit(solution)/shard_map/pallas_call | solution.py:219
  119.6 9.9 %shard_map.113 = (bf16[2,8,128,256]{3,2,1,0:T(8,128)(2,1)}, f32[2,8,128,256]{3,2,1,0:T(8,128)}) custom-call(s32[9]{0:T(128)} %pad_add_fusion.scalar_ref, bf16[16,256,128]{2,1,0:T(8,128)(2,1)} %shard_map.111.hidden_ref, bf16[16,2048,128]{2,1,0:T(8,128)(2,1)} %down_ref.3, bf16[8,128,512]{2,1,0:T(8,128)(2,1)} %get-tuple-element.13.place_ref, ...), custom_call_target="tpu_custom_call" | custom-call | flops 2147483648 | bytes 9437184 | tf_op jit(solution)/shard_map/pallas_call | solution.py:219
  129.9 1.6 collective-permute-start.23
  133.4 10.9 %collective-permute-done.23 = bf16[8,128,256]{2,1,0:T(8,128)(2,1)S(1)} collective-permute-done((bf16[8,128,256]{2,1,0:T(8,128)(2,1)S(1)}, bf16[8,128,256]{2,1,0:T(8,128)(2,1)S(1)}, u32[]{:S(2)}, u32[]{:S(2)}) %collective-permute-start.23) | collective-permute-done | bytes 524320 | tf_op jit(solution)/shard_map/ppermute | solution.py:245
  145.0 1.8 %collective-permute-done.29 = bf16[2,4,128,256]{3,2,1,0:T(8,128)(2,1)S(1)} collective-permute-done((bf16[2,4,128,256]{3,2,1,0:T(8,128)(2,1)S(1)}, bf16[2,4,128,256]{3,2,1,0:T(8,128)(2,1)S(1)}, u32[]{:S(2)}, u32[]{:S(2)}) %collective-permute-start.29) | collective-permute-done | bytes 524320 | tf_op jit(solution)/shard_map/ppermute | solution.py:245
  147.0 1.6 collective-permute-start.30
  148.6 3.9 %collective-permute-done.24 = bf16[4,128,256]{2,1,0:T(8,128)(2,1)S(1)} collective-permute-done((bf16[4,128,256]{2,1,0:T(8,128)(2,1)S(1)}, bf16[4,128,256]{2,1,0:T(8,128)(2,1)S(1)}, u32[]{:S(2)}, u32[]{:S(2)}) %collective-permute-start.24) | collective-permute-done | bytes 262176 | tf_op jit(solution)/shard_map/ppermute | solution.py:245
  152.6 3.0 %collective-permute-start.26 = (bf16[128,256]{1,0:T(8,128)(2,1)S(1)}, bf16[128,256]{1,0:T(8,128)(2,1)S(1)}, u32[]{:S(2)}, u32[]{:S(2)}) collective-permute-start(bf16[128,256]{1,0:T(8,128)(2,1)S(1)} %get-tuple-element.27), channel_id=1, source_target_pairs={{0,16},{4,20},{8,24},{12,28},{16,0},{20,4},{24,8},{28,12},{1,17},{... | collective-permute-start | bytes 196616 | tf_op jit(solution)/shard_map/ppermute | solution.py:245
  155.6 1.4 collective-permute-start.27
  157.2 3.0 %collective-permute-start.32 = (bf16[128,256]{1,0:T(8,128)(2,1)S(1)}, bf16[128,256]{1,0:T(8,128)(2,1)S(1)}, u32[]{:S(2)}, u32[]{:S(2)}) collective-permute-start(bf16[128,256]{1,0:T(8,128)(2,1)S(1)} %get-tuple-element.30), channel_id=1, source_target_pairs={{0,16},{4,20},{8,24},{12,28},{16,0},{20,4},{24,8},{28,12},{1,17},{... | collective-permute-start | bytes 196616 | tf_op jit(solution)/shard_map/ppermute | solution.py:245
  160.2 1.4 collective-permute-start.33
  162.6 2.7 %collective-permute-done.32 = bf16[128,256]{1,0:T(8,128)(2,1)S(1)} collective-permute-done((bf16[128,256]{1,0:T(8,128)(2,1)S(1)}, bf16[128,256]{1,0:T(8,128)(2,1)S(1)}, u32[]{:S(2)}, u32[]{:S(2)}) %collective-permute-start.32) | collective-permute-done | bytes 65568 | tf_op jit(solution)/shard_map/ppermute | solution.py:245
  (130 shorter events, 25.2 us)
Async XLA Ops:
  2.4 35.9 %collective-permute-start.1 = (bf16[136,512]{1,0:T(8,128)(2,1)S(1)}, bf16[136,512]{1,0:T(8,128)(2,1)S(1)}, u32[]{:S(2)}, u32[]{:S(2)}) collective-permute-start(bf16[136,512]{1,0:T(8,128)(2,1)S(1)} %maximum_maximum_fusion), channel_id=1, source_target_pairs={{0,8},{4,12},{8,0},{12,4},{16,24},{20,28},{24,16},{28,20},{1,9},{5... | collective-permute-start | bytes 417800 | tf_op jit(solution)/shard_map/ppermute | solution.py:245
  5.5 32.8 %collective-permute-start.2 = (bf16[136,512]{1,0:T(8,128)(2,1)S(1)}, bf16[136,512]{1,0:T(8,128)(2,1)S(1)}, u32[]{:S(2)}, u32[]{:S(2)}) collective-permute-start(bf16[136,512]{1,0:T(8,128)(2,1)S(1)} %maximum_maximum_fusion), channel_id=1, source_target_pairs={{0,16},{4,20},{8,24},{12,28},{16,0},{20,4},{24,8},{28,12},{1,17},{... | collective-permute-start | bytes 417800 | tf_op jit(solution)/shard_map/ppermute | solution.py:245
  8.0 30.3 %collective-permute-start.3 = (bf16[136,512]{1,0:T(8,128)(2,1)S(1)}, bf16[136,512]{1,0:T(8,128)(2,1)S(1)}, u32[]{:S(2)}, u32[]{:S(2)}) collective-permute-start(bf16[136,512]{1,0:T(8,128)(2,1)S(1)} %maximum_maximum_fusion), channel_id=1, source_target_pairs={{0,24},{4,28},{8,16},{12,20},{16,8},{20,12},{24,0},{28,4},{1,25},{... | collective-permute-start | bytes 417800 | tf_op jit(solution)/shard_map/ppermute | solution.py:245
  9.4 18.9 %collective-permute-start.11 = (bf16[128,512]{1,0:T(8,128)(2,1)S(1)}, bf16[128,512]{1,0:T(8,128)(2,1)S(1)}, u32[]{:S(2)}, u32[]{:S(2)}) collective-permute-start(bf16[128,512]{1,0:T(8,128)(2,1)S(1)} %slice.133), channel_id=1, source_target_pairs={{0,16},{4,20},{8,24},{12,28},{16,0},{20,4},{24,8},{28,12},{1,17},{... | collective-permute-start | bytes 393224 | tf_op jit(solution)/shard_map/ppermute | solution.py:245
  13.3 15.7 %collective-permute-start.19 = (bf16[256,128]{1,0:T(8,128)(2,1)S(1)}, bf16[256,128]{1,0:T(8,128)(2,1)S(1)}, u32[]{:S(2)}, u32[]{:S(2)}) collective-permute-start(bf16[256,128]{1,0:T(8,128)(2,1)S(1)} %broadcast_select_fusion.2), channel_id=1, source_target_pairs={{0,16},{4,20},{8,24},{12,28},{16,0},{20,4},{24,8},{28,12},{1,17},{... | collective-permute-start | bytes 196616 | tf_op jit(solution)/shard_map/ppermute | solution.py:245
  28.2 4.3 %collective-permute-start.12 = (bf16[64,512]{1,0:T(8,128)(2,1)S(1)}, bf16[64,512]{1,0:T(8,128)(2,1)S(1)}, u32[]{:S(2)}, u32[]{:S(2)}) collective-permute-start(bf16[64,512]{1,0:T(8,128)(2,1)S(1)} %slice.135), channel_id=1, source_target_pairs={{0,8},{4,12},{8,0},{12,4},{16,24},{20,28},{24,16},{28,20},{1,9},{5... | collective-permute-start | bytes 196616 | tf_op jit(solution)/shard_map/ppermute | solution.py:245
  29.0 5.8 %collective-permute-start.20 = (bf16[256,128]{1,0:T(8,128)(2,1)S(1)}, bf16[256,128]{1,0:T(8,128)(2,1)S(1)}, u32[]{:S(2)}, u32[]{:S(2)}) collective-permute-start(bf16[256,128]{1,0:T(8,128)(2,1)S(1)} %select_add_fusion), channel_id=1, source_target_pairs={{0,8},{4,12},{8,0},{12,4},{16,24},{20,28},{24,16},{28,20},{1,9},{5... | collective-permute-start | bytes 196616 | tf_op jit(solution)/shard_map/ppermute | solution.py:245
  32.6 4.0 %collective-permute-start.13 = (bf16[32,512]{1,0:T(8,128)(2,1)S(1)}, bf16[32,512]{1,0:T(8,128)(2,1)S(1)}, u32[]{:S(2)}, u32[]{:S(2)}) collective-permute-start(bf16[32,512]{1,0:T(8,128)(2,1)S(1)} %slice.137), channel_id=1, source_target_pairs={{0,4},{4,0},{8,12},{12,8},{16,20},{20,16},{24,28},{28,24},{1,5},{5... | collective-permute-start | bytes 98312 | tf_op jit(solution)/shard_map/ppermute | solution.py:245
  34.8 5.1 %collective-permute-start = (bf16[136,512]{1,0:T(8,128)(2,1)S(1)}, bf16[136,512]{1,0:T(8,128)(2,1)S(1)}, u32[]{:S(2)}, u32[]{:S(2)}) collective-permute-start(bf16[136,512]{1,0:T(8,128)(2,1)S(1)} %maximum_maximum_fusion), channel_id=1, source_target_pairs={{0,4},{4,0},{8,12},{12,8},{16,20},{20,16},{24,28},{28,24},{1,5},{5... | collective-permute-start | bytes 417800 | tf_op jit(solution)/shard_map/ppermute | solution.py:245
  36.6 6.2 %collective-permute-start.21 = (bf16[256,128]{1,0:T(8,128)(2,1)S(1)}, bf16[256,128]{1,0:T(8,128)(2,1)S(1)}, u32[]{:S(2)}, u32[]{:S(2)}) collective-permute-start(bf16[256,128]{1,0:T(8,128)(2,1)S(1)} %add.137), channel_id=1, source_target_pairs={{0,4},{4,0},{8,12},{12,8},{16,20},{20,16},{24,28},{28,24},{1,5},{5... | collective-permute-start | bytes 196616 | tf_op jit(solution)/shard_map/ppermute | solution.py:245
  40.0 3.8 %collective-permute-start.15 = (f32[32,128]{1,0:T(8,128)S(1)}, f32[32,128]{1,0:T(8,128)S(1)}, u32[]{:S(2)}, u32[]{:S(2)}) collective-permute-start(f32[32,128]{1,0:T(8,128)S(1)} %add.130), channel_id=1, source_target_pairs={{0,2},{1,3},{2,0},{3,1},{4,6},{5,7},{6,4},{7,5},{8,10},{9,11},{10,... | collective-permute-start | bytes 49160 | tf_op jit(solution)/shard_map/ppermute | solution.py:245
  41.6 28.3 %collective-permute-start.9 = (bf16[4,136,512]{2,1,0:T(8,128)(2,1)S(1)}, bf16[4,136,512]{2,1,0:T(8,128)(2,1)S(1)}, u32[]{:S(2)}, u32[]{:S(2)}) collective-permute-start(bf16[4,136,512]{2,1,0:T(8,128)(2,1)S(1)} %pad_maximum_fusion.refs_1_), channel_id=1, source_target_pairs={{0,1},{1,0},{2,3},{3,2},{4,5},{5,4},{6,7},{7,6},{8,9},{9,8},{10,11... | collective-permute-start | bytes 1671176 | tf_op jit(solution)/shard_map/ppermute | solution.py:245
  41.7 15.9 %collective-permute-start.4 = (bf16[4,136,512]{2,1,0:T(8,128)(2,1)S(1)}, bf16[4,136,512]{2,1,0:T(8,128)(2,1)S(1)}, u32[]{:S(2)}, u32[]{:S(2)}) collective-permute-start(bf16[4,136,512]{2,1,0:T(8,128)(2,1)S(1)} %pad_maximum_fusion.refs_1_), channel_id=1, source_target_pairs={{0,2},{1,3},{2,0},{3,1},{4,6},{5,7},{6,4},{7,5},{8,10},{9,11},{10,... | collective-permute-start | bytes 1671176 | tf_op jit(solution)/shard_map/ppermute | solution.py:245
  42.3 13.7 %collective-permute-start.5 = (bf16[3,136,512]{2,1,0:T(8,128)(2,1)S(1)}, bf16[3,136,512]{2,1,0:T(8,128)(2,1)S(1)}, u32[]{:S(2)}, u32[]{:S(2)}) collective-permute-start(bf16[3,136,512]{2,1,0:T(8,128)(2,1)S(1)} %pad_maximum_fusion.1.refs_1_), channel_id=1, source_target_pairs={{0,4},{4,0},{8,12},{12,8},{16,20},{20,16},{24,28},{28,24},{1,5},{5... | collective-permute-start | bytes 1253384 | tf_op jit(solution)/shard_map/ppermute | solution.py:245
  43.8 4.5 %collective-permute-start.16 = (bf16[1,32,128]{2,1,0:T(8,128)(2,1)S(1)}, bf16[1,32,128]{2,1,0:T(8,128)(2,1)S(1)}, u32[]{:S(2)}, u32[]{:S(2)}) collective-permute-start(bf16[1,32,128]{2,1,0:T(8,128)(2,1)S(1)} %get-tuple-element.24), channel_id=1, source_target_pairs={{0,16},{4,20},{8,24},{12,28},{16,0},{20,4},{24,8},{28,12},{1,17},{... | collective-permute-start | bytes 24584 | tf_op jit(solution)/shard_map/ppermute | solution.py:245
  48.3 3.7 %collective-permute-start.17 = (bf16[2,32,128]{2,1,0:T(8,128)(2,1)S(1)}, bf16[2,32,128]{2,1,0:T(8,128)(2,1)S(1)}, u32[]{:S(2)}, u32[]{:S(2)}) collective-permute-start(bf16[2,32,128]{2,1,0:T(8,128)(2,1)S(1)} %pad_maximum_fusion.5), channel_id=1, source_target_pairs={{0,8},{4,12},{8,0},{12,4},{16,24},{20,28},{24,16},{28,20},{1,9},{5... | collective-permute-start | bytes 49160 | tf_op jit(solution)/shard_map/ppermute | solution.py:245
  52.1 3.9 %collective-permute-start.18 = (bf16[4,32,128]{2,1,0:T(8,128)(2,1)S(1)}, bf16[4,32,128]{2,1,0:T(8,128)(2,1)S(1)}, u32[]{:S(2)}, u32[]{:S(2)}) collective-permute-start(bf16[4,32,128]{2,1,0:T(8,128)(2,1)S(1)} %pad_maximum_fusion.4), channel_id=1, source_target_pairs={{0,4},{4,0},{8,12},{12,8},{16,20},{20,16},{24,28},{28,24},{1,5},{5... | collective-permute-start | bytes 98312 | tf_op jit(solution)/shard_map/ppermute | solution.py:245
  56.0 9.7 %collective-permute-start.6 = (bf16[3,136,512]{2,1,0:T(8,128)(2,1)S(1)}, bf16[3,136,512]{2,1,0:T(8,128)(2,1)S(1)}, u32[]{:S(2)}, u32[]{:S(2)}) collective-permute-start(bf16[3,136,512]{2,1,0:T(8,128)(2,1)S(1)} %collective-permute-done.5.refs_3_.refs_2_), channel_id=1, source_target_pairs={{0,2},{1,3},{2,0},{3,1},{4,6},{5,7},{6,4},{7,5},{8,10},{9,11},{10,... | collective-permute-start | bytes 1253384 | tf_op jit(solution)/shard_map/ppermute | solution.py:245
  57.6 12.3 %collective-permute-start.10 = (bf16[3,136,512]{2,1,0:T(8,128)(2,1)S(1)}, bf16[3,136,512]{2,1,0:T(8,128)(2,1)S(1)}, u32[]{:S(2)}, u32[]{:S(2)}) collective-permute-start(bf16[3,136,512]{2,1,0:T(8,128)(2,1)S(1)} %collective-permute-done.5.refs_3_.refs_2_), channel_id=1, source_target_pairs={{0,1},{1,0},{2,3},{3,2},{4,5},{5,4},{6,7},{7,6},{8,9},{9,8},{10,11... | collective-permute-start | bytes 1253384 | tf_op jit(solution)/shard_map/ppermute | solution.py:245
  57.6 30.8 %collective-permute-start.7 = (bf16[4,136,512]{2,1,0:T(8,128)(2,1)S(1)}, bf16[4,136,512]{2,1,0:T(8,128)(2,1)S(1)}, u32[]{:S(2)}, u32[]{:S(2)}) collective-permute-start(bf16[4,136,512]{2,1,0:T(8,128)(2,1)S(1)} %collective-permute-done.4.refs_1_), channel_id=1, source_target_pairs={{0,1},{1,0},{2,3},{3,2},{4,5},{5,4},{6,7},{7,6},{8,9},{9,8},{10,11... | collective-permute-start | bytes 1671176 | tf_op jit(solution)/shard_map/ppermute | solution.py:245
  65.7 22.8 %collective-permute-start.8 = (bf16[3,136,512]{2,1,0:T(8,128)(2,1)S(1)}, bf16[3,136,512]{2,1,0:T(8,128)(2,1)S(1)}, u32[]{:S(2)}, u32[]{:S(2)}) collective-permute-start(bf16[3,136,512]{2,1,0:T(8,128)(2,1)S(1)} %collective-permute-done.6.refs_2_), channel_id=1, source_target_pairs={{0,1},{1,0},{2,3},{3,2},{4,5},{5,4},{6,7},{7,6},{8,9},{9,8},{10,11... | collective-permute-start | bytes 1253384 | tf_op jit(solution)/shard_map/ppermute | solution.py:245
  119.1 10.4 %collective-permute-start.22 = (bf16[2,8,128,256]{3,2,1,0:T(8,128)(2,1)}, bf16[2,8,128,256]{3,2,1,0:T(8,128)(2,1)S(1)}, u32[]{:S(2)}, u32[]{:S(2)}) collective-permute-start(bf16[2,8,128,256]{3,2,1,0:T(8,128)(2,1)} %get-tuple-element.16), channel_id=1, source_target_pairs={{0,1},{1,0},{2,3},{3,2},{4,5},{5,4},{6,7},{7,6},{8,9},{9,8},{10,11... | collective-permute-start | bytes 3145736 | tf_op jit(solution)/shard_map/ppermute | solution.py:245
  129.9 14.4 %collective-permute-start.23 = (bf16[8,128,256]{2,1,0:T(8,128)(2,1)S(1)}, bf16[8,128,256]{2,1,0:T(8,128)(2,1)S(1)}, u32[]{:S(2)}, u32[]{:S(2)}) collective-permute-start(bf16[8,128,256]{2,1,0:T(8,128)(2,1)S(1)} %fusion.1), channel_id=1, source_target_pairs={{0,2},{1,3},{2,0},{3,1},{4,6},{5,7},{6,4},{7,5},{8,10},{9,11},{10,... | collective-permute-start | bytes 1572872 | tf_op jit(solution)/shard_map/ppermute | solution.py:245
  132.8 14.0 %collective-permute-start.29 = (bf16[2,4,128,256]{3,2,1,0:T(8,128)(2,1)S(1)}, bf16[2,4,128,256]{3,2,1,0:T(8,128)(2,1)S(1)}, u32[]{:S(2)}, u32[]{:S(2)}) collective-permute-start(bf16[2,4,128,256]{3,2,1,0:T(8,128)(2,1)S(1)} %slice.216), channel_id=1, source_target_pairs={{0,4},{4,0},{8,12},{12,8},{16,20},{20,16},{24,28},{28,24},{1,5},{5... | collective-permute-start | bytes 1572872 | tf_op jit(solution)/shard_map/ppermute | solution.py:245
  144.4 8.0 %collective-permute-start.24 = (bf16[4,128,256]{2,1,0:T(8,128)(2,1)S(1)}, bf16[4,128,256]{2,1,0:T(8,128)(2,1)S(1)}, u32[]{:S(2)}, u32[]{:S(2)}) collective-permute-start(bf16[4,128,256]{2,1,0:T(8,128)(2,1)S(1)} %slice.217), channel_id=1, source_target_pairs={{0,4},{4,0},{8,12},{12,8},{16,20},{20,16},{24,28},{28,24},{1,5},{5... | collective-permute-start | bytes 786440 | tf_op jit(solution)/shard_map/ppermute | solution.py:245
  147.0 10.0 %collective-permute-start.30 = (bf16[4,128,256]{2,1,0:T(8,128)(2,1)S(1)}, bf16[4,128,256]{2,1,0:T(8,128)(2,1)S(1)}, u32[]{:S(2)}, u32[]{:S(2)}) collective-permute-start(bf16[4,128,256]{2,1,0:T(8,128)(2,1)S(1)} %fusion.3), channel_id=1, source_target_pairs={{0,2},{1,3},{2,0},{3,1},{4,6},{5,7},{6,4},{7,5},{8,10},{9,11},{10,... | collective-permute-start | bytes 786440 | tf_op jit(solution)/shard_map/ppermute | solution.py:245
  152.5 7.7 %collective-permute-start.25 = (bf16[128,256]{1,0:T(8,128)(2,1)S(1)}, bf16[128,256]{1,0:T(8,128)(2,1)S(1)}, u32[]{:S(2)}, u32[]{:S(2)}) collective-permute-start(bf16[128,256]{1,0:T(8,128)(2,1)S(1)} %get-tuple-element.25), channel_id=1, source_target_pairs={{0,8},{4,12},{8,0},{12,4},{16,24},{20,28},{24,16},{28,20},{1,9},{5... | collective-permute-start | bytes 196616 | tf_op jit(solution)/shard_map/ppermute | solution.py:245
  152.6 8.9 %collective-permute-start.26 = (bf16[128,256]{1,0:T(8,128)(2,1)S(1)}, bf16[128,256]{1,0:T(8,128)(2,1)S(1)}, u32[]{:S(2)}, u32[]{:S(2)}) collective-permute-start(bf16[128,256]{1,0:T(8,128)(2,1)S(1)} %get-tuple-element.27), channel_id=1, source_target_pairs={{0,16},{4,20},{8,24},{12,28},{16,0},{20,4},{24,8},{28,12},{1,17},{... | collective-permute-start | bytes 196616 | tf_op jit(solution)/shard_map/ppermute | solution.py:245
  155.6 6.4 %collective-permute-start.27 = (bf16[128,256]{1,0:T(8,128)(2,1)S(1)}, bf16[128,256]{1,0:T(8,128)(2,1)S(1)}, u32[]{:S(2)}, u32[]{:S(2)}) collective-permute-start(bf16[128,256]{1,0:T(8,128)(2,1)S(1)} %get-tuple-element.26), channel_id=1, source_target_pairs={{0,24},{4,28},{8,16},{12,20},{16,8},{20,12},{24,0},{28,4},{1,25},{... | collective-permute-start | bytes 196616 | tf_op jit(solution)/shard_map/ppermute | solution.py:245
  157.1 5.5 %collective-permute-start.31 = (bf16[128,256]{1,0:T(8,128)(2,1)S(1)}, bf16[128,256]{1,0:T(8,128)(2,1)S(1)}, u32[]{:S(2)}, u32[]{:S(2)}) collective-permute-start(bf16[128,256]{1,0:T(8,128)(2,1)S(1)} %get-tuple-element.28), channel_id=1, source_target_pairs={{0,8},{4,12},{8,0},{12,4},{16,24},{20,28},{24,16},{28,20},{1,9},{5... | collective-permute-start | bytes 196616 | tf_op jit(solution)/shard_map/ppermute | solution.py:245
  157.2 8.1 %collective-permute-start.32 = (bf16[128,256]{1,0:T(8,128)(2,1)S(1)}, bf16[128,256]{1,0:T(8,128)(2,1)S(1)}, u32[]{:S(2)}, u32[]{:S(2)}) collective-permute-start(bf16[128,256]{1,0:T(8,128)(2,1)S(1)} %get-tuple-element.30), channel_id=1, source_target_pairs={{0,16},{4,20},{8,24},{12,28},{16,0},{20,4},{24,8},{28,12},{1,17},{... | collective-permute-start | bytes 196616 | tf_op jit(solution)/shard_map/ppermute | solution.py:245
  160.2 6.2 %collective-permute-start.33 = (bf16[128,256]{1,0:T(8,128)(2,1)S(1)}, bf16[128,256]{1,0:T(8,128)(2,1)S(1)}, u32[]{:S(2)}, u32[]{:S(2)}) collective-permute-start(bf16[128,256]{1,0:T(8,128)(2,1)S(1)} %get-tuple-element.29), channel_id=1, source_target_pairs={{0,24},{4,28},{8,16},{12,20},{16,8},{20,12},{24,0},{28,4},{1,25},{... | collective-permute-start | bytes 196616 | tf_op jit(solution)/shard_map/ppermute | solution.py:245
  (16 other events, 196.1 us)

commit v2 on v1

v2 whole, which is shorter than its diff:
```python
import functools

import jax
import jax.numpy as jnp
from jax import lax
from jax.experimental import pallas as pl
from jax.experimental.pallas import tpu as pltpu
from jax.sharding import PartitionSpec as P

ADAPTER_RANK = 16
DOUBLE_RANK = 2 * ADAPTER_RANK
CAP = 28
SLOT = 32
GROUP = 8
BF16 = jnp.bfloat16
F32 = jnp.float32
VMEM_BYTES = 12 * 1024 * 1024
EXPAND_BYTES = 46 * 1024 * 1024
UNROLL = 16
COST = pl.CostEstimate(flops=1_000_000, bytes_accessed=1_000, transcendentals=0)
ORDER = (0, 2, 4, 6, 1, 3, 5, 7)
HALVING = (0, 4, 2, 6, 1, 5, 3, 7)


def params(size=VMEM_BYTES):
    return pltpu.CompilerParams(vmem_limit_bytes=size)


def full_spec(shape):
    return pl.BlockSpec(shape, lambda *_: (0,) * len(shape))


def nt_dot(a, b):
    return lax.dot_general(a, b, (((1,), (1,)), ((), ())), preferred_element_type=F32)


def slots_kernel(units, scalar_ref, *refs):
    metas, (pick_ref, place_ref, gain_ref) = refs[:-3], refs[-3:]
    metas = [m.at[n] for m in metas for n in range(m.shape[0])]
    rows = max(units, 8)
    topk = metas[0].shape[0]
    tokens = metas[0].shape[1] // 4
    first = scalar_ref[0]
    expert = (lax.broadcasted_iota(jnp.int32, (rows, tokens), 0) + first).astype(F32)
    token = lax.broadcasted_iota(jnp.int32, (rows, tokens), 1)
    slot = lax.broadcasted_iota(jnp.int32, (units, SLOT, tokens), 1).astype(F32)
    before = (
        lax.broadcasted_iota(jnp.int32, (tokens, tokens), 0)
        < lax.broadcasted_iota(jnp.int32, (tokens, tokens), 1)
    ).astype(BF16)
    for r in range(GROUP):
        live = token < scalar_ref[1 + r]
        meta = metas[r][...].astype(F32)
        ids = meta[:, :tokens]
        weights = meta[:, tokens : 2 * tokens] + meta[:, 2 * tokens : 3 * tokens] + meta[:, 3 * tokens :]
        hit = jnp.zeros((rows, tokens), F32)
        gain = jnp.zeros((rows, tokens), F32)
        for k in range(topk):
            same = jnp.broadcast_to(ids[k : k + 1], (rows, tokens)) == expert
            hit = hit + jnp.where(same, 1.0, 0.0)
            gain = gain + jnp.where(same, jnp.broadcast_to(weights[k : k + 1], (rows, tokens)), 0.0)
        hit = jnp.where(live, hit, 0.0)
        position = jnp.dot(hit.astype(BF16), before, preferred_element_type=F32)
        position = jnp.where(hit > 0.5, position, -1.0)[:units]
        pick = jnp.where(jnp.broadcast_to(position[:, None, :], slot.shape) == slot, 1.0, 0.0)
        gains = jnp.sum(pick * gain[:units][:, None, :], axis=2, keepdims=True)
        gain_ref[:, r * SLOT : (r + 1) * SLOT, :] = jnp.broadcast_to(gains, (units, SLOT, 128))
        pick = pick.reshape(units * SLOT, tokens)
        pick_ref[r] = pick.astype(BF16)
        place_ref[r] = pick.T.astype(BF16)


def make_slots(metas, specs, tokens, scalars, units):
    slots = units * SLOT
    return pl.pallas_call(
        functools.partial(slots_kernel, units),
        grid_spec=pltpu.PrefetchScalarGridSpec(
            num_scalar_prefetch=1,
            grid=(1,),
            in_specs=specs,
            out_specs=[
                full_spec((GROUP, slots, tokens)),
                full_spec((GROUP, tokens, slots)),
                full_spec((units, GROUP * SLOT, 128)),
            ],
        ),
        out_shape=[
            jax.ShapeDtypeStruct((GROUP, slots, tokens), BF16),
            jax.ShapeDtypeStruct((GROUP, tokens, slots), BF16),
            jax.ShapeDtypeStruct((units, GROUP * SLOT, 128), F32),
        ],
        compiler_params=params(),
        cost_estimate=COST,
    )(scalars, *metas)


def expand_kernel(units, quarters, first, layout, final, scalar_ref, *refs):
    count = len(layout)
    groups, refs = refs[: quarters * count], refs[quarters * count :]
    if final:
        pick_ref, gate_hbm, up_hbm, start_ref, low_ref, table_ref = refs[:6]
        out_ref, gathered, both_ref, done, low_rows, tables = refs[6:]
    else:
        pick_ref, gate_hbm, up_hbm, out_ref, gathered, both_ref, done = refs
    tokens, wide = pick_ref.shape[2], gathered.shape[3]
    places = [slice(r * SLOT, (r + 1) * SLOT) for r in range(GROUP)]
    at = [
        pl.ds(pl.multiple_of((scalar_ref[0] ^ (first + turn)) * wide, wide), wide)
        for turn in range(quarters)
    ]

    block = min(units, 4)
    copies = []
    for g in range(units // block):
        part = pl.ds(g * block, block)
        for turn in range(quarters):
            for n, weight in enumerate((gate_hbm, up_hbm)):
                copy = pltpu.make_async_copy(
                    weight.at[part, at[turn], :], both_ref.at[turn, n, part], done.at[g, turn, n]
                )
                copy.start()
                copies.append(copy)

    def scatter(target, r, rows):
        target[:, places[r], :] = rows.astype(BF16).reshape(units, SLOT, rows.shape[1])

    for turn in range(quarters):
        for source, spots in zip(groups[turn * count : (turn + 1) * count], layout, strict=True):
            for n, r in enumerate(spots):
                if len(source.shape) == 2:
                    block_rows = source[:, at[turn]]
                elif source.shape[2] == wide:
                    block_rows = source[n, :tokens, :]
                else:
                    block_rows = source[n, :, at[turn]]
                scatter(gathered.at[turn], r, jnp.dot(pick_ref[r], block_rows, preferred_element_type=F32))
    if final:
        zero = jnp.zeros((SLOT, tokens), BF16)
        for r in range(GROUP):
            spread = jnp.concatenate([zero] * r + [low_ref[r]] + [zero] * (GROUP - 1 - r), axis=0)
            scatter(low_rows, r, nt_dot(pick_ref[r], spread))
            tables[places[r], :] = table_ref[scalar_ref[1 + r]]

    def one(unit, carry):
        value = None
        for turn in range(quarters):
            both = jnp.concatenate([both_ref[turn, 0, unit], both_ref[turn, 1, unit]], axis=1)
            product = jnp.dot(gathered[turn, unit], both, preferred_element_type=F32)
            value = product if value is None else value + product
        if final:
            value = value + jnp.dot(low_rows[unit], tables[...], preferred_element_type=F32)
            value = value + start_ref[unit]
            half = value.shape[1] // 2
            gate, up = value[:, :half], value[:, half:]
            out_ref[unit] = (gate / (1.0 + jnp.exp(-gate)) * up).astype(BF16)
        else:
            out_ref[unit] = value
        return carry

    for g in range(units // block):
        for copy in copies[g * 2 * quarters : (g + 1) * 2 * quarters]:
            copy.wait()
        lax.fori_loop(g * block, (g + 1) * block, one, 0, unroll=block)


def expand(sources, layout, first, scalars, pick, gate_weight, up_weight, final=None):
    units, width, share = gate_weight.shape
    wide = width // 4
    quarters = len(sources) // len(layout)
    rows = GROUP * SLOT
    args = list(sources) + [pick, gate_weight, up_weight]
    scratch = [
        pltpu.VMEM((quarters, units, rows, wide), BF16),
        pltpu.VMEM((quarters, 2, units, wide, share), BF16),
        pltpu.SemaphoreType.DMA((units, quarters, 2)),
    ]
    if final is None:
        out_shape = jax.ShapeDtypeStruct((units, rows, 2 * share), F32)
    else:
        args += list(final)
        out_shape = jax.ShapeDtypeStruct((units, rows, share), BF16)
        scratch += [pltpu.VMEM((units, rows, rows), BF16), pltpu.VMEM((rows, 2 * share), BF16)]
    count = len(sources) + 1
    vmem = pl.BlockSpec(memory_space=pltpu.VMEM)
    hbm = pl.BlockSpec(memory_space=pl.ANY)
    return pl.pallas_call(
        functools.partial(expand_kernel, units, quarters, first, layout, final is not None),
        in_specs=[pl.BlockSpec(memory_space=pltpu.SMEM)] + [vmem] * count + [hbm, hbm] + [vmem] * (len(args) - count - 2),
        out_specs=vmem,
        scratch_shapes=scratch,
        out_shape=out_shape,
        compiler_params=params(EXPAND_BYTES),
        cost_estimate=COST,
    )(scalars, *args)


def contract_kernel(units, jobs, parts, scalar_ref, down_hbm, hidden_ref, place_ref, gain_ref, *refs):
    outs, (table, down_ref, done) = refs[:-3], refs[-3:]
    wide = table.shape[2]
    copies = []
    for n, (part, q) in enumerate(jobs):
        at = pl.ds(pl.multiple_of(((scalar_ref[0] ^ q) * parts + part) * wide, wide), wide)
        copies.append(pltpu.make_async_copy(down_hbm.at[:, at, :], down_ref.at[n], done.at[n]))
        copies[n].start()
    for n in range(len(jobs)):
        copies[n].wait()

        def one(unit, carry, n=n):
            rows = nt_dot(hidden_ref[unit], down_ref[n, unit])
            gain = jnp.concatenate([gain_ref[unit]] * (wide // 128), axis=1)
            spot = pl.ds(pl.multiple_of(unit * SLOT, SLOT), SLOT)
            table[:, spot, :] = (rows * gain).astype(BF16).reshape(GROUP, SLOT, wide)
            return carry

        lax.fori_loop(0, units, one, 0, unroll=min(units, UNROLL))
        for r in range(GROUP):
            sums = jnp.dot(place_ref[r], table[r], preferred_element_type=F32)
            outs[n][r] = sums.astype(outs[n].dtype)


def contract(hidden, down_weight, place, gain, scalars, jobs, parts):
    units, width, share = down_weight.shape
    tokens = place.shape[1]
    wide = width // 4 // parts
    vmem = pl.BlockSpec(memory_space=pltpu.VMEM)
    return pl.pallas_call(
        functools.partial(contract_kernel, units, jobs, parts),
        in_specs=[pl.BlockSpec(memory_space=pltpu.SMEM), pl.BlockSpec(memory_space=pl.ANY)] + [vmem] * 3,
        out_specs=[vmem] * len(jobs),
        scratch_shapes=[
            pltpu.VMEM((GROUP, units * SLOT, wide), BF16),
            pltpu.VMEM((len(jobs), units, wide, share), BF16),
            pltpu.SemaphoreType.DMA((len(jobs),)),
        ],
        out_shape=[jax.ShapeDtypeStruct((GROUP, tokens, wide), BF16 if q % 2 else F32) for _, q in jobs],
        compiler_params=params(EXPAND_BYTES),
        cost_estimate=COST,
    )(scalars, down_weight, hidden, place, gain)


def xor_move(value, axis, bits):
    size = lax.axis_size(axis)
    return lax.ppermute(value, axis, [(i, i ^ bits) for i in range(size)])


def every_request(value, axis="dp"):
    blocks, found = value[None], [0]
    for bits in (4, 2, 1):
        blocks = jnp.concatenate([blocks, xor_move(blocks, axis, bits)], axis=0)
        found = found + [f ^ bits for f in found]
    return [blocks[found.index(n)] for n in range(8)]


def select_adapters(request_adapter, rows_local, row_index):
    wanted = request_adapter[:, None] * DOUBLE_RANK + jnp.arange(DOUBLE_RANK)[None, :]
    held = row_index * rows_local + jnp.arange(rows_local)
    return (wanted.reshape(-1)[:, None] == held[None, :]).astype(BF16)


def widen_tables(tables):
    is_gate = (jnp.arange(DOUBLE_RANK) < ADAPTER_RANK)[None, :, None]
    zero = jnp.zeros_like(tables)
    return jnp.concatenate([jnp.where(is_gate, tables, zero), jnp.where(is_gate, zero, tables)], axis=2)


def meta_of(token_experts, router_weight):
    left = router_weight.T
    terms = []
    for _ in range(3):
        term = lax.reduce_precision(left, 8, 7)
        terms.append(term.astype(BF16))
        left = left - term
    return jnp.concatenate([token_experts.T.astype(BF16)] + terms, axis=1)


def end_along_z(here):
    last = here[0]
    for k in (1, 2, 3):
        last = last + xor_move(here[k].astype(BF16), "dp", 2 * k).astype(F32)
    return last.astype(BF16)


def near_device(
    tokens,
    lengths,
    request_adapter,
    token_experts,
    router_weight,
    gate_weight,
    up_weight,
    down_weight,
    adapter_input_maps,
    adapter_output_maps,
):
    width = tokens.shape[1]
    units = gate_weight.shape[0]
    dp_count = lax.axis_size("dp")
    tp_count = lax.axis_size("tensor")
    i = lax.axis_index("dp")
    j = lax.axis_index("tensor")
    experts_all = units * dp_count // 2
    quarter = width // tp_count
    rel = i ^ jnp.array(ORDER, jnp.int32)
    tok_rows = tokens.shape[0]
    own = lax.dynamic_slice_in_dim(tokens, j * quarter, quarter, 1)

    block = jnp.concatenate([own, meta_of(token_experts, router_weight)], axis=0)
    ahead = [xor_move(block, "dp", n) for n in (1, 2, 4, 6)]
    layout = ((0,), (4, 1, 2, 3), (5, 6, 7))

    natural = i ^ jnp.array(HALVING, jnp.int32)
    adapters = jnp.sum(
        jnp.where(natural[:, None] == jnp.arange(dp_count)[None, :], request_adapter[None, :], 0), axis=1
    )
    columns = nt_dot(select_adapters(adapters, adapter_input_maps.shape[1], i), adapter_input_maps)
    columns = columns.astype(BF16)

    halves = adapter_output_maps.reshape(adapter_output_maps.shape[0], -1)
    tables = jnp.dot(
        select_adapters(request_adapter, halves.shape[0], i), halves, preferred_element_type=F32
    ).astype(BF16)
    share = halves.shape[1] // 2
    upper = i >= dp_count // 2
    first_expert = (i * units) % experts_all
    is_rel = rel[:, None] == jnp.arange(dp_count)[None, :]
    lengths_rel = jnp.sum(jnp.where(is_rel, lengths[None, :], 0), axis=1)
    slot_scalars = jnp.concatenate([first_expert[None], lengths_rel]).astype(jnp.int32)
    scalars = jnp.concatenate([j[None], rel]).astype(jnp.int32)
    strips = quarter // share

    def strip(rows):
        return [rows[:, n * share : (n + 1) * share] for n in range(rows.shape[1] // share)]

    def halve(columns, given, bits):
        kept = columns.shape[0] // 2
        got = xor_move(jnp.concatenate(strip(columns[kept:]) + given, axis=0), "dp", bits)
        more = jnp.concatenate([got[n * kept : (n + 1) * kept] for n in range(strips)], axis=1)
        got = got[strips * kept :]
        size = given[0].shape[0]
        return columns[:kept] + more, [got[n * size : (n + 1) * size] for n in range(len(given))]

    tables = strip(tables)
    for bits in (1, 2):
        columns, came = halve(columns, tables, bits)
        tables = [t + c for t, c in zip(tables, came, strict=True)]
    mine, other = jnp.where(upper, tables[1], tables[0]), jnp.where(upper, tables[0], tables[1])

    ahead, columns, mine, other = lax.optimization_barrier((ahead, columns, mine, other))
    behind = xor_move(jnp.stack(ahead[1:]), "dp", 1)
    ahead = jnp.stack(ahead)
    side_ahead = xor_move(ahead, "tensor", 2)
    core_ahead = xor_move(ahead, "tensor", 1)
    columns, came = halve(columns, [other], 4)
    tables = mine + came[0]
    low = nt_dot(columns, own)
    low = low + xor_move(low, "tensor", 1)

    behind, low, tables, side_ahead = lax.optimization_barrier((behind, low, tables, side_ahead))
    low = low + xor_move(low, "tensor", 2)
    side_behind = xor_move(behind, "tensor", 2)
    core_behind = xor_move(behind, "tensor", 1)
    low = every_request(low.astype(BF16))
    low = jnp.stack([low[n] for n in ORDER])
    both_ahead = xor_move(side_ahead, "tensor", 1)
    tables = widen_tables(tables.reshape(dp_count, DOUBLE_RANK, share))

    routes = block.shape[0] - tok_rows
    meta_specs = [
        pl.BlockSpec((n, routes, quarter), lambda *_: (0, tok_rows // routes, 0)) for n in (1, 3, 1, 3)
    ]
    meta_specs[2] = pl.BlockSpec((1, routes, quarter), lambda *_: (0, tok_rows // routes, 0))
    meta_specs[1] = pl.BlockSpec((3, routes, quarter), lambda *_: (0, tok_rows // routes, 0))
    pick, place, gain = make_slots(
        [block[None], ahead[1:], ahead[:1], behind], meta_specs, tok_rows, slot_scalars, units
    )

    def sources(*pairs):
        return [x for pair in pairs for x in (tokens,) + pair]

    start = expand(
        sources((ahead, behind), (core_ahead, core_behind)), layout, 0, scalars, pick, gate_weight, up_weight
    )
    start, side_behind = lax.optimization_barrier((start, side_behind))
    both_behind = xor_move(side_behind, "tensor", 1)
    hidden = expand(
        sources((side_ahead, side_behind), (both_ahead, both_behind)),
        layout,
        2,
        scalars,
        pick,
        gate_weight,
        up_weight,
        (start, low, tables),
    )

    def core_sum(send, keep):
        return keep + xor_move(send, "tensor", 1).astype(F32)

    early = contract(hidden, down_weight, place, gain, scalars, ((0, 3), (0, 2)), 2)
    there = core_sum(*early).astype(BF16)
    there, hidden = lax.optimization_barrier((there, hidden))
    late = ((1, 3), (1, 2), (1, 1), (1, 0), (0, 1), (0, 0))
    late = contract(hidden, down_weight, place, gain, scalars, late, 2)

    here = core_sum(*late[4:]) + xor_move(there, "tensor", 2).astype(F32)
    here = here[:4] + xor_move(here[4:].astype(BF16), "dp", 1).astype(F32)
    first = end_along_z(here)

    here, there = core_sum(*late[2:4]), core_sum(*late[:2])
    sums = xor_move(jnp.stack([here[4:].astype(BF16), there[4:].astype(BF16)]), "dp", 1).astype(F32)
    here, there = here[:4] + sums[0], there[:4] + sums[1]
    here = here + xor_move(there.astype(BF16), "tensor", 2).astype(F32)
    second = end_along_z(here)
    return jnp.concatenate([first, second], axis=1)


def any_device(
    tokens,
    lengths,
    request_adapter,
    token_experts,
    router_weight,
    gate_weight,
    up_weight,
    down_weight,
    adapter_input_maps,
    adapter_output_maps,
):
    tok_rows, width = tokens.shape
    units = gate_weight.shape[0]
    dp_count = lax.axis_size("dp")
    tp_count = lax.axis_size("tensor")
    i = lax.axis_index("dp")
    j = lax.axis_index("tensor")
    experts_all = units * dp_count // 2
    quarter = width // tp_count
    meta = lax.all_gather(meta_of(token_experts, router_weight), "dp", axis=0)
    rows = lax.all_gather(tokens, "dp", axis=0)
    maps = lax.all_gather(adapter_input_maps, "dp", axis=1, tiled=True)
    adapter = jnp.sum(jnp.where(jnp.arange(dp_count) == i, request_adapter, 0))
    columns = nt_dot(select_adapters(adapter[None], maps.shape[1], 0), maps).astype(BF16)
    x_part = lax.dynamic_slice_in_dim(tokens, j * quarter, quarter, 1)
    low = lax.psum(nt_dot(columns, x_part), "tensor").astype(BF16)
    low = lax.all_gather(low, "dp", axis=0)
    every = lax.all_gather(adapter_output_maps, "dp", axis=0, tiled=True)
    half = jnp.where(i * units >= experts_all, every[:, 1], every[:, 0])
    tables = jnp.dot(
        select_adapters(request_adapter, half.shape[0], 0), half, preferred_element_type=F32
    ).astype(BF16)
    tables = widen_tables(tables.reshape(dp_count, DOUBLE_RANK, half.shape[1]))
    first_expert = (i * units) % experts_all
    natural = jnp.concatenate([j[None], jnp.arange(GROUP)]).astype(jnp.int32)

    def one_group(group):
        meta_g, rows_g, low_g, tables_g, lengths_g = group
        pick, place, gain = make_slots(
            [meta_g],
            [full_spec(meta_g.shape)],
            tok_rows,
            jnp.concatenate([first_expert[None], lengths_g]).astype(jnp.int32),
            units,
        )
        layout = (tuple(range(GROUP)),)

        start = expand([rows_g] * 2, layout, 0, natural, pick, gate_weight, up_weight)
        hidden = expand(
            [rows_g] * 2, layout, 2, natural, pick, gate_weight, up_weight, (start, low_g, tables_g)
        )
        jobs = tuple((0, q) for q in range(4))
        sums = contract(hidden, down_weight, place, gain, natural, jobs, 1)
        return tuple(a.astype(BF16) for a in sums)

    groups = dp_count // GROUP
    grouped = [
        a.reshape((groups, GROUP) + a.shape[1:]) for a in (meta, rows, low, tables, lengths)
    ]
    sums = lax.map(one_group, tuple(grouped))
    sums = [a.reshape(dp_count * tok_rows, quarter) for a in sums]
    here = sums[0].astype(F32)
    for q in range(1, 4):
        here = here + xor_move(sums[q], "tensor", q).astype(F32)
    return lax.psum_scatter(here, "dp", scatter_dimension=0, tiled=True).astype(BF16)


def solution(mesh):
    near = mesh.shape["dp"] == 8 and mesh.shape["tensor"] == 4
    in_specs = (
        P("dp", None),
        P(),
        P(),
        P("dp", None),
        P("dp", None),
        P("dp", None, "tensor"),
        P("dp", None, "tensor"),
        P("dp", None, "tensor"),
        P("tensor", "dp"),
        P("dp", None, "tensor"),
    )
    return jax.shard_map(
        near_device if near else any_device,
        mesh=mesh,
        in_specs=in_specs,
        out_specs=P("dp", "tensor"),
        check_vma=False,
    )
```

time: 168 us -> 132 us (0.79)
  Pallas kernels: 60.7 us -> 33.7 us
  waiting for transfers between devices: 57.1 us -> 53.3 us
  starting transfers between devices: 34.2 us -> 32.3 us
  other arithmetic: 9.23 us -> 7.52 us
    pallas_call x4, Pallas kernels: 56.5 us -> 32.1 us  [the longest x2 18.4 us: expand(): pl.pallas_call(functools.partial(expand_kernel, units, quarters, first, l...]
    ppermute x34 -> x33, waiting for transfers between devices: 57.1 us -> 53.3 us  [xor_move(): return lax.ppermute(value, axis, [(i, i ^ bits) for i in range(size)])]
    pallas_call x1, Pallas kernels: 4.19 us -> 1.6 us  [make_slots(): pl.pallas_call(functools.partial(slots_kernel, units), grid_spec=pltpu.Pr...]
    ppermute x34 -> x33, starting transfers between devices: 34.2 us -> 32.3 us  [xor_move(): return lax.ppermute(value, axis, [(i, i ^ bits) for i in range(size)])]
  transfers between devices with their start and end apart: 34 -> 33, of which waited for: 18 -> 18; matrix products, arithmetic and copies ran while one was open for 5% -> 5% of each run, Pallas kernels for 19% -> 7%
where the time goes in v2:
time: 132 us
  waiting for transfers between devices  53.3 us (40%)
  Pallas kernels  33.7 us (26%)
  starting transfers between devices  32.3 us (24%)
  other arithmetic  7.52 us (6%)
  local copies, waits for them, and re-layouts  3.38 us (3%)
  matrix products  1.54 us (1%)
    ppermute x33, waiting for transfers between devices, xor_move(): return lax.ppermute(value, axis, [(i, i ^ bits) for i in range(size)])  53.3 us
    ppermute x33, starting transfers between devices, xor_move(): return lax.ppermute(value, axis, [(i, i ^ bits) for i in range(size)])  32.3 us
    pallas_call x2, Pallas kernels, expand(): pl.pallas_call(functools.partial(expand_kernel, units, quarters, first, l...  18.4 us
    pallas_call x2, Pallas kernels, contract(): pl.pallas_call(functools.partial(contract_kernel, units, jobs, parts), in...  13.7 us
  transfers between devices with their start and end apart: 33, of which 18 were waited for; matrix products, arithmetic and copies ran while one was open for 5% of the time, Pallas kernels for 7%

profile of v2, /device:TPU:0, one launch (start us, length us, event | category | flops | bytes accessed | tf_op | source)
XLA Modules:
  0.0 132.2 jit_solution(5572033701805466307)
XLA Ops:
  2.4 3.0 %collective-permute-start = (bf16[136,512]{1,0:T(8,128)(2,1)S(1)}, bf16[136,512]{1,0:T(8,128)(2,1)S(1)}, u32[]{:S(2)}, u32[]{:S(2)}) collective-permute-start(bf16[136,512]{1,0:T(8,128)(2,1)S(1)} %maximum_maximum_fusion), channel_id=1, source_target_pairs={{0,4},{4,0},{8,12},{12,8},{16,20},{20,16},{24,28},{28,24},{1,5},{5... | collective-permute-start | bytes 417800 | tf_op jit(solution)/shard_map/ppermute | solution.py:243
  5.4 1.6 %collective-permute-start.1 = (bf16[136,512]{1,0:T(8,128)(2,1)S(1)}, bf16[136,512]{1,0:T(8,128)(2,1)S(1)}, u32[]{:S(2)}, u32[]{:S(2)}) collective-permute-start(bf16[136,512]{1,0:T(8,128)(2,1)S(1)} %maximum_maximum_fusion), channel_id=1, source_target_pairs={{0,8},{4,12},{8,0},{12,4},{16,24},{20,28},{24,16},{28,20},{1,9},{5... | collective-permute-start | bytes 417800 | tf_op jit(solution)/shard_map/ppermute | solution.py:243
  7.0 2.6 %collective-permute-start.2 = (bf16[136,512]{1,0:T(8,128)(2,1)S(1)}, bf16[136,512]{1,0:T(8,128)(2,1)S(1)}, u32[]{:S(2)}, u32[]{:S(2)}) collective-permute-start(bf16[136,512]{1,0:T(8,128)(2,1)S(1)} %maximum_maximum_fusion), channel_id=1, source_target_pairs={{0,16},{4,20},{8,24},{12,28},{16,0},{20,4},{24,8},{28,12},{1,17},{... | collective-permute-start | bytes 417800 | tf_op jit(solution)/shard_map/ppermute | solution.py:243
  15.7 5.2 %collective-permute-done.4 = bf16[1024,128]{1,0:T(8,128)(2,1)S(1)} collective-permute-done((bf16[1024,128]{1,0:T(8,128)(2,1)S(1)}, bf16[1024,128]{1,0:T(8,128)(2,1)S(1)}, u32[]{:S(2)}, u32[]{:S(2)}) %collective-permute-start.4) | collective-permute-done | bytes 262176 | tf_op jit(solution)/shard_map/ppermute | solution.py:243
  21.8 5.0 %collective-permute-done.5 = bf16[768,128]{1,0:T(8,128)(2,1)S(1)} collective-permute-done((bf16[768,128]{1,0:T(8,128)(2,1)S(1)}, bf16[768,128]{1,0:T(8,128)(2,1)S(1)}, u32[]{:S(2)}, u32[]{:S(2)}) %collective-permute-start.5) | collective-permute-done | bytes 196640 | tf_op jit(solution)/shard_map/ppermute | solution.py:243
  27.0 1.6 %collective-permute-start.9 = (bf16[4,136,512]{2,1,0:T(8,128)(2,1)S(1)}, bf16[4,136,512]{2,1,0:T(8,128)(2,1)S(1)}, u32[]{:S(2)}, u32[]{:S(2)}) collective-permute-start(bf16[4,136,512]{2,1,0:T(8,128)(2,1)S(1)} %pad_maximum_fusion.refs_1_), channel_id=1, source_target_pairs={{0,2},{1,3},{2,0},{3,1},{4,6},{5,7},{6,4},{7,5},{8,10},{9,11},{10,... | collective-permute-start | bytes 1671176 | tf_op jit(solution)/shard_map/ppermute | solution.py:243
  28.6 2.1 %collective-permute-start.7 = (bf16[384,128]{1,0:T(8,128)(2,1)S(1)}, bf16[384,128]{1,0:T(8,128)(2,1)S(1)}, u32[]{:S(2)}, u32[]{:S(2)}) collective-permute-start(bf16[384,128]{1,0:T(8,128)(2,1)S(1)} %constant_dynamic-update-slice_fusion.10), channel_id=1, source_target_pairs={{0,16},{4,20},{8,24},{12,28},{16,0},{20,4},{24,8},{28,12},{1,17},{... | collective-permute-start | bytes 294920 | tf_op jit(solution)/shard_map/ppermute | solution.py:243
  31.3 3.9 %collective-permute-done.7 = bf16[384,128]{1,0:T(8,128)(2,1)S(1)} collective-permute-done((bf16[384,128]{1,0:T(8,128)(2,1)S(1)}, bf16[384,128]{1,0:T(8,128)(2,1)S(1)}, u32[]{:S(2)}, u32[]{:S(2)}) %collective-permute-start.7) | collective-permute-done | bytes 98336 | tf_op jit(solution)/shard_map/ppermute | solution.py:243
  35.4 1.2 collective-permute-done.8
  36.6 2.3 %collective-permute-done.6.refs_3_.refs_2_ = bf16[3,136,512]{2,1,0:T(8,128)(2,1)S(1)} collective-permute-done((bf16[3,136,512]{2,1,0:T(8,128)(2,1)S(1)}, bf16[3,136,512]{2,1,0:T(8,128)(2,1)S(1)}, u32[]{:S(2)}, u32[]{:S(2)}) %collective-permute-start.6) | collective-permute-done | bytes 417824 | tf_op jit(solution)/shard_map/ppermute | solution.py:243
  40.3 1.1 collective-permute-start.12
  42.6 1.7 %collective-permute-start.16 = (bf16[1,32,128]{2,1,0:T(8,128)(2,1)S(1)}, bf16[1,32,128]{2,1,0:T(8,128)(2,1)S(1)}, u32[]{:S(2)}, u32[]{:S(2)}) collective-permute-start(bf16[1,32,128]{2,1,0:T(8,128)(2,1)S(1)} %get-tuple-element.62), channel_id=1, source_target_pairs={{0,16},{4,20},{8,24},{12,28},{16,0},{20,4},{24,8},{28,12},{1,17},{... | collective-permute-start | bytes 24584 | tf_op jit(solution)/shard_map/ppermute | solution.py:243
  44.4 2.8 %collective-permute-done.16 = bf16[1,32,128]{2,1,0:T(8,128)(2,1)S(1)} collective-permute-done((bf16[1,32,128]{2,1,0:T(8,128)(2,1)S(1)}, bf16[1,32,128]{2,1,0:T(8,128)(2,1)S(1)}, u32[]{:S(2)}, u32[]{:S(2)}) %collective-permute-start.16) | collective-permute-done | bytes 8224 | tf_op jit(solution)/shard_map/ppermute | solution.py:243
  47.2 2.0 %collective-permute-start.17 = (bf16[2,32,128]{2,1,0:T(8,128)(2,1)S(1)}, bf16[2,32,128]{2,1,0:T(8,128)(2,1)S(1)}, u32[]{:S(2)}, u32[]{:S(2)}) collective-permute-start(bf16[2,32,128]{2,1,0:T(8,128)(2,1)S(1)} %pad_maximum_fusion.6), channel_id=1, source_target_pairs={{0,8},{4,12},{8,0},{12,4},{16,24},{20,28},{24,16},{28,20},{1,9},{5... | collective-permute-start | bytes 49160 | tf_op jit(solution)/shard_map/ppermute | solution.py:243
  49.2 1.6 %shard_map.118 = (bf16[8,512,128]{2,1,0:T(8,128)(2,1)S(1)}, bf16[8,128,512]{2,1,0:T(8,128)(2,1)S(1)}, f32[16,256,128]{2,1,0:T(8,128)S(1)}) custom-call(s32[9]{0:T(128)S(1)} %pad_add_fusion.1.scalar_ref, bf16[1,136,512]{2,1,0:T(8,128)(2,1)S(1)} %fusion.43.refs_0_, bf16[3,136,512]{2,1,0:T(8,128)(2,1)S(1)} %pad_maximum_fusion.2.refs_1_, ...), custom_call_target="tpu_custom_call" | custom-call | flops 1000000 | bytes 1000 | tf_op jit(solution)/shard_map/pallas_call | solution.py:75
  51.5 3.4 %collective-permute-done.18 = bf16[4,32,128]{2,1,0:T(8,128)(2,1)S(1)} collective-permute-done((bf16[4,32,128]{2,1,0:T(8,128)(2,1)S(1)}, bf16[4,32,128]{2,1,0:T(8,128)(2,1)S(1)}, u32[]{:S(2)}, u32[]{:S(2)}) %collective-permute-start.18) | collective-permute-done | bytes 32800 | tf_op jit(solution)/shard_map/ppermute | solution.py:243
  54.9 7.7 %shard_map.119.refs_9_ = f32[16,256,256]{2,1,0:T(8,128)S(1)} custom-call(s32[9]{0:T(128)S(1)} %pad_add_fusion.scalar_ref, bf16[128,2048]{1,0:T(8,128)(2,1)S(1)} %copy-done.2, bf16[4,136,512]{2,1,0:T(8,128)(2,1)S(1)} %pad_maximum_fusion.refs_1_, bf16[3,136,512]{2,1,0:T(8,128)(2,1)S(1)} %collective-permute-done.6.refs_3_.refs_2_, ...), custom_call_target="tpu_custom_call" | custom-call | flops 1000000 | bytes 1000 | tf_op jit(solution)/shard_map/pallas_call | solution.py:186
  62.6 2.0 %copy-done.1 = f32[16,256,256]{2,1,0:T(8,128)} copy-done((f32[16,256,256]{2,1,0:T(8,128)}, f32[16,256,256]{2,1,0:T(8,128)S(1)}, u32[]{:S(2)}) %copy-start.1) | copy-done | bytes 4194328
  64.6 1.7 %collective-permute-done.14.refs_5_ = bf16[3,136,512]{2,1,0:T(8,128)(2,1)S(1)} collective-permute-done((bf16[3,136,512]{2,1,0:T(8,128)(2,1)S(1)}, bf16[3,136,512]{2,1,0:T(8,128)(2,1)S(1)}, u32[]{:S(2)}, u32[]{:S(2)}) %collective-permute-start.14) | collective-permute-done | bytes 417824 | tf_op jit(solution)/shard_map/ppermute | solution.py:243
  66.4 10.7 %shard_map.120.hidden_ref = bf16[16,256,128]{2,1,0:T(8,128)(2,1)S(1)} custom-call(s32[9]{0:T(128)S(1)} %pad_add_fusion.scalar_ref, bf16[128,2048]{1,0:T(8,128)(2,1)S(1)} %copy-done.2, bf16[4,136,512]{2,1,0:T(8,128)(2,1)S(1)} %collective-permute-done.9.refs_1_, bf16[3,136,512]{2,1,0:T(8,128)(2,1)S(1)} %collective-permute-done.12.refs_2_, ...), custom_call_target="tpu_custom_call" | custom-call | flops 1000000 | bytes 1000 | tf_op jit(solution)/shard_map/pallas_call | solution.py:186
  77.1 4.1 %shard_map.121 = (bf16[8,128,256]{2,1,0:T(8,128)(2,1)S(1)}, f32[8,128,256]{2,1,0:T(8,128)S(1)}) custom-call(s32[9]{0:T(128)S(1)} %pad_add_fusion.scalar_ref, bf16[16,2048,128]{2,1,0:T(8,128)(2,1)} %down_hbm.3, bf16[16,256,128]{2,1,0:T(8,128)(2,1)S(1)} %shard_map.120.hidden_ref, bf16[8,128,512]{2,1,0:T(8,128)(2,1)S(1)} %get-tuple-element.45.place_ref, ...), custom_call_target="tpu_custom_call" | custom-call | flops 1000000 | bytes 1000 | tf_op jit(solution)/shard_map/pallas_call | solution.py:226
  81.4 1.8 %collective-permute-done.19 = bf16[8,128,256]{2,1,0:T(8,128)(2,1)S(1)} collective-permute-done((bf16[8,128,256]{2,1,0:T(8,128)(2,1)S(1)}, bf16[8,128,256]{2,1,0:T(8,128)(2,1)S(1)}, u32[]{:S(2)}, u32[]{:S(2)}) %collective-permute-start.19) | collective-permute-done | bytes 524320 | tf_op jit(solution)/shard_map/ppermute | solution.py:243
  83.3 9.6 %shard_map.122 = (bf16[8,128,256]{2,1,0:T(8,128)(2,1)S(1)}, f32[8,128,256]{2,1,0:T(8,128)S(1)}, bf16[8,128,256]{2,1,0:T(8,128)(2,1)S(1)}, f32[8,128,256]{2,1,0:T...) custom-call(s32[9]{0:T(128)S(1)} %pad_add_fusion.scalar_ref, bf16[16,2048,128]{2,1,0:T(8,128)(2,1)} %down_hbm.3, ...), custom_call_target="tpu_custom_call" | custom-call | flops 1000000 | bytes 1000 | tf_op jit(solution)/shard_map/pallas_call | solution.py:226
  95.0 1.3 %collective-permute-done.27 = bf16[8,128,256]{2,1,0:T(8,128)(2,1)S(1)} collective-permute-done((bf16[8,128,256]{2,1,0:T(8,128)(2,1)S(1)}, bf16[8,128,256]{2,1,0:T(8,128)(2,1)S(1)}, u32[]{:S(2)}, u32[]{:S(2)}) %collective-permute-start.27) | collective-permute-done | bytes 524320 | tf_op jit(solution)/shard_map/ppermute | solution.py:243
  97.2 10.3 %collective-permute-done.21 = bf16[8,128,256]{2,1,0:T(8,128)(2,1)S(1)} collective-permute-done((bf16[8,128,256]{2,1,0:T(8,128)(2,1)S(1)}, bf16[8,128,256]{2,1,0:T(8,128)(2,1)S(1)}, u32[]{:S(2)}, u32[]{:S(2)}) %collective-permute-start.21) | collective-permute-done | bytes 524320 | tf_op jit(solution)/shard_map/ppermute | solution.py:243
  108.3 3.2 %collective-permute-done.28 = bf16[2,4,128,256]{3,2,1,0:T(8,128)(2,1)S(1)} collective-permute-done((bf16[2,4,128,256]{3,2,1,0:T(8,128)(2,1)S(1)}, bf16[2,4,128,256]{3,2,1,0:T(8,128)(2,1)S(1)}, u32[]{:S(2)}, u32[]{:S(2)}) %collective-permute-start.28) | collective-permute-done | bytes 524320 | tf_op jit(solution)/shard_map/ppermute | solution.py:243
  112.7 3.5 %collective-permute-done.22 = bf16[4,128,256]{2,1,0:T(8,128)(2,1)S(1)} collective-permute-done((bf16[4,128,256]{2,1,0:T(8,128)(2,1)S(1)}, bf16[4,128,256]{2,1,0:T(8,128)(2,1)S(1)}, u32[]{:S(2)}, u32[]{:S(2)}) %collective-permute-start.22) | collective-permute-done | bytes 262176 | tf_op jit(solution)/shard_map/ppermute | solution.py:243
  116.4 2.0 %collective-permute-start.23 = (bf16[128,256]{1,0:T(8,128)(2,1)S(1)}, bf16[128,256]{1,0:T(8,128)(2,1)S(1)}, u32[]{:S(2)}, u32[]{:S(2)}) collective-permute-start(bf16[128,256]{1,0:T(8,128)(2,1)S(1)} %get-tuple-element.65), channel_id=1, source_target_pairs={{0,8},{4,12},{8,0},{12,4},{16,24},{20,28},{24,16},{28,20},{1,9},{5... | collective-permute-start | bytes 196616 | tf_op jit(solution)/shard_map/ppermute | solution.py:243
  118.4 2.2 %collective-permute-start.24 = (bf16[128,256]{1,0:T(8,128)(2,1)S(1)}, bf16[128,256]{1,0:T(8,128)(2,1)S(1)}, u32[]{:S(2)}, u32[]{:S(2)}) collective-permute-start(bf16[128,256]{1,0:T(8,128)(2,1)S(1)} %get-tuple-element.67), channel_id=1, source_target_pairs={{0,16},{4,20},{8,24},{12,28},{16,0},{20,4},{24,8},{28,12},{1,17},{... | collective-permute-start | bytes 196616 | tf_op jit(solution)/shard_map/ppermute | solution.py:243
  122.1 3.1 %collective-permute-start.31 = (bf16[128,256]{1,0:T(8,128)(2,1)S(1)}, bf16[128,256]{1,0:T(8,128)(2,1)S(1)}, u32[]{:S(2)}, u32[]{:S(2)}) collective-permute-start(bf16[128,256]{1,0:T(8,128)(2,1)S(1)} %get-tuple-element.70), channel_id=1, source_target_pairs={{0,16},{4,20},{8,24},{12,28},{16,0},{20,4},{24,8},{28,12},{1,17},{... | collective-permute-start | bytes 196616 | tf_op jit(solution)/shard_map/ppermute | solution.py:243
  125.4 1.5 %collective-permute-done.24 = bf16[128,256]{1,0:T(8,128)(2,1)S(1)} collective-permute-done((bf16[128,256]{1,0:T(8,128)(2,1)S(1)}, bf16[128,256]{1,0:T(8,128)(2,1)S(1)}, u32[]{:S(2)}, u32[]{:S(2)}) %collective-permute-start.24) | collective-permute-done | bytes 65568 | tf_op jit(solution)/shard_map/ppermute | solution.py:243
  127.0 4.5 %collective-permute-done.31 = bf16[128,256]{1,0:T(8,128)(2,1)S(1)} collective-permute-done((bf16[128,256]{1,0:T(8,128)(2,1)S(1)}, bf16[128,256]{1,0:T(8,128)(2,1)S(1)}, u32[]{:S(2)}, u32[]{:S(2)}) %collective-permute-start.31) | collective-permute-done | bytes 65568 | tf_op jit(solution)/shard_map/ppermute | solution.py:243
  (125 shorter events, 21.5 us)
Async XLA Ops:
  2.4 24.4 %collective-permute-start = (bf16[136,512]{1,0:T(8,128)(2,1)S(1)}, bf16[136,512]{1,0:T(8,128)(2,1)S(1)}, u32[]{:S(2)}, u32[]{:S(2)}) collective-permute-start(bf16[136,512]{1,0:T(8,128)(2,1)S(1)} %maximum_maximum_fusion), channel_id=1, source_target_pairs={{0,4},{4,0},{8,12},{12,8},{16,20},{20,16},{24,28},{28,24},{1,5},{5... | collective-permute-start | bytes 417800 | tf_op jit(solution)/shard_map/ppermute | solution.py:243
  5.4 21.4 %collective-permute-start.1 = (bf16[136,512]{1,0:T(8,128)(2,1)S(1)}, bf16[136,512]{1,0:T(8,128)(2,1)S(1)}, u32[]{:S(2)}, u32[]{:S(2)}) collective-permute-start(bf16[136,512]{1,0:T(8,128)(2,1)S(1)} %maximum_maximum_fusion), channel_id=1, source_target_pairs={{0,8},{4,12},{8,0},{12,4},{16,24},{20,28},{24,16},{28,20},{1,9},{5... | collective-permute-start | bytes 417800 | tf_op jit(solution)/shard_map/ppermute | solution.py:243
  7.0 19.9 %collective-permute-start.2 = (bf16[136,512]{1,0:T(8,128)(2,1)S(1)}, bf16[136,512]{1,0:T(8,128)(2,1)S(1)}, u32[]{:S(2)}, u32[]{:S(2)}) collective-permute-start(bf16[136,512]{1,0:T(8,128)(2,1)S(1)} %maximum_maximum_fusion), channel_id=1, source_target_pairs={{0,16},{4,20},{8,24},{12,28},{16,0},{20,4},{24,8},{28,12},{1,17},{... | collective-permute-start | bytes 417800 | tf_op jit(solution)/shard_map/ppermute | solution.py:243
  9.6 17.3 %collective-permute-start.3 = (bf16[136,512]{1,0:T(8,128)(2,1)S(1)}, bf16[136,512]{1,0:T(8,128)(2,1)S(1)}, u32[]{:S(2)}, u32[]{:S(2)}) collective-permute-start(bf16[136,512]{1,0:T(8,128)(2,1)S(1)} %maximum_maximum_fusion), channel_id=1, source_target_pairs={{0,24},{4,28},{8,16},{12,20},{16,8},{20,12},{24,0},{28,4},{1,25},{... | collective-permute-start | bytes 417800 | tf_op jit(solution)/shard_map/ppermute | solution.py:243
  13.8 7.1 %collective-permute-start.4 = (bf16[1024,128]{1,0:T(8,128)(2,1)S(1)}, bf16[1024,128]{1,0:T(8,128)(2,1)S(1)}, u32[]{:S(2)}, u32[]{:S(2)}) collective-permute-start(bf16[1024,128]{1,0:T(8,128)(2,1)S(1)} %slice_dynamic-update-slice_fusion), channel_id=1, source_target_pairs={{0,4},{4,0},{8,12},{12,8},{16,20},{20,16},{24,28},{28,24},{1,5},{5... | collective-permute-start | bytes 786440 | tf_op jit(solution)/shard_map/ppermute | solution.py:243
  21.0 5.7 %collective-permute-start.5 = (bf16[768,128]{1,0:T(8,128)(2,1)S(1)}, bf16[768,128]{1,0:T(8,128)(2,1)S(1)}, u32[]{:S(2)}, u32[]{:S(2)}) collective-permute-start(bf16[768,128]{1,0:T(8,128)(2,1)S(1)} %constant_dynamic-update-slice_fusion.4), channel_id=1, source_target_pairs={{0,8},{4,12},{8,0},{12,4},{16,24},{20,28},{24,16},{28,20},{1,9},{5... | collective-permute-start | bytes 589832 | tf_op jit(solution)/shard_map/ppermute | solution.py:243
  27.0 11.9 %collective-permute-start.9 = (bf16[4,136,512]{2,1,0:T(8,128)(2,1)S(1)}, bf16[4,136,512]{2,1,0:T(8,128)(2,1)S(1)}, u32[]{:S(2)}, u32[]{:S(2)}) collective-permute-start(bf16[4,136,512]{2,1,0:T(8,128)(2,1)S(1)} %pad_maximum_fusion.refs_1_), channel_id=1, source_target_pairs={{0,2},{1,3},{2,0},{3,1},{4,6},{5,7},{6,4},{7,5},{8,10},{9,11},{10,... | collective-permute-start | bytes 1671176 | tf_op jit(solution)/shard_map/ppermute | solution.py:243
  28.6 6.6 %collective-permute-start.7 = (bf16[384,128]{1,0:T(8,128)(2,1)S(1)}, bf16[384,128]{1,0:T(8,128)(2,1)S(1)}, u32[]{:S(2)}, u32[]{:S(2)}) collective-permute-start(bf16[384,128]{1,0:T(8,128)(2,1)S(1)} %constant_dynamic-update-slice_fusion.10), channel_id=1, source_target_pairs={{0,16},{4,20},{8,24},{12,28},{16,0},{20,4},{24,8},{28,12},{1,17},{... | collective-permute-start | bytes 294920 | tf_op jit(solution)/shard_map/ppermute | solution.py:243
  30.8 8.1 %collective-permute-start.6 = (bf16[3,136,512]{2,1,0:T(8,128)(2,1)S(1)}, bf16[3,136,512]{2,1,0:T(8,128)(2,1)S(1)}, u32[]{:S(2)}, u32[]{:S(2)}) collective-permute-start(bf16[3,136,512]{2,1,0:T(8,128)(2,1)S(1)} %pad_maximum_fusion.2.refs_1_), channel_id=1, source_target_pairs={{0,4},{4,0},{8,12},{12,8},{16,20},{20,16},{24,28},{28,24},{1,5},{5... | collective-permute-start | bytes 1253384 | tf_op jit(solution)/shard_map/ppermute | solution.py:243
  38.9 3.7 %collective-permute-start.15 = (f32[32,128]{1,0:T(8,128)S(1)}, f32[32,128]{1,0:T(8,128)S(1)}, u32[]{:S(2)}, u32[]{:S(2)}) collective-permute-start(f32[32,128]{1,0:T(8,128)S(1)} %add.152), channel_id=1, source_target_pairs={{0,2},{1,3},{2,0},{3,1},{4,6},{5,7},{6,4},{7,5},{8,10},{9,11},{10,... | collective-permute-start | bytes 49160 | tf_op jit(solution)/shard_map/ppermute | solution.py:243
  39.8 15.1 %collective-permute-start.10 = (bf16[4,136,512]{2,1,0:T(8,128)(2,1)S(1)}, bf16[4,136,512]{2,1,0:T(8,128)(2,1)S(1)}, u32[]{:S(2)}, u32[]{:S(2)}) collective-permute-start(bf16[4,136,512]{2,1,0:T(8,128)(2,1)S(1)} %pad_maximum_fusion.refs_1_), channel_id=1, source_target_pairs={{0,1},{1,0},{2,3},{3,2},{4,5},{5,4},{6,7},{7,6},{8,9},{9,8},{10,11... | collective-permute-start | bytes 1671176 | tf_op jit(solution)/shard_map/ppermute | solution.py:243
  39.8 15.1 %collective-permute-start.11 = (bf16[3,136,512]{2,1,0:T(8,128)(2,1)S(1)}, bf16[3,136,512]{2,1,0:T(8,128)(2,1)S(1)}, u32[]{:S(2)}, u32[]{:S(2)}) collective-permute-start(bf16[3,136,512]{2,1,0:T(8,128)(2,1)S(1)} %collective-permute-done.6.refs_3_.refs_2_), channel_id=1, source_target_pairs={{0,1},{1,0},{2,3},{3,2},{4,5},{5,4},{6,7},{7,6},{8,9},{9,8},{10,11... | collective-permute-start | bytes 1253384 | tf_op jit(solution)/shard_map/ppermute | solution.py:243
  40.3 24.3 %collective-permute-start.12 = (bf16[3,136,512]{2,1,0:T(8,128)(2,1)S(1)}, bf16[3,136,512]{2,1,0:T(8,128)(2,1)S(1)}, u32[]{:S(2)}, u32[]{:S(2)}) collective-permute-start(bf16[3,136,512]{2,1,0:T(8,128)(2,1)S(1)} %collective-permute-done.6.refs_3_.refs_2_), channel_id=1, source_target_pairs={{0,2},{1,3},{2,0},{3,1},{4,6},{5,7},{6,4},{7,5},{8,10},{9,11},{10,... | collective-permute-start | bytes 1253384 | tf_op jit(solution)/shard_map/ppermute | solution.py:243
  41.5 23.1 %collective-permute-start.13 = (bf16[4,136,512]{2,1,0:T(8,128)(2,1)S(1)}, bf16[4,136,512]{2,1,0:T(8,128)(2,1)S(1)}, u32[]{:S(2)}, u32[]{:S(2)}) collective-permute-start(bf16[4,136,512]{2,1,0:T(8,128)(2,1)S(1)} %collective-permute-done.9.refs_1_), channel_id=1, source_target_pairs={{0,1},{1,0},{2,3},{3,2},{4,5},{5,4},{6,7},{7,6},{8,9},{9,8},{10,11... | collective-permute-start | bytes 1671176 | tf_op jit(solution)/shard_map/ppermute | solution.py:243
  42.6 4.6 %collective-permute-start.16 = (bf16[1,32,128]{2,1,0:T(8,128)(2,1)S(1)}, bf16[1,32,128]{2,1,0:T(8,128)(2,1)S(1)}, u32[]{:S(2)}, u32[]{:S(2)}) collective-permute-start(bf16[1,32,128]{2,1,0:T(8,128)(2,1)S(1)} %get-tuple-element.62), channel_id=1, source_target_pairs={{0,16},{4,20},{8,24},{12,28},{16,0},{20,4},{24,8},{28,12},{1,17},{... | collective-permute-start | bytes 24584 | tf_op jit(solution)/shard_map/ppermute | solution.py:243
  47.2 3.7 %collective-permute-start.17 = (bf16[2,32,128]{2,1,0:T(8,128)(2,1)S(1)}, bf16[2,32,128]{2,1,0:T(8,128)(2,1)S(1)}, u32[]{:S(2)}, u32[]{:S(2)}) collective-permute-start(bf16[2,32,128]{2,1,0:T(8,128)(2,1)S(1)} %pad_maximum_fusion.6), channel_id=1, source_target_pairs={{0,8},{4,12},{8,0},{12,4},{16,24},{20,28},{24,16},{28,20},{1,9},{5... | collective-permute-start | bytes 49160 | tf_op jit(solution)/shard_map/ppermute | solution.py:243
  51.0 3.9 %collective-permute-start.18 = (bf16[4,32,128]{2,1,0:T(8,128)(2,1)S(1)}, bf16[4,32,128]{2,1,0:T(8,128)(2,1)S(1)}, u32[]{:S(2)}, u32[]{:S(2)}) collective-permute-start(bf16[4,32,128]{2,1,0:T(8,128)(2,1)S(1)} %pad_maximum_fusion.5), channel_id=1, source_target_pairs={{0,4},{4,0},{8,12},{12,8},{16,20},{20,16},{24,28},{28,24},{1,5},{5... | collective-permute-start | bytes 98312 | tf_op jit(solution)/shard_map/ppermute | solution.py:243
  64.6 1.8 %collective-permute-start.14 = (bf16[3,136,512]{2,1,0:T(8,128)(2,1)S(1)}, bf16[3,136,512]{2,1,0:T(8,128)(2,1)S(1)}, u32[]{:S(2)}, u32[]{:S(2)}) collective-permute-start(bf16[3,136,512]{2,1,0:T(8,128)(2,1)S(1)} %collective-permute-done.12.refs_2_), channel_id=1, source_target_pairs={{0,1},{1,0},{2,3},{3,2},{4,5},{5,4},{6,7},{7,6},{8,9},{9,8},{10,11... | collective-permute-start | bytes 1253384 | tf_op jit(solution)/shard_map/ppermute | solution.py:243
  81.2 2.0 %collective-permute-start.19 = (bf16[8,128,256]{2,1,0:T(8,128)(2,1)S(1)}, bf16[8,128,256]{2,1,0:T(8,128)(2,1)S(1)}, u32[]{:S(2)}, u32[]{:S(2)}) collective-permute-start(bf16[8,128,256]{2,1,0:T(8,128)(2,1)S(1)} %get-tuple-element.48), channel_id=1, source_target_pairs={{0,1},{1,0},{2,3},{3,2},{4,5},{5,4},{6,7},{7,6},{8,9},{9,8},{10,11... | collective-permute-start | bytes 1572872 | tf_op jit(solution)/shard_map/ppermute | solution.py:243
  92.9 2.0 %collective-permute-start.26 = (bf16[8,128,256]{2,1,0:T(8,128)(2,1)S(1)}, bf16[8,128,256]{2,1,0:T(8,128)(2,1)S(1)}, u32[]{:S(2)}, u32[]{:S(2)}) collective-permute-start(bf16[8,128,256]{2,1,0:T(8,128)(2,1)S(1)} %get-tuple-element.54), channel_id=1, source_target_pairs={{0,1},{1,0},{2,3},{3,2},{4,5},{5,4},{6,7},{7,6},{8,9},{9,8},{10,11... | collective-permute-start | bytes 1572872 | tf_op jit(solution)/shard_map/ppermute | solution.py:243
  93.1 4.1 %collective-permute-start.20 = (bf16[8,128,256]{2,1,0:T(8,128)(2,1)S(1)}, bf16[8,128,256]{2,1,0:T(8,128)(2,1)S(1)}, u32[]{:S(2)}, u32[]{:S(2)}) collective-permute-start(bf16[8,128,256]{2,1,0:T(8,128)(2,1)S(1)} %get-tuple-element.51), channel_id=1, source_target_pairs={{0,1},{1,0},{2,3},{3,2},{4,5},{5,4},{6,7},{7,6},{8,9},{9,8},{10,11... | collective-permute-start | bytes 1572872 | tf_op jit(solution)/shard_map/ppermute | solution.py:243
  93.5 14.0 %collective-permute-start.21 = (bf16[8,128,256]{2,1,0:T(8,128)(2,1)S(1)}, bf16[8,128,256]{2,1,0:T(8,128)(2,1)S(1)}, u32[]{:S(2)}, u32[]{:S(2)}) collective-permute-start(bf16[8,128,256]{2,1,0:T(8,128)(2,1)S(1)} %add_convert_fusion), channel_id=1, source_target_pairs={{0,2},{1,3},{2,0},{3,1},{4,6},{5,7},{6,4},{7,5},{8,10},{9,11},{10,... | collective-permute-start | bytes 1572872 | tf_op jit(solution)/shard_map/ppermute | solution.py:243
  94.3 2.1 %collective-permute-start.27 = (bf16[8,128,256]{2,1,0:T(8,128)(2,1)S(1)}, bf16[8,128,256]{2,1,0:T(8,128)(2,1)S(1)}, u32[]{:S(2)}, u32[]{:S(2)}) collective-permute-start(bf16[8,128,256]{2,1,0:T(8,128)(2,1)S(1)} %get-tuple-element.56), channel_id=1, source_target_pairs={{0,1},{1,0},{2,3},{3,2},{4,5},{5,4},{6,7},{7,6},{8,9},{9,8},{10,11... | collective-permute-start | bytes 1572872 | tf_op jit(solution)/shard_map/ppermute | solution.py:243
  96.6 14.8 %collective-permute-start.28 = (bf16[2,4,128,256]{3,2,1,0:T(8,128)(2,1)S(1)}, bf16[2,4,128,256]{3,2,1,0:T(8,128)(2,1)S(1)}, u32[]{:S(2)}, u32[]{:S(2)}) collective-permute-start(bf16[2,4,128,256]{3,2,1,0:T(8,128)(2,1)S(1)} %pad_maximum_fusion.1), channel_id=1, source_target_pairs={{0,4},{4,0},{8,12},{12,8},{16,20},{20,16},{24,28},{28,24},{1,5},{5... | collective-permute-start | bytes 1572872 | tf_op jit(solution)/shard_map/ppermute | solution.py:243
  107.7 8.6 %collective-permute-start.22 = (bf16[4,128,256]{2,1,0:T(8,128)(2,1)S(1)}, bf16[4,128,256]{2,1,0:T(8,128)(2,1)S(1)}, u32[]{:S(2)}, u32[]{:S(2)}) collective-permute-start(bf16[4,128,256]{2,1,0:T(8,128)(2,1)S(1)} %slice.416), channel_id=1, source_target_pairs={{0,4},{4,0},{8,12},{12,8},{16,20},{20,16},{24,28},{28,24},{1,5},{5... | collective-permute-start | bytes 786440 | tf_op jit(solution)/shard_map/ppermute | solution.py:243
  111.6 9.2 %collective-permute-start.29 = (bf16[4,128,256]{2,1,0:T(8,128)(2,1)S(1)}, bf16[4,128,256]{2,1,0:T(8,128)(2,1)S(1)}, u32[]{:S(2)}, u32[]{:S(2)}) collective-permute-start(bf16[4,128,256]{2,1,0:T(8,128)(2,1)S(1)} %fusion.1), channel_id=1, source_target_pairs={{0,2},{1,3},{2,0},{3,1},{4,6},{5,7},{6,4},{7,5},{8,10},{9,11},{10,... | collective-permute-start | bytes 786440 | tf_op jit(solution)/shard_map/ppermute | solution.py:243
  116.4 8.8 %collective-permute-start.23 = (bf16[128,256]{1,0:T(8,128)(2,1)S(1)}, bf16[128,256]{1,0:T(8,128)(2,1)S(1)}, u32[]{:S(2)}, u32[]{:S(2)}) collective-permute-start(bf16[128,256]{1,0:T(8,128)(2,1)S(1)} %get-tuple-element.65), channel_id=1, source_target_pairs={{0,8},{4,12},{8,0},{12,4},{16,24},{20,28},{24,16},{28,20},{1,9},{5... | collective-permute-start | bytes 196616 | tf_op jit(solution)/shard_map/ppermute | solution.py:243
  118.4 8.5 %collective-permute-start.24 = (bf16[128,256]{1,0:T(8,128)(2,1)S(1)}, bf16[128,256]{1,0:T(8,128)(2,1)S(1)}, u32[]{:S(2)}, u32[]{:S(2)}) collective-permute-start(bf16[128,256]{1,0:T(8,128)(2,1)S(1)} %get-tuple-element.67), channel_id=1, source_target_pairs={{0,16},{4,20},{8,24},{12,28},{16,0},{20,4},{24,8},{28,12},{1,17},{... | collective-permute-start | bytes 196616 | tf_op jit(solution)/shard_map/ppermute | solution.py:243
  120.6 6.3 %collective-permute-start.25 = (bf16[128,256]{1,0:T(8,128)(2,1)S(1)}, bf16[128,256]{1,0:T(8,128)(2,1)S(1)}, u32[]{:S(2)}, u32[]{:S(2)}) collective-permute-start(bf16[128,256]{1,0:T(8,128)(2,1)S(1)} %get-tuple-element.66), channel_id=1, source_target_pairs={{0,24},{4,28},{8,16},{12,20},{16,8},{20,12},{24,0},{28,4},{1,25},{... | collective-permute-start | bytes 196616 | tf_op jit(solution)/shard_map/ppermute | solution.py:243
  121.0 6.0 %collective-permute-start.30 = (bf16[128,256]{1,0:T(8,128)(2,1)S(1)}, bf16[128,256]{1,0:T(8,128)(2,1)S(1)}, u32[]{:S(2)}, u32[]{:S(2)}) collective-permute-start(bf16[128,256]{1,0:T(8,128)(2,1)S(1)} %get-tuple-element.68), channel_id=1, source_target_pairs={{0,8},{4,12},{8,0},{12,4},{16,24},{20,28},{24,16},{28,20},{1,9},{5... | collective-permute-start | bytes 196616 | tf_op jit(solution)/shard_map/ppermute | solution.py:243
  122.1 9.4 %collective-permute-start.31 = (bf16[128,256]{1,0:T(8,128)(2,1)S(1)}, bf16[128,256]{1,0:T(8,128)(2,1)S(1)}, u32[]{:S(2)}, u32[]{:S(2)}) collective-permute-start(bf16[128,256]{1,0:T(8,128)(2,1)S(1)} %get-tuple-element.70), channel_id=1, source_target_pairs={{0,16},{4,20},{8,24},{12,28},{16,0},{20,4},{24,8},{28,12},{1,17},{... | collective-permute-start | bytes 196616 | tf_op jit(solution)/shard_map/ppermute | solution.py:243
  125.2 6.2 %collective-permute-start.32 = (bf16[128,256]{1,0:T(8,128)(2,1)S(1)}, bf16[128,256]{1,0:T(8,128)(2,1)S(1)}, u32[]{:S(2)}, u32[]{:S(2)}) collective-permute-start(bf16[128,256]{1,0:T(8,128)(2,1)S(1)} %get-tuple-element.69), channel_id=1, source_target_pairs={{0,24},{4,28},{8,16},{12,20},{16,8},{20,12},{24,0},{28,4},{1,25},{... | collective-permute-start | bytes 196616 | tf_op jit(solution)/shard_map/ppermute | solution.py:243
  (5 other events, 96.5 us)

commit v3 on v2

--- a/solution.py
+++ b/solution.py
@@ -20,6 +20,7 @@
 COST = pl.CostEstimate(flops=1_000_000, bytes_accessed=1_000, transcendentals=0)
 ORDER = (0, 2, 4, 6, 1, 3, 5, 7)
 HALVING = (0, 4, 2, 6, 1, 5, 3, 7)
+GATHERED = (0, 4, 2, 6, 1, 5, 3, 7)
 
 
 def params(size=VMEM_BYTES):
@@ -243,14 +244,6 @@
     return lax.ppermute(value, axis, [(i, i ^ bits) for i in range(size)])
 
 
-def every_request(value, axis="dp"):
-    blocks, found = value[None], [0]
-    for bits in (4, 2, 1):
-        blocks = jnp.concatenate([blocks, xor_move(blocks, axis, bits)], axis=0)
-        found = found + [f ^ bits for f in found]
-    return [blocks[found.index(n)] for n in range(8)]
-
-
 def select_adapters(request_adapter, rows_local, row_index):
     wanted = request_adapter[:, None] * DOUBLE_RANK + jnp.arange(DOUBLE_RANK)[None, :]
     held = row_index * rows_local + jnp.arange(rows_local)
@@ -340,16 +333,17 @@
         return columns[:kept] + more, [got[n * size : (n + 1) * size] for n in range(len(given))]
 
     tables = strip(tables)
-    for bits in (1, 2):
-        columns, came = halve(columns, tables, bits)
-        tables = [t + c for t, c in zip(tables, came, strict=True)]
-    mine, other = jnp.where(upper, tables[1], tables[0]), jnp.where(upper, tables[0], tables[1])
-
-    ahead, columns, mine, other = lax.optimization_barrier((ahead, columns, mine, other))
+    columns, came = halve(columns, tables, 1)
+    tables = [t + c for t, c in zip(tables, came, strict=True)]
+
+    ahead, columns, tables = lax.optimization_barrier((ahead, columns, tables))
     behind = xor_move(jnp.stack(ahead[1:]), "dp", 1)
     ahead = jnp.stack(ahead)
     side_ahead = xor_move(ahead, "tensor", 2)
     core_ahead = xor_move(ahead, "tensor", 1)
+    columns, came = halve(columns, tables, 2)
+    tables = [t + c for t, c in zip(tables, came, strict=True)]
+    mine, other = jnp.where(upper, tables[1], tables[0]), jnp.where(upper, tables[0], tables[1])
     columns, came = halve(columns, [other], 4)
     tables = mine + came[0]
     low = nt_dot(columns, own)
@@ -359,8 +353,9 @@
     low = low + xor_move(low, "tensor", 2)
     side_behind = xor_move(behind, "tensor", 2)
     core_behind = xor_move(behind, "tensor", 1)
-    low = every_request(low.astype(BF16))
-    low = jnp.stack([low[n] for n in ORDER])
+    low = low.astype(BF16)[None]
+    for bits in (4, 2):
+        low = jnp.concatenate([low, xor_move(low, "dp", bits)], axis=0)
     both_ahead = xor_move(side_ahead, "tensor", 1)
     tables = widen_tables(tables.reshape(dp_count, DOUBLE_RANK, share))
 
@@ -380,7 +375,9 @@
     start = expand(
         sources((ahead, behind), (core_ahead, core_behind)), layout, 0, scalars, pick, gate_weight, up_weight
     )
-    start, side_behind = lax.optimization_barrier((start, side_behind))
+    start, side_behind, low = lax.optimization_barrier((start, side_behind, low))
+    low = jnp.concatenate([low, xor_move(low, "dp", 1)], axis=0)
+    low = jnp.stack([low[GATHERED.index(n)] for n in ORDER])
     both_behind = xor_move(side_behind, "tensor", 1)
     hidden = expand(
         sources((side_ahead, side_behind), (both_ahead, both_behind)),
@@ -396,20 +393,23 @@
     def core_sum(send, keep):
         return keep + xor_move(send, "tensor", 1).astype(F32)
 
-    early = contract(hidden, down_weight, place, gain, scalars, ((0, 3), (0, 2)), 2)
-    there = core_sum(*early).astype(BF16)
-    there, hidden = lax.optimization_barrier((there, hidden))
-    late = ((1, 3), (1, 2), (1, 1), (1, 0), (0, 1), (0, 0))
-    late = contract(hidden, down_weight, place, gain, scalars, late, 2)
-
-    here = core_sum(*late[4:]) + xor_move(there, "tensor", 2).astype(F32)
-    here = here[:4] + xor_move(here[4:].astype(BF16), "dp", 1).astype(F32)
+    early = contract(hidden, down_weight, place, gain, scalars, ((1, 3), (1, 2), (0, 3), (0, 2)), 2)
+    there = core_sum(*early[2:]).astype(BF16)
+    second_there = core_sum(*early[:2])
+    there, second_there, hidden = lax.optimization_barrier((there, second_there, hidden))
+    above = xor_move(there[4:], "tensor", 2)
+    below = xor_move(there[:4], "tensor", 2)
+    across = xor_move(second_there[4:].astype(BF16), "dp", 1)
+
+    late = contract(hidden, down_weight, place, gain, scalars, ((0, 1), (0, 0), (1, 1), (1, 0)), 2)
+    late, above, across = lax.optimization_barrier((late, above, across))
+    second_there = xor_move((second_there[:4] + across.astype(F32)).astype(BF16), "tensor", 2)
+    here = core_sum(*late[:2])
+    given = (here[4:] + above.astype(F32)).astype(BF16)
+    here = here[:4] + below.astype(F32) + xor_move(given, "dp", 1).astype(F32)
     first = end_along_z(here)
-
-    here, there = core_sum(*late[2:4]), core_sum(*late[:2])
-    sums = xor_move(jnp.stack([here[4:].astype(BF16), there[4:].astype(BF16)]), "dp", 1).astype(F32)
-    here, there = here[:4] + sums[0], there[:4] + sums[1]
-    here = here + xor_move(there.astype(BF16), "tensor", 2).astype(F32)
+    here = core_sum(*late[2:])
+    here = here[:4] + xor_move(here[4:].astype(BF16), "dp", 1).astype(F32) + second_there.astype(F32)
     second = end_along_z(here)
     return jnp.concatenate([first, second], axis=1)
 

time: 132 us -> 120 us (0.909)
  waiting for transfers between devices: 53.3 us -> 40.1 us
  starting transfers between devices: 32.3 us -> 34.1 us
    ppermute x33 -> x35, waiting for transfers between devices: 53.3 us -> 40.1 us  [xor_move(): return lax.ppermute(value, axis, [(i, i ^ bits) for i in range(size)])]
    ppermute x33 -> x35, starting transfers between devices: 32.3 us -> 34.1 us  [xor_move(): return lax.ppermute(value, axis, [(i, i ^ bits) for i in range(size)])]
  transfers between devices with their start and end apart: 33 -> 35, of which waited for: 18 -> 17; matrix products, arithmetic and copies ran while one was open for 5% -> 6% of each run, Pallas kernels for 7% -> 13%
where the time goes in v3:
time: 120 us
  waiting for transfers between devices  40.1 us (33%)
  starting transfers between devices  34.1 us (28%)
  Pallas kernels  32.7 us (27%)
  other arithmetic  7.37 us (6%)
  local copies, waits for them, and re-layouts  3.4 us (3%)
  matrix products  1.54 us (1%)
    ppermute x35, waiting for transfers between devices, xor_move(): return lax.ppermute(value, axis, [(i, i ^ bits) for i in range(size)])  40.1 us
    ppermute x35, starting transfers between devices, xor_move(): return lax.ppermute(value, axis, [(i, i ^ bits) for i in range(size)])  34.1 us
    pallas_call x2, Pallas kernels, expand(): pl.pallas_call(functools.partial(expand_kernel, units, quarters, first, l...  18.4 us
    pallas_call x2, Pallas kernels, contract(): pl.pallas_call(functools.partial(contract_kernel, units, jobs, parts), in...  12.7 us
  transfers between devices with their start and end apart: 35, of which 17 were waited for; matrix products, arithmetic and copies ran while one was open for 6% of the time, Pallas kernels for 13%

profile of v3, /device:TPU:0, one launch (start us, length us, event | category | flops | bytes accessed | tf_op | source)
XLA Modules:
  0.0 119.6 jit_solution(11900167584753247753)
XLA Ops:
  2.4 3.0 %collective-permute-start = (bf16[136,512]{1,0:T(8,128)(2,1)S(1)}, bf16[136,512]{1,0:T(8,128)(2,1)S(1)}, u32[]{:S(2)}, u32[]{:S(2)}) collective-permute-start(bf16[136,512]{1,0:T(8,128)(2,1)S(1)} %maximum_maximum_fusion), channel_id=1, source_target_pairs={{0,4},{4,0},{8,12},{12,8},{16,20},{20,16},{24,28},{28,24},{1,5},{5... | collective-permute-start | bytes 417800 | tf_op jit(solution)/shard_map/ppermute | solution.py:244
  5.4 1.6 %collective-permute-start.1 = (bf16[136,512]{1,0:T(8,128)(2,1)S(1)}, bf16[136,512]{1,0:T(8,128)(2,1)S(1)}, u32[]{:S(2)}, u32[]{:S(2)}) collective-permute-start(bf16[136,512]{1,0:T(8,128)(2,1)S(1)} %maximum_maximum_fusion), channel_id=1, source_target_pairs={{0,8},{4,12},{8,0},{12,4},{16,24},{20,28},{24,16},{28,20},{1,9},{5... | collective-permute-start | bytes 417800 | tf_op jit(solution)/shard_map/ppermute | solution.py:244
  7.0 2.6 %collective-permute-start.2 = (bf16[136,512]{1,0:T(8,128)(2,1)S(1)}, bf16[136,512]{1,0:T(8,128)(2,1)S(1)}, u32[]{:S(2)}, u32[]{:S(2)}) collective-permute-start(bf16[136,512]{1,0:T(8,128)(2,1)S(1)} %maximum_maximum_fusion), channel_id=1, source_target_pairs={{0,16},{4,20},{8,24},{12,28},{16,0},{20,4},{24,8},{28,12},{1,17},{... | collective-permute-start | bytes 417800 | tf_op jit(solution)/shard_map/ppermute | solution.py:244
  12.6 1.1 convolution_convert_fusion.1
  15.7 5.2 %collective-permute-done.4 = bf16[1024,128]{1,0:T(8,128)(2,1)S(1)} collective-permute-done((bf16[1024,128]{1,0:T(8,128)(2,1)S(1)}, bf16[1024,128]{1,0:T(8,128)(2,1)S(1)}, u32[]{:S(2)}, u32[]{:S(2)}) %collective-permute-start.4) | collective-permute-done | bytes 262176 | tf_op jit(solution)/shard_map/ppermute | solution.py:244
  21.1 1.4 %collective-permute-start.6 = (bf16[768,128]{1,0:T(8,128)(2,1)S(1)}, bf16[768,128]{1,0:T(8,128)(2,1)S(1)}, u32[]{:S(2)}, u32[]{:S(2)}) collective-permute-start(bf16[768,128]{1,0:T(8,128)(2,1)S(1)} %constant_dynamic-update-slice_fusion.4), channel_id=1, source_target_pairs={{0,8},{4,12},{8,0},{12,4},{16,24},{20,28},{24,16},{28,20},{1,9},{5... | collective-permute-start | bytes 589832 | tf_op jit(solution)/shard_map/ppermute | solution.py:244
  22.6 1.6 %collective-permute-start.9 = (bf16[4,136,512]{2,1,0:T(8,128)(2,1)S(1)}, bf16[4,136,512]{2,1,0:T(8,128)(2,1)S(1)}, u32[]{:S(2)}, u32[]{:S(2)}) collective-permute-start(bf16[4,136,512]{2,1,0:T(8,128)(2,1)S(1)} %pad_maximum_fusion.refs_1_), channel_id=1, source_target_pairs={{0,2},{1,3},{2,0},{3,1},{4,6},{5,7},{6,4},{7,5},{8,10},{9,11},{10,... | collective-permute-start | bytes 1671176 | tf_op jit(solution)/shard_map/ppermute | solution.py:244
  24.2 2.6 %collective-permute-done.6 = bf16[768,128]{1,0:T(8,128)(2,1)S(1)} collective-permute-done((bf16[768,128]{1,0:T(8,128)(2,1)S(1)}, bf16[768,128]{1,0:T(8,128)(2,1)S(1)}, u32[]{:S(2)}, u32[]{:S(2)}) %collective-permute-start.6) | collective-permute-done | bytes 196640 | tf_op jit(solution)/shard_map/ppermute | solution.py:244
  27.0 2.4 %collective-permute-start.7 = (bf16[384,128]{1,0:T(8,128)(2,1)S(1)}, bf16[384,128]{1,0:T(8,128)(2,1)S(1)}, u32[]{:S(2)}, u32[]{:S(2)}) collective-permute-start(bf16[384,128]{1,0:T(8,128)(2,1)S(1)} %select_dynamic-update-slice_fusion), channel_id=1, source_target_pairs={{0,16},{4,20},{8,24},{12,28},{16,0},{20,4},{24,8},{28,12},{1,17},{... | collective-permute-start | bytes 294920 | tf_op jit(solution)/shard_map/ppermute | solution.py:244
  30.0 3.6 %collective-permute-done.7 = bf16[384,128]{1,0:T(8,128)(2,1)S(1)} collective-permute-done((bf16[384,128]{1,0:T(8,128)(2,1)S(1)}, bf16[384,128]{1,0:T(8,128)(2,1)S(1)}, u32[]{:S(2)}, u32[]{:S(2)}) %collective-permute-start.7) | collective-permute-done | bytes 98336 | tf_op jit(solution)/shard_map/ppermute | solution.py:244
  33.8 1.2 collective-permute-done.8
  34.9 3.4 %collective-permute-done.5.refs_3_.refs_2_ = bf16[3,136,512]{2,1,0:T(8,128)(2,1)S(1)} collective-permute-done((bf16[3,136,512]{2,1,0:T(8,128)(2,1)S(1)}, bf16[3,136,512]{2,1,0:T(8,128)(2,1)S(1)}, u32[]{:S(2)}, u32[]{:S(2)}) %collective-permute-start.5) | collective-permute-done | bytes 417824 | tf_op jit(solution)/shard_map/ppermute | solution.py:244
  38.3 1.5 %collective-permute-start.13 = (f32[32,128]{1,0:T(8,128)S(1)}, f32[32,128]{1,0:T(8,128)S(1)}, u32[]{:S(2)}, u32[]{:S(2)}) collective-permute-start(f32[32,128]{1,0:T(8,128)S(1)} %add.155), channel_id=1, source_target_pairs={{0,2},{1,3},{2,0},{3,1},{4,6},{5,7},{6,4},{7,5},{8,10},{9,11},{10,... | collective-permute-start | bytes 49160 | tf_op jit(solution)/shard_map/ppermute | solution.py:244
  42.5 4.2 %collective-permute-done.14 = bf16[1,32,128]{2,1,0:T(8,128)(2,1)S(1)} collective-permute-done((bf16[1,32,128]{2,1,0:T(8,128)(2,1)S(1)}, bf16[1,32,128]{2,1,0:T(8,128)(2,1)S(1)}, u32[]{:S(2)}, u32[]{:S(2)}) %collective-permute-start.14) | collective-permute-done | bytes 8224 | tf_op jit(solution)/shard_map/ppermute | solution.py:244
  47.6 1.6 %shard_map.118 = (bf16[8,512,128]{2,1,0:T(8,128)(2,1)S(1)}, bf16[8,128,512]{2,1,0:T(8,128)(2,1)S(1)}, f32[16,256,128]{2,1,0:T(8,128)S(1)}) custom-call(s32[9]{0:T(128)S(1)} %pad_add_fusion.1.scalar_ref, bf16[1,136,512]{2,1,0:T(8,128)(2,1)S(1)} %fusion.41.refs_0_, bf16[3,136,512]{2,1,0:T(8,128)(2,1)S(1)} %pad_maximum_fusion.1.refs_1_, ...), custom_call_target="tpu_custom_call" | custom-call | flops 1000000 | bytes 1000 | tf_op jit(solution)/shard_map/pallas_call | solution.py:76
  49.2 1.2 collective-permute-done.15
  50.4 7.7 %shard_map.119.refs_9_ = f32[16,256,256]{2,1,0:T(8,128)S(1)} custom-call(s32[9]{0:T(128)S(1)} %pad_add_fusion.scalar_ref, bf16[128,2048]{1,0:T(8,128)(2,1)S(1)} %copy-done.2, bf16[4,136,512]{2,1,0:T(8,128)(2,1)S(1)} %pad_maximum_fusion.refs_1_, bf16[3,136,512]{2,1,0:T(8,128)(2,1)S(1)} %collective-permute-done.5.refs_3_.refs_2_, ...), custom_call_target="tpu_custom_call" | custom-call | flops 1000000 | bytes 1000 | tf_op jit(solution)/shard_map/pallas_call | solution.py:187
  58.1 1.9 %copy-done.1 = f32[16,256,256]{2,1,0:T(8,128)} copy-done((f32[16,256,256]{2,1,0:T(8,128)}, f32[16,256,256]{2,1,0:T(8,128)S(1)}, u32[]{:S(2)}) %copy-start.1) | copy-done | bytes 4194328
  60.7 3.3 %collective-permute-done.18 = bf16[4,32,128]{2,1,0:T(8,128)(2,1)S(1)} collective-permute-done((bf16[4,32,128]{2,1,0:T(8,128)(2,1)S(1)}, bf16[4,32,128]{2,1,0:T(8,128)(2,1)S(1)}, u32[]{:S(2)}, u32[]{:S(2)}) %collective-permute-start.18) | collective-permute-done | bytes 32800 | tf_op jit(solution)/shard_map/ppermute | solution.py:244
  64.0 10.7 %shard_map.120.hidden_ref = bf16[16,256,128]{2,1,0:T(8,128)(2,1)S(1)} custom-call(s32[9]{0:T(128)S(1)} %pad_add_fusion.scalar_ref, bf16[128,2048]{1,0:T(8,128)(2,1)S(1)} %copy-done.2, bf16[4,136,512]{2,1,0:T(8,128)(2,1)S(1)} %collective-permute-done.9.refs_1_, bf16[3,136,512]{2,1,0:T(8,128)(2,1)S(1)} %collective-permute-done.12.refs_2_, ...), custom_call_target="tpu_custom_call" | custom-call | flops 1000000 | bytes 1000 | tf_op jit(solution)/shard_map/pallas_call | solution.py:187
  74.8 6.3 %shard_map.121 = (bf16[8,128,256]{2,1,0:T(8,128)(2,1)S(1)}, f32[8,128,256]{2,1,0:T(8,128)S(1)}, bf16[8,128,256]{2,1,0:T(8,128)(2,1)S(1)}, f32[8,128,256]{2,1,0:T(8,128)S(1)}) custom-call(s32[9]{0:T(128)S(1)} %pad_add_fusion.scalar_ref, bf16[16,2048,128]{2,1,0:T(8,128)(2,1)} %down_hbm.3, bf16[16,256,128]{2,1,0:T(8,128)(2,1)S(1)} %shard_map.120.hidden_ref, ...), custom_call_target="tpu_custom_call" | custom-call | flops 1000000 | bytes 1000 | tf_op jit(solution)/shard_map/pallas_call | solution.py:227
  81.7 1.4 %collective-permute-done.20 = bf16[8,128,256]{2,1,0:T(8,128)(2,1)S(1)} collective-permute-done((bf16[8,128,256]{2,1,0:T(8,128)(2,1)S(1)}, bf16[8,128,256]{2,1,0:T(8,128)(2,1)S(1)}, u32[]{:S(2)}, u32[]{:S(2)}) %collective-permute-start.20) | collective-permute-done | bytes 524320 | tf_op jit(solution)/shard_map/ppermute | solution.py:244
  84.0 1.6 %collective-permute-start.21 = (bf16[4,128,256]{2,1,0:T(8,128)(2,1)S(1)}, bf16[4,128,256]{2,1,0:T(8,128)(2,1)S(1)}, u32[]{:S(2)}, u32[]{:S(2)}) collective-permute-start(bf16[4,128,256]{2,1,0:T(8,128)(2,1)S(1)} %get-tuple-element.78), channel_id=1, source_target_pairs={{0,2},{1,3},{2,0},{3,1},{4,6},{5,7},{6,4},{7,5},{8,10},{9,11},{10,... | collective-permute-start | bytes 786440 | tf_op jit(solution)/shard_map/ppermute | solution.py:244
  86.2 6.3 %shard_map.122 = (bf16[8,128,256]{2,1,0:T(8,128)(2,1)S(1)}, f32[8,128,256]{2,1,0:T(8,128)S(1)}, bf16[8,128,256]{2,1,0:T(8,128)(2,1)S(1)}, f32[8,128,256]{2,1,0:T(8,128)S(1)}) custom-call(s32[9]{0:T(128)S(1)} %pad_add_fusion.scalar_ref, bf16[16,2048,128]{2,1,0:T(8,128)(2,1)} %down_hbm.3, bf16[16,256,128]{2,1,0:T(8,128)(2,1)S(1)} %shard_map.120.hidden_ref, ...), custom_call_target="tpu_custom_call" | custom-call | flops 1000000 | bytes 1000 | tf_op jit(solution)/shard_map/pallas_call | solution.py:227
  92.5 1.2 %collective-permute-done.22 = bf16[4,128,256]{2,1,0:T(8,128)(2,1)S(1)} collective-permute-done((bf16[4,128,256]{2,1,0:T(8,128)(2,1)S(1)}, bf16[4,128,256]{2,1,0:T(8,128)(2,1)S(1)}, u32[]{:S(2)}, u32[]{:S(2)}) %collective-permute-start.22) | collective-permute-done | bytes 262176 | tf_op jit(solution)/shard_map/ppermute | solution.py:244
  94.6 1.6 %collective-permute-start.31 = (bf16[4,128,256]{2,1,0:T(8,128)(2,1)S(1)}, bf16[4,128,256]{2,1,0:T(8,128)(2,1)S(1)}, u32[]{:S(2)}, u32[]{:S(2)}) collective-permute-start(bf16[4,128,256]{2,1,0:T(8,128)(2,1)S(1)} %add_convert_fusion.1), channel_id=1, source_target_pairs={{0,2},{1,3},{2,0},{3,1},{4,6},{5,7},{6,4},{7,5},{8,10},{9,11},{10,... | collective-permute-start | bytes 786440 | tf_op jit(solution)/shard_map/ppermute | solution.py:244
  97.1 1.6 %collective-permute-start.30 = (bf16[4,128,256]{2,1,0:T(8,128)(2,1)S(1)}, bf16[4,128,256]{2,1,0:T(8,128)(2,1)S(1)}, u32[]{:S(2)}, u32[]{:S(2)}) collective-permute-start(bf16[4,128,256]{2,1,0:T(8,128)(2,1)S(1)} %slice.386), channel_id=1, source_target_pairs={{0,4},{4,0},{8,12},{12,8},{16,20},{20,16},{24,28},{28,24},{1,5},{5... | collective-permute-start | bytes 786440 | tf_op jit(solution)/shard_map/ppermute | solution.py:244
  98.7 4.2 %collective-permute-done.24 = bf16[4,128,256]{2,1,0:T(8,128)(2,1)S(1)} collective-permute-done((bf16[4,128,256]{2,1,0:T(8,128)(2,1)S(1)}, bf16[4,128,256]{2,1,0:T(8,128)(2,1)S(1)}, u32[]{:S(2)}, u32[]{:S(2)}) %collective-permute-start.24) | collective-permute-done | bytes 262176 | tf_op jit(solution)/shard_map/ppermute | solution.py:244
  102.8 2.7 %collective-permute-done.25 = bf16[4,128,256]{2,1,0:T(8,128)(2,1)S(1)} collective-permute-done((bf16[4,128,256]{2,1,0:T(8,128)(2,1)S(1)}, bf16[4,128,256]{2,1,0:T(8,128)(2,1)S(1)}, u32[]{:S(2)}, u32[]{:S(2)}) %collective-permute-start.25) | collective-permute-done | bytes 262176 | tf_op jit(solution)/shard_map/ppermute | solution.py:244
  107.5 2.6 %collective-permute-start.28 = (bf16[128,256]{1,0:T(8,128)(2,1)S(1)}, bf16[128,256]{1,0:T(8,128)(2,1)S(1)}, u32[]{:S(2)}, u32[]{:S(2)}) collective-permute-start(bf16[128,256]{1,0:T(8,128)(2,1)S(1)} %get-tuple-element.82), channel_id=1, source_target_pairs={{0,24},{4,28},{8,16},{12,20},{16,8},{20,12},{24,0},{28,4},{1,25},{... | collective-permute-start | bytes 196616 | tf_op jit(solution)/shard_map/ppermute | solution.py:244
  112.2 2.6 %collective-permute-start.34 = (bf16[128,256]{1,0:T(8,128)(2,1)S(1)}, bf16[128,256]{1,0:T(8,128)(2,1)S(1)}, u32[]{:S(2)}, u32[]{:S(2)}) collective-permute-start(bf16[128,256]{1,0:T(8,128)(2,1)S(1)} %get-tuple-element.85), channel_id=1, source_target_pairs={{0,24},{4,28},{8,16},{12,20},{16,8},{20,12},{24,0},{28,4},{1,25},{... | collective-permute-start | bytes 196616 | tf_op jit(solution)/shard_map/ppermute | solution.py:244
  115.2 3.6 %collective-permute-done.33 = bf16[128,256]{1,0:T(8,128)(2,1)S(1)} collective-permute-done((bf16[128,256]{1,0:T(8,128)(2,1)S(1)}, bf16[128,256]{1,0:T(8,128)(2,1)S(1)}, u32[]{:S(2)}, u32[]{:S(2)}) %collective-permute-start.33) | collective-permute-done | bytes 65568 | tf_op jit(solution)/shard_map/ppermute | solution.py:244
  (127 shorter events, 21.6 us)
Async XLA Ops:
  2.4 18.6 %collective-permute-start = (bf16[136,512]{1,0:T(8,128)(2,1)S(1)}, bf16[136,512]{1,0:T(8,128)(2,1)S(1)}, u32[]{:S(2)}, u32[]{:S(2)}) collective-permute-start(bf16[136,512]{1,0:T(8,128)(2,1)S(1)} %maximum_maximum_fusion), channel_id=1, source_target_pairs={{0,4},{4,0},{8,12},{12,8},{16,20},{20,16},{24,28},{28,24},{1,5},{5... | collective-permute-start | bytes 417800 | tf_op jit(solution)/shard_map/ppermute | solution.py:244
  5.4 15.5 %collective-permute-start.1 = (bf16[136,512]{1,0:T(8,128)(2,1)S(1)}, bf16[136,512]{1,0:T(8,128)(2,1)S(1)}, u32[]{:S(2)}, u32[]{:S(2)}) collective-permute-start(bf16[136,512]{1,0:T(8,128)(2,1)S(1)} %maximum_maximum_fusion), channel_id=1, source_target_pairs={{0,8},{4,12},{8,0},{12,4},{16,24},{20,28},{24,16},{28,20},{1,9},{5... | collective-permute-start | bytes 417800 | tf_op jit(solution)/shard_map/ppermute | solution.py:244
  7.0 14.0 %collective-permute-start.2 = (bf16[136,512]{1,0:T(8,128)(2,1)S(1)}, bf16[136,512]{1,0:T(8,128)(2,1)S(1)}, u32[]{:S(2)}, u32[]{:S(2)}) collective-permute-start(bf16[136,512]{1,0:T(8,128)(2,1)S(1)} %maximum_maximum_fusion), channel_id=1, source_target_pairs={{0,16},{4,20},{8,24},{12,28},{16,0},{20,4},{24,8},{28,12},{1,17},{... | collective-permute-start | bytes 417800 | tf_op jit(solution)/shard_map/ppermute | solution.py:244
  9.6 11.4 %collective-permute-start.3 = (bf16[136,512]{1,0:T(8,128)(2,1)S(1)}, bf16[136,512]{1,0:T(8,128)(2,1)S(1)}, u32[]{:S(2)}, u32[]{:S(2)}) collective-permute-start(bf16[136,512]{1,0:T(8,128)(2,1)S(1)} %maximum_maximum_fusion), channel_id=1, source_target_pairs={{0,24},{4,28},{8,16},{12,20},{16,8},{20,12},{24,0},{28,4},{1,25},{... | collective-permute-start | bytes 417800 | tf_op jit(solution)/shard_map/ppermute | solution.py:244
  13.8 7.1 %collective-permute-start.4 = (bf16[1024,128]{1,0:T(8,128)(2,1)S(1)}, bf16[1024,128]{1,0:T(8,128)(2,1)S(1)}, u32[]{:S(2)}, u32[]{:S(2)}) collective-permute-start(bf16[1024,128]{1,0:T(8,128)(2,1)S(1)} %slice_dynamic-update-slice_fusion), channel_id=1, source_target_pairs={{0,4},{4,0},{8,12},{12,8},{16,20},{20,16},{24,28},{28,24},{1,5},{5... | collective-permute-start | bytes 786440 | tf_op jit(solution)/shard_map/ppermute | solution.py:244
  21.1 5.7 %collective-permute-start.6 = (bf16[768,128]{1,0:T(8,128)(2,1)S(1)}, bf16[768,128]{1,0:T(8,128)(2,1)S(1)}, u32[]{:S(2)}, u32[]{:S(2)}) collective-permute-start(bf16[768,128]{1,0:T(8,128)(2,1)S(1)} %constant_dynamic-update-slice_fusion.4), channel_id=1, source_target_pairs={{0,8},{4,12},{8,0},{12,4},{16,24},{20,28},{24,16},{28,20},{1,9},{5... | collective-permute-start | bytes 589832 | tf_op jit(solution)/shard_map/ppermute | solution.py:244
  22.6 15.7 %collective-permute-start.9 = (bf16[4,136,512]{2,1,0:T(8,128)(2,1)S(1)}, bf16[4,136,512]{2,1,0:T(8,128)(2,1)S(1)}, u32[]{:S(2)}, u32[]{:S(2)}) collective-permute-start(bf16[4,136,512]{2,1,0:T(8,128)(2,1)S(1)} %pad_maximum_fusion.refs_1_), channel_id=1, source_target_pairs={{0,2},{1,3},{2,0},{3,1},{4,6},{5,7},{6,4},{7,5},{8,10},{9,11},{10,... | collective-permute-start | bytes 1671176 | tf_op jit(solution)/shard_map/ppermute | solution.py:244
  27.0 6.6 %collective-permute-start.7 = (bf16[384,128]{1,0:T(8,128)(2,1)S(1)}, bf16[384,128]{1,0:T(8,128)(2,1)S(1)}, u32[]{:S(2)}, u32[]{:S(2)}) collective-permute-start(bf16[384,128]{1,0:T(8,128)(2,1)S(1)} %select_dynamic-update-slice_fusion), channel_id=1, source_target_pairs={{0,16},{4,20},{8,24},{12,28},{16,0},{20,4},{24,8},{28,12},{1,17},{... | collective-permute-start | bytes 294920 | tf_op jit(solution)/shard_map/ppermute | solution.py:244
  29.4 8.9 %collective-permute-start.5 = (bf16[3,136,512]{2,1,0:T(8,128)(2,1)S(1)}, bf16[3,136,512]{2,1,0:T(8,128)(2,1)S(1)}, u32[]{:S(2)}, u32[]{:S(2)}) collective-permute-start(bf16[3,136,512]{2,1,0:T(8,128)(2,1)S(1)} %pad_maximum_fusion.1.refs_1_), channel_id=1, source_target_pairs={{0,4},{4,0},{8,12},{12,8},{16,20},{20,16},{24,28},{28,24},{1,5},{5... | collective-permute-start | bytes 1253384 | tf_op jit(solution)/shard_map/ppermute | solution.py:244
  38.3 3.7 %collective-permute-start.13 = (f32[32,128]{1,0:T(8,128)S(1)}, f32[32,128]{1,0:T(8,128)S(1)}, u32[]{:S(2)}, u32[]{:S(2)}) collective-permute-start(f32[32,128]{1,0:T(8,128)S(1)} %add.155), channel_id=1, source_target_pairs={{0,2},{1,3},{2,0},{3,1},{4,6},{5,7},{6,4},{7,5},{8,10},{9,11},{10,... | collective-permute-start | bytes 49160 | tf_op jit(solution)/shard_map/ppermute | solution.py:244
  39.9 10.5 %collective-permute-start.10 = (bf16[4,136,512]{2,1,0:T(8,128)(2,1)S(1)}, bf16[4,136,512]{2,1,0:T(8,128)(2,1)S(1)}, u32[]{:S(2)}, u32[]{:S(2)}) collective-permute-start(bf16[4,136,512]{2,1,0:T(8,128)(2,1)S(1)} %pad_maximum_fusion.refs_1_), channel_id=1, source_target_pairs={{0,1},{1,0},{2,3},{3,2},{4,5},{5,4},{6,7},{7,6},{8,9},{9,8},{10,11... | collective-permute-start | bytes 1671176 | tf_op jit(solution)/shard_map/ppermute | solution.py:244
  39.9 10.5 %collective-permute-start.11 = (bf16[3,136,512]{2,1,0:T(8,128)(2,1)S(1)}, bf16[3,136,512]{2,1,0:T(8,128)(2,1)S(1)}, u32[]{:S(2)}, u32[]{:S(2)}) collective-permute-start(bf16[3,136,512]{2,1,0:T(8,128)(2,1)S(1)} %collective-permute-done.5.refs_3_.refs_2_), channel_id=1, source_target_pairs={{0,1},{1,0},{2,3},{3,2},{4,5},{5,4},{6,7},{7,6},{8,9},{9,8},{10,11... | collective-permute-start | bytes 1253384 | tf_op jit(solution)/shard_map/ppermute | solution.py:244
  40.4 19.7 %collective-permute-start.12 = (bf16[3,136,512]{2,1,0:T(8,128)(2,1)S(1)}, bf16[3,136,512]{2,1,0:T(8,128)(2,1)S(1)}, u32[]{:S(2)}, u32[]{:S(2)}) collective-permute-start(bf16[3,136,512]{2,1,0:T(8,128)(2,1)S(1)} %collective-permute-done.5.refs_3_.refs_2_), channel_id=1, source_target_pairs={{0,2},{1,3},{2,0},{3,1},{4,6},{5,7},{6,4},{7,5},{8,10},{9,11},{10,... | collective-permute-start | bytes 1253384 | tf_op jit(solution)/shard_map/ppermute | solution.py:244
  40.9 23.1 %collective-permute-start.16 = (bf16[4,136,512]{2,1,0:T(8,128)(2,1)S(1)}, bf16[4,136,512]{2,1,0:T(8,128)(2,1)S(1)}, u32[]{:S(2)}, u32[]{:S(2)}) collective-permute-start(bf16[4,136,512]{2,1,0:T(8,128)(2,1)S(1)} %collective-permute-done.9.refs_1_), channel_id=1, source_target_pairs={{0,1},{1,0},{2,3},{3,2},{4,5},{5,4},{6,7},{7,6},{8,9},{9,8},{10,11... | collective-permute-start | bytes 1671176 | tf_op jit(solution)/shard_map/ppermute | solution.py:244
  42.1 4.5 %collective-permute-start.14 = (bf16[1,32,128]{2,1,0:T(8,128)(2,1)S(1)}, bf16[1,32,128]{2,1,0:T(8,128)(2,1)S(1)}, u32[]{:S(2)}, u32[]{:S(2)}) collective-permute-start(bf16[1,32,128]{2,1,0:T(8,128)(2,1)S(1)} %fusion.27), channel_id=1, source_target_pairs={{0,16},{4,20},{8,24},{12,28},{16,0},{20,4},{24,8},{28,12},{1,17},{... | collective-permute-start | bytes 24584 | tf_op jit(solution)/shard_map/ppermute | solution.py:244
  46.6 3.7 %collective-permute-start.15 = (bf16[2,32,128]{2,1,0:T(8,128)(2,1)S(1)}, bf16[2,32,128]{2,1,0:T(8,128)(2,1)S(1)}, u32[]{:S(2)}, u32[]{:S(2)}) collective-permute-start(bf16[2,32,128]{2,1,0:T(8,128)(2,1)S(1)} %pad_maximum_fusion.5), channel_id=1, source_target_pairs={{0,8},{4,12},{8,0},{12,4},{16,24},{20,28},{24,16},{28,20},{1,9},{5... | collective-permute-start | bytes 49160 | tf_op jit(solution)/shard_map/ppermute | solution.py:244
  60.1 3.9 %collective-permute-start.18 = (bf16[4,32,128]{2,1,0:T(8,128)(2,1)S(1)}, bf16[4,32,128]{2,1,0:T(8,128)(2,1)S(1)}, u32[]{:S(2)}, u32[]{:S(2)}) collective-permute-start(bf16[4,32,128]{2,1,0:T(8,128)(2,1)S(1)} %pad_maximum_fusion.4), channel_id=1, source_target_pairs={{0,4},{4,0},{8,12},{12,8},{16,20},{20,16},{24,28},{28,24},{1,5},{5... | collective-permute-start | bytes 98312 | tf_op jit(solution)/shard_map/ppermute | solution.py:244
  60.6 3.4 %collective-permute-start.17 = (bf16[3,136,512]{2,1,0:T(8,128)(2,1)S(1)}, bf16[3,136,512]{2,1,0:T(8,128)(2,1)S(1)}, u32[]{:S(2)}, u32[]{:S(2)}) collective-permute-start(bf16[3,136,512]{2,1,0:T(8,128)(2,1)S(1)} %collective-permute-done.12.refs_2_), channel_id=1, source_target_pairs={{0,1},{1,0},{2,3},{3,2},{4,5},{5,4},{6,7},{7,6},{8,9},{9,8},{10,11... | collective-permute-start | bytes 1253384 | tf_op jit(solution)/shard_map/ppermute | solution.py:244
  81.2 2.6 %collective-permute-start.19 = (bf16[8,128,256]{2,1,0:T(8,128)(2,1)S(1)}, bf16[8,128,256]{2,1,0:T(8,128)(2,1)S(1)}, u32[]{:S(2)}, u32[]{:S(2)}) collective-permute-start(bf16[8,128,256]{2,1,0:T(8,128)(2,1)S(1)} %get-tuple-element.57), channel_id=1, source_target_pairs={{0,1},{1,0},{2,3},{3,2},{4,5},{5,4},{6,7},{7,6},{8,9},{9,8},{10,11... | collective-permute-start | bytes 1572872 | tf_op jit(solution)/shard_map/ppermute | solution.py:244
  84.0 8.5 %collective-permute-start.21 = (bf16[4,128,256]{2,1,0:T(8,128)(2,1)S(1)}, bf16[4,128,256]{2,1,0:T(8,128)(2,1)S(1)}, u32[]{:S(2)}, u32[]{:S(2)}) collective-permute-start(bf16[4,128,256]{2,1,0:T(8,128)(2,1)S(1)} %get-tuple-element.78), channel_id=1, source_target_pairs={{0,2},{1,3},{2,0},{3,1},{4,6},{5,7},{6,4},{7,5},{8,10},{9,11},{10,... | collective-permute-start | bytes 786440 | tf_op jit(solution)/shard_map/ppermute | solution.py:244
  85.6 8.1 %collective-permute-start.22 = (bf16[4,128,256]{2,1,0:T(8,128)(2,1)S(1)}, bf16[4,128,256]{2,1,0:T(8,128)(2,1)S(1)}, u32[]{:S(2)}, u32[]{:S(2)}) collective-permute-start(bf16[4,128,256]{2,1,0:T(8,128)(2,1)S(1)} %slice.387), channel_id=1, source_target_pairs={{0,4},{4,0},{8,12},{12,8},{16,20},{20,16},{24,28},{28,24},{1,5},{5... | collective-permute-start | bytes 786440 | tf_op jit(solution)/shard_map/ppermute | solution.py:244
  93.7 9.1 %collective-permute-start.24 = (bf16[4,128,256]{2,1,0:T(8,128)(2,1)S(1)}, bf16[4,128,256]{2,1,0:T(8,128)(2,1)S(1)}, u32[]{:S(2)}, u32[]{:S(2)}) collective-permute-start(bf16[4,128,256]{2,1,0:T(8,128)(2,1)S(1)} %get-tuple-element.77), channel_id=1, source_target_pairs={{0,2},{1,3},{2,0},{3,1},{4,6},{5,7},{6,4},{7,5},{8,10},{9,11},{10,... | collective-permute-start | bytes 786440 | tf_op jit(solution)/shard_map/ppermute | solution.py:244
  94.3 2.6 %collective-permute-start.29 = (bf16[8,128,256]{2,1,0:T(8,128)(2,1)S(1)}, bf16[8,128,256]{2,1,0:T(8,128)(2,1)S(1)}, u32[]{:S(2)}, u32[]{:S(2)}) collective-permute-start(bf16[8,128,256]{2,1,0:T(8,128)(2,1)S(1)} %get-tuple-element.71), channel_id=1, source_target_pairs={{0,1},{1,0},{2,3},{3,2},{4,5},{5,4},{6,7},{7,6},{8,9},{9,8},{10,11... | collective-permute-start | bytes 1572872 | tf_op jit(solution)/shard_map/ppermute | solution.py:244
  94.6 15.6 %collective-permute-start.31 = (bf16[4,128,256]{2,1,0:T(8,128)(2,1)S(1)}, bf16[4,128,256]{2,1,0:T(8,128)(2,1)S(1)}, u32[]{:S(2)}, u32[]{:S(2)}) collective-permute-start(bf16[4,128,256]{2,1,0:T(8,128)(2,1)S(1)} %add_convert_fusion.1), channel_id=1, source_target_pairs={{0,2},{1,3},{2,0},{3,1},{4,6},{5,7},{6,4},{7,5},{8,10},{9,11},{10,... | collective-permute-start | bytes 786440 | tf_op jit(solution)/shard_map/ppermute | solution.py:244
  96.3 9.2 %collective-permute-start.25 = (bf16[4,128,256]{2,1,0:T(8,128)(2,1)S(1)}, bf16[4,128,256]{2,1,0:T(8,128)(2,1)S(1)}, u32[]{:S(2)}, u32[]{:S(2)}) collective-permute-start(bf16[4,128,256]{2,1,0:T(8,128)(2,1)S(1)} %fusion.1), channel_id=1, source_target_pairs={{0,4},{4,0},{8,12},{12,8},{16,20},{20,16},{24,28},{28,24},{1,5},{5... | collective-permute-start | bytes 786440 | tf_op jit(solution)/shard_map/ppermute | solution.py:244
  97.1 13.2 %collective-permute-start.30 = (bf16[4,128,256]{2,1,0:T(8,128)(2,1)S(1)}, bf16[4,128,256]{2,1,0:T(8,128)(2,1)S(1)}, u32[]{:S(2)}, u32[]{:S(2)}) collective-permute-start(bf16[4,128,256]{2,1,0:T(8,128)(2,1)S(1)} %slice.386), channel_id=1, source_target_pairs={{0,4},{4,0},{8,12},{12,8},{16,20},{20,16},{24,28},{28,24},{1,5},{5... | collective-permute-start | bytes 786440 | tf_op jit(solution)/shard_map/ppermute | solution.py:244
  105.7 6.5 %collective-permute-start.26 = (bf16[128,256]{1,0:T(8,128)(2,1)S(1)}, bf16[128,256]{1,0:T(8,128)(2,1)S(1)}, u32[]{:S(2)}, u32[]{:S(2)}) collective-permute-start(bf16[128,256]{1,0:T(8,128)(2,1)S(1)} %get-tuple-element.81), channel_id=1, source_target_pairs={{0,8},{4,12},{8,0},{12,4},{16,24},{20,28},{24,16},{28,20},{1,9},{5... | collective-permute-start | bytes 196616 | tf_op jit(solution)/shard_map/ppermute | solution.py:244
  106.7 8.1 %collective-permute-start.27 = (bf16[128,256]{1,0:T(8,128)(2,1)S(1)}, bf16[128,256]{1,0:T(8,128)(2,1)S(1)}, u32[]{:S(2)}, u32[]{:S(2)}) collective-permute-start(bf16[128,256]{1,0:T(8,128)(2,1)S(1)} %get-tuple-element.83), channel_id=1, source_target_pairs={{0,16},{4,20},{8,24},{12,28},{16,0},{20,4},{24,8},{28,12},{1,17},{... | collective-permute-start | bytes 196616 | tf_op jit(solution)/shard_map/ppermute | solution.py:244
  107.5 7.3 %collective-permute-start.28 = (bf16[128,256]{1,0:T(8,128)(2,1)S(1)}, bf16[128,256]{1,0:T(8,128)(2,1)S(1)}, u32[]{:S(2)}, u32[]{:S(2)}) collective-permute-start(bf16[128,256]{1,0:T(8,128)(2,1)S(1)} %get-tuple-element.82), channel_id=1, source_target_pairs={{0,24},{4,28},{8,16},{12,20},{16,8},{20,12},{24,0},{28,4},{1,25},{... | collective-permute-start | bytes 196616 | tf_op jit(solution)/shard_map/ppermute | solution.py:244
  110.4 4.9 %collective-permute-start.32 = (bf16[128,256]{1,0:T(8,128)(2,1)S(1)}, bf16[128,256]{1,0:T(8,128)(2,1)S(1)}, u32[]{:S(2)}, u32[]{:S(2)}) collective-permute-start(bf16[128,256]{1,0:T(8,128)(2,1)S(1)} %get-tuple-element.84), channel_id=1, source_target_pairs={{0,8},{4,12},{8,0},{12,4},{16,24},{20,28},{24,16},{28,20},{1,9},{5... | collective-permute-start | bytes 196616 | tf_op jit(solution)/shard_map/ppermute | solution.py:244
  111.4 7.5 %collective-permute-start.33 = (bf16[128,256]{1,0:T(8,128)(2,1)S(1)}, bf16[128,256]{1,0:T(8,128)(2,1)S(1)}, u32[]{:S(2)}, u32[]{:S(2)}) collective-permute-start(bf16[128,256]{1,0:T(8,128)(2,1)S(1)} %get-tuple-element.86), channel_id=1, source_target_pairs={{0,16},{4,20},{8,24},{12,28},{16,0},{20,4},{24,8},{28,12},{1,17},{... | collective-permute-start | bytes 196616 | tf_op jit(solution)/shard_map/ppermute | solution.py:244
  112.2 6.7 %collective-permute-start.34 = (bf16[128,256]{1,0:T(8,128)(2,1)S(1)}, bf16[128,256]{1,0:T(8,128)(2,1)S(1)}, u32[]{:S(2)}, u32[]{:S(2)}) collective-permute-start(bf16[128,256]{1,0:T(8,128)(2,1)S(1)} %get-tuple-element.85), channel_id=1, source_target_pairs={{0,24},{4,28},{8,16},{12,20},{16,8},{20,12},{24,0},{28,4},{1,25},{... | collective-permute-start | bytes 196616 | tf_op jit(solution)/shard_map/ppermute | solution.py:244
  (6 other events, 70.1 us)

commit v4 on v3

--- a/solution.py
+++ b/solution.py
@@ -15,7 +15,7 @@
 BF16 = jnp.bfloat16
 F32 = jnp.float32
 VMEM_BYTES = 12 * 1024 * 1024
-EXPAND_BYTES = 46 * 1024 * 1024
+EXPAND_BYTES = 42 * 1024 * 1024
 UNROLL = 16
 COST = pl.CostEstimate(flops=1_000_000, bytes_accessed=1_000, transcendentals=0)
 ORDER = (0, 2, 4, 6, 1, 3, 5, 7)

time: 120 us -> 116 us (0.967)
  local copies, waits for them, and re-layouts: 3.4 us -> 1.45 us
  Pallas kernels: 32.7 us -> 31.1 us
    unnamed x27 -> x25, local copies, waits for them, and re-layouts: 2.15 us -> 0.2 us
    pallas_call x2, Pallas kernels: 18.4 us -> 16.9 us  [expand(): pl.pallas_call(functools.partial(expand_kernel, units, quarters, first, l...]
where the time goes in v4:
time: 116 us
  waiting for transfers between devices  40 us (34%)
  starting transfers between devices  34.2 us (29%)
  Pallas kernels  31.1 us (27%)
  other arithmetic  7.42 us (6%)
  matrix products  1.54 us (1%)
  local copies, waits for them, and re-layouts  1.45 us (1%)
    ppermute x35, waiting for transfers between devices, xor_move(): return lax.ppermute(value, axis, [(i, i ^ bits) for i in range(size)])  40 us
    ppermute x35, starting transfers between devices, xor_move(): return lax.ppermute(value, axis, [(i, i ^ bits) for i in range(size)])  34.2 us
    pallas_call x2, Pallas kernels, expand(): pl.pallas_call(functools.partial(expand_kernel, units, quarters, first, l...  16.9 us
    pallas_call x2, Pallas kernels, contract(): pl.pallas_call(functools.partial(contract_kernel, units, jobs, parts), in...  12.7 us
  transfers between devices with their start and end apart: 35, of which 17 were waited for; matrix products, arithmetic and copies ran while one was open for 6% of the time, Pallas kernels for 13%

profile of v4, /device:TPU:0, one launch (start us, length us, event | category | flops | bytes accessed | tf_op | source)
XLA Modules:
  0.0 116.2 jit_solution(11063066040117299444)
XLA Ops:
  2.4 3.0 %collective-permute-start = (bf16[136,512]{1,0:T(8,128)(2,1)S(1)}, bf16[136,512]{1,0:T(8,128)(2,1)S(1)}, u32[]{:S(2)}, u32[]{:S(2)}) collective-permute-start(bf16[136,512]{1,0:T(8,128)(2,1)S(1)} %maximum_maximum_fusion), channel_id=1, source_target_pairs={{0,4},{4,0},{8,12},{12,8},{16,20},{20,16},{24,28},{28,24},{1,5},{5... | collective-permute-start | bytes 417800 | tf_op jit(solution)/shard_map/ppermute | solution.py:244
  5.4 1.6 %collective-permute-start.1 = (bf16[136,512]{1,0:T(8,128)(2,1)S(1)}, bf16[136,512]{1,0:T(8,128)(2,1)S(1)}, u32[]{:S(2)}, u32[]{:S(2)}) collective-permute-start(bf16[136,512]{1,0:T(8,128)(2,1)S(1)} %maximum_maximum_fusion), channel_id=1, source_target_pairs={{0,8},{4,12},{8,0},{12,4},{16,24},{20,28},{24,16},{28,20},{1,9},{5... | collective-permute-start | bytes 417800 | tf_op jit(solution)/shard_map/ppermute | solution.py:244
  7.0 2.6 %collective-permute-start.2 = (bf16[136,512]{1,0:T(8,128)(2,1)S(1)}, bf16[136,512]{1,0:T(8,128)(2,1)S(1)}, u32[]{:S(2)}, u32[]{:S(2)}) collective-permute-start(bf16[136,512]{1,0:T(8,128)(2,1)S(1)} %maximum_maximum_fusion), channel_id=1, source_target_pairs={{0,16},{4,20},{8,24},{12,28},{16,0},{20,4},{24,8},{28,12},{1,17},{... | collective-permute-start | bytes 417800 | tf_op jit(solution)/shard_map/ppermute | solution.py:244
  12.6 1.1 convolution_convert_fusion.1
  15.7 5.2 %collective-permute-done.4 = bf16[1024,128]{1,0:T(8,128)(2,1)S(1)} collective-permute-done((bf16[1024,128]{1,0:T(8,128)(2,1)S(1)}, bf16[1024,128]{1,0:T(8,128)(2,1)S(1)}, u32[]{:S(2)}, u32[]{:S(2)}) %collective-permute-start.4) | collective-permute-done | bytes 262176 | tf_op jit(solution)/shard_map/ppermute | solution.py:244
  21.1 1.4 %collective-permute-start.6 = (bf16[768,128]{1,0:T(8,128)(2,1)S(1)}, bf16[768,128]{1,0:T(8,128)(2,1)S(1)}, u32[]{:S(2)}, u32[]{:S(2)}) collective-permute-start(bf16[768,128]{1,0:T(8,128)(2,1)S(1)} %constant_dynamic-update-slice_fusion.4), channel_id=1, source_target_pairs={{0,8},{4,12},{8,0},{12,4},{16,24},{20,28},{24,16},{28,20},{1,9},{5... | collective-permute-start | bytes 589832 | tf_op jit(solution)/shard_map/ppermute | solution.py:244
  22.6 1.6 %collective-permute-start.9 = (bf16[4,136,512]{2,1,0:T(8,128)(2,1)S(1)}, bf16[4,136,512]{2,1,0:T(8,128)(2,1)S(1)}, u32[]{:S(2)}, u32[]{:S(2)}) collective-permute-start(bf16[4,136,512]{2,1,0:T(8,128)(2,1)S(1)} %pad_maximum_fusion.refs_1_), channel_id=1, source_target_pairs={{0,2},{1,3},{2,0},{3,1},{4,6},{5,7},{6,4},{7,5},{8,10},{9,11},{10,... | collective-permute-start | bytes 1671176 | tf_op jit(solution)/shard_map/ppermute | solution.py:244
  24.2 2.6 %collective-permute-done.6 = bf16[768,128]{1,0:T(8,128)(2,1)S(1)} collective-permute-done((bf16[768,128]{1,0:T(8,128)(2,1)S(1)}, bf16[768,128]{1,0:T(8,128)(2,1)S(1)}, u32[]{:S(2)}, u32[]{:S(2)}) %collective-permute-start.6) | collective-permute-done | bytes 196640 | tf_op jit(solution)/shard_map/ppermute | solution.py:244
  27.0 2.4 %collective-permute-start.7 = (bf16[384,128]{1,0:T(8,128)(2,1)S(1)}, bf16[384,128]{1,0:T(8,128)(2,1)S(1)}, u32[]{:S(2)}, u32[]{:S(2)}) collective-permute-start(bf16[384,128]{1,0:T(8,128)(2,1)S(1)} %select_dynamic-update-slice_fusion), channel_id=1, source_target_pairs={{0,16},{4,20},{8,24},{12,28},{16,0},{20,4},{24,8},{28,12},{1,17},{... | collective-permute-start | bytes 294920 | tf_op jit(solution)/shard_map/ppermute | solution.py:244
  30.0 3.6 %collective-permute-done.7 = bf16[384,128]{1,0:T(8,128)(2,1)S(1)} collective-permute-done((bf16[384,128]{1,0:T(8,128)(2,1)S(1)}, bf16[384,128]{1,0:T(8,128)(2,1)S(1)}, u32[]{:S(2)}, u32[]{:S(2)}) %collective-permute-start.7) | collective-permute-done | bytes 98336 | tf_op jit(solution)/shard_map/ppermute | solution.py:244
  33.8 1.2 collective-permute-done.8
  34.9 3.4 %collective-permute-done.5.refs_3_.refs_2_ = bf16[3,136,512]{2,1,0:T(8,128)(2,1)S(1)} collective-permute-done((bf16[3,136,512]{2,1,0:T(8,128)(2,1)S(1)}, bf16[3,136,512]{2,1,0:T(8,128)(2,1)S(1)}, u32[]{:S(2)}, u32[]{:S(2)}) %collective-permute-start.5) | collective-permute-done | bytes 417824 | tf_op jit(solution)/shard_map/ppermute | solution.py:244
  38.3 1.5 %collective-permute-start.13 = (f32[32,128]{1,0:T(8,128)S(1)}, f32[32,128]{1,0:T(8,128)S(1)}, u32[]{:S(2)}, u32[]{:S(2)}) collective-permute-start(f32[32,128]{1,0:T(8,128)S(1)} %add.155), channel_id=1, source_target_pairs={{0,2},{1,3},{2,0},{3,1},{4,6},{5,7},{6,4},{7,5},{8,10},{9,11},{10,... | collective-permute-start | bytes 49160 | tf_op jit(solution)/shard_map/ppermute | solution.py:244
  41.0 1.1 collective-permute-done.13
  42.5 4.2 %collective-permute-done.14 = bf16[1,32,128]{2,1,0:T(8,128)(2,1)S(1)} collective-permute-done((bf16[1,32,128]{2,1,0:T(8,128)(2,1)S(1)}, bf16[1,32,128]{2,1,0:T(8,128)(2,1)S(1)}, u32[]{:S(2)}, u32[]{:S(2)}) %collective-permute-start.14) | collective-permute-done | bytes 8224 | tf_op jit(solution)/shard_map/ppermute | solution.py:244
  47.6 1.6 %shard_map.118 = (bf16[8,512,128]{2,1,0:T(8,128)(2,1)S(1)}, bf16[8,128,512]{2,1,0:T(8,128)(2,1)S(1)}, f32[16,256,128]{2,1,0:T(8,128)S(1)}) custom-call(s32[9]{0:T(128)S(1)} %pad_add_fusion.1.scalar_ref, bf16[1,136,512]{2,1,0:T(8,128)(2,1)S(1)} %fusion.41.refs_0_, bf16[3,136,512]{2,1,0:T(8,128)(2,1)S(1)} %pad_maximum_fusion.1.refs_1_, ...), custom_call_target="tpu_custom_call" | custom-call | flops 1000000 | bytes 1000 | tf_op jit(solution)/shard_map/pallas_call | solution.py:76
  49.2 1.2 collective-permute-done.15
  50.4 7.7 %shard_map.119.refs_9_ = f32[16,256,256]{2,1,0:T(8,128)S(1)} custom-call(s32[9]{0:T(128)S(1)} %pad_add_fusion.scalar_ref, bf16[128,2048]{1,0:T(8,128)(2,1)S(1)} %copy-done.1, bf16[4,136,512]{2,1,0:T(8,128)(2,1)S(1)} %pad_maximum_fusion.refs_1_, bf16[3,136,512]{2,1,0:T(8,128)(2,1)S(1)} %collective-permute-done.5.refs_3_.refs_2_, ...), custom_call_target="tpu_custom_call" | custom-call | flops 1000000 | bytes 1000 | tf_op jit(solution)/shard_map/pallas_call | solution.py:187
  58.8 3.3 %collective-permute-done.18 = bf16[4,32,128]{2,1,0:T(8,128)(2,1)S(1)} collective-permute-done((bf16[4,32,128]{2,1,0:T(8,128)(2,1)S(1)}, bf16[4,32,128]{2,1,0:T(8,128)(2,1)S(1)}, u32[]{:S(2)}, u32[]{:S(2)}) %collective-permute-start.18) | collective-permute-done | bytes 32800 | tf_op jit(solution)/shard_map/ppermute | solution.py:244
  62.2 9.2 %shard_map.120.hidden_ref = bf16[16,256,128]{2,1,0:T(8,128)(2,1)S(1)} custom-call(s32[9]{0:T(128)S(1)} %pad_add_fusion.scalar_ref, bf16[128,2048]{1,0:T(8,128)(2,1)S(1)} %copy-done.1, bf16[4,136,512]{2,1,0:T(8,128)(2,1)S(1)} %collective-permute-done.9.refs_1_, bf16[3,136,512]{2,1,0:T(8,128)(2,1)S(1)} %collective-permute-done.12.refs_2_, ...), custom_call_target="tpu_custom_call" | custom-call | flops 1000000 | bytes 1000 | tf_op jit(solution)/shard_map/pallas_call | solution.py:187
  71.4 6.3 %shard_map.121 = (bf16[8,128,256]{2,1,0:T(8,128)(2,1)S(1)}, f32[8,128,256]{2,1,0:T(8,128)S(1)}, bf16[8,128,256]{2,1,0:T(8,128)(2,1)S(1)}, f32[8,128,256]{2,1,0:T(8,128)S(1)}) custom-call(s32[9]{0:T(128)S(1)} %pad_add_fusion.scalar_ref, bf16[16,2048,128]{2,1,0:T(8,128)(2,1)} %down_hbm.3, bf16[16,256,128]{2,1,0:T(8,128)(2,1)S(1)} %shard_map.120.hidden_ref, ...), custom_call_target="tpu_custom_call" | custom-call | flops 1000000 | bytes 1000 | tf_op jit(solution)/shard_map/pallas_call | solution.py:227
  78.3 1.4 %collective-permute-done.20 = bf16[8,128,256]{2,1,0:T(8,128)(2,1)S(1)} collective-permute-done((bf16[8,128,256]{2,1,0:T(8,128)(2,1)S(1)}, bf16[8,128,256]{2,1,0:T(8,128)(2,1)S(1)}, u32[]{:S(2)}, u32[]{:S(2)}) %collective-permute-start.20) | collective-permute-done | bytes 524320 | tf_op jit(solution)/shard_map/ppermute | solution.py:244
  80.6 1.6 %collective-permute-start.21 = (bf16[4,128,256]{2,1,0:T(8,128)(2,1)S(1)}, bf16[4,128,256]{2,1,0:T(8,128)(2,1)S(1)}, u32[]{:S(2)}, u32[]{:S(2)}) collective-permute-start(bf16[4,128,256]{2,1,0:T(8,128)(2,1)S(1)} %get-tuple-element.78), channel_id=1, source_target_pairs={{0,2},{1,3},{2,0},{3,1},{4,6},{5,7},{6,4},{7,5},{8,10},{9,11},{10,... | collective-permute-start | bytes 786440 | tf_op jit(solution)/shard_map/ppermute | solution.py:244
  82.8 6.3 %shard_map.122 = (bf16[8,128,256]{2,1,0:T(8,128)(2,1)S(1)}, f32[8,128,256]{2,1,0:T(8,128)S(1)}, bf16[8,128,256]{2,1,0:T(8,128)(2,1)S(1)}, f32[8,128,256]{2,1,0:T(8,128)S(1)}) custom-call(s32[9]{0:T(128)S(1)} %pad_add_fusion.scalar_ref, bf16[16,2048,128]{2,1,0:T(8,128)(2,1)} %down_hbm.3, bf16[16,256,128]{2,1,0:T(8,128)(2,1)S(1)} %shard_map.120.hidden_ref, ...), custom_call_target="tpu_custom_call" | custom-call | flops 1000000 | bytes 1000 | tf_op jit(solution)/shard_map/pallas_call | solution.py:227
  89.1 1.2 %collective-permute-done.22 = bf16[4,128,256]{2,1,0:T(8,128)(2,1)S(1)} collective-permute-done((bf16[4,128,256]{2,1,0:T(8,128)(2,1)S(1)}, bf16[4,128,256]{2,1,0:T(8,128)(2,1)S(1)}, u32[]{:S(2)}, u32[]{:S(2)}) %collective-permute-start.22) | collective-permute-done | bytes 262176 | tf_op jit(solution)/shard_map/ppermute | solution.py:244
  91.2 1.6 %collective-permute-start.31 = (bf16[4,128,256]{2,1,0:T(8,128)(2,1)S(1)}, bf16[4,128,256]{2,1,0:T(8,128)(2,1)S(1)}, u32[]{:S(2)}, u32[]{:S(2)}) collective-permute-start(bf16[4,128,256]{2,1,0:T(8,128)(2,1)S(1)} %add_convert_fusion.1), channel_id=1, source_target_pairs={{0,2},{1,3},{2,0},{3,1},{4,6},{5,7},{6,4},{7,5},{8,10},{9,11},{10,... | collective-permute-start | bytes 786440 | tf_op jit(solution)/shard_map/ppermute | solution.py:244
  93.7 1.6 %collective-permute-start.30 = (bf16[4,128,256]{2,1,0:T(8,128)(2,1)S(1)}, bf16[4,128,256]{2,1,0:T(8,128)(2,1)S(1)}, u32[]{:S(2)}, u32[]{:S(2)}) collective-permute-start(bf16[4,128,256]{2,1,0:T(8,128)(2,1)S(1)} %slice.386), channel_id=1, source_target_pairs={{0,4},{4,0},{8,12},{12,8},{16,20},{20,16},{24,28},{28,24},{1,5},{5... | collective-permute-start | bytes 786440 | tf_op jit(solution)/shard_map/ppermute | solution.py:244
  95.2 4.2 %collective-permute-done.24 = bf16[4,128,256]{2,1,0:T(8,128)(2,1)S(1)} collective-permute-done((bf16[4,128,256]{2,1,0:T(8,128)(2,1)S(1)}, bf16[4,128,256]{2,1,0:T(8,128)(2,1)S(1)}, u32[]{:S(2)}, u32[]{:S(2)}) %collective-permute-start.24) | collective-permute-done | bytes 262176 | tf_op jit(solution)/shard_map/ppermute | solution.py:244
  99.4 2.7 %collective-permute-done.25 = bf16[4,128,256]{2,1,0:T(8,128)(2,1)S(1)} collective-permute-done((bf16[4,128,256]{2,1,0:T(8,128)(2,1)S(1)}, bf16[4,128,256]{2,1,0:T(8,128)(2,1)S(1)}, u32[]{:S(2)}, u32[]{:S(2)}) %collective-permute-start.25) | collective-permute-done | bytes 262176 | tf_op jit(solution)/shard_map/ppermute | solution.py:244
  104.1 2.6 %collective-permute-start.28 = (bf16[128,256]{1,0:T(8,128)(2,1)S(1)}, bf16[128,256]{1,0:T(8,128)(2,1)S(1)}, u32[]{:S(2)}, u32[]{:S(2)}) collective-permute-start(bf16[128,256]{1,0:T(8,128)(2,1)S(1)} %get-tuple-element.82), channel_id=1, source_target_pairs={{0,24},{4,28},{8,16},{12,20},{16,8},{20,12},{24,0},{28,4},{1,25},{... | collective-permute-start | bytes 196616 | tf_op jit(solution)/shard_map/ppermute | solution.py:244
  108.8 2.6 %collective-permute-start.34 = (bf16[128,256]{1,0:T(8,128)(2,1)S(1)}, bf16[128,256]{1,0:T(8,128)(2,1)S(1)}, u32[]{:S(2)}, u32[]{:S(2)}) collective-permute-start(bf16[128,256]{1,0:T(8,128)(2,1)S(1)} %get-tuple-element.85), channel_id=1, source_target_pairs={{0,24},{4,28},{8,16},{12,20},{16,8},{20,12},{24,0},{28,4},{1,25},{... | collective-permute-start | bytes 196616 | tf_op jit(solution)/shard_map/ppermute | solution.py:244
  111.8 3.6 %collective-permute-done.33 = bf16[128,256]{1,0:T(8,128)(2,1)S(1)} collective-permute-done((bf16[128,256]{1,0:T(8,128)(2,1)S(1)}, bf16[128,256]{1,0:T(8,128)(2,1)S(1)}, u32[]{:S(2)}, u32[]{:S(2)}) %collective-permute-start.33) | collective-permute-done | bytes 65568 | tf_op jit(solution)/shard_map/ppermute | solution.py:244
  (125 shorter events, 20.6 us)
Async XLA Ops:
  2.4 18.6 %collective-permute-start = (bf16[136,512]{1,0:T(8,128)(2,1)S(1)}, bf16[136,512]{1,0:T(8,128)(2,1)S(1)}, u32[]{:S(2)}, u32[]{:S(2)}) collective-permute-start(bf16[136,512]{1,0:T(8,128)(2,1)S(1)} %maximum_maximum_fusion), channel_id=1, source_target_pairs={{0,4},{4,0},{8,12},{12,8},{16,20},{20,16},{24,28},{28,24},{1,5},{5... | collective-permute-start | bytes 417800 | tf_op jit(solution)/shard_map/ppermute | solution.py:244
  5.4 15.5 %collective-permute-start.1 = (bf16[136,512]{1,0:T(8,128)(2,1)S(1)}, bf16[136,512]{1,0:T(8,128)(2,1)S(1)}, u32[]{:S(2)}, u32[]{:S(2)}) collective-permute-start(bf16[136,512]{1,0:T(8,128)(2,1)S(1)} %maximum_maximum_fusion), channel_id=1, source_target_pairs={{0,8},{4,12},{8,0},{12,4},{16,24},{20,28},{24,16},{28,20},{1,9},{5... | collective-permute-start | bytes 417800 | tf_op jit(solution)/shard_map/ppermute | solution.py:244
  7.0 14.0 %collective-permute-start.2 = (bf16[136,512]{1,0:T(8,128)(2,1)S(1)}, bf16[136,512]{1,0:T(8,128)(2,1)S(1)}, u32[]{:S(2)}, u32[]{:S(2)}) collective-permute-start(bf16[136,512]{1,0:T(8,128)(2,1)S(1)} %maximum_maximum_fusion), channel_id=1, source_target_pairs={{0,16},{4,20},{8,24},{12,28},{16,0},{20,4},{24,8},{28,12},{1,17},{... | collective-permute-start | bytes 417800 | tf_op jit(solution)/shard_map/ppermute | solution.py:244
  9.6 11.4 %collective-permute-start.3 = (bf16[136,512]{1,0:T(8,128)(2,1)S(1)}, bf16[136,512]{1,0:T(8,128)(2,1)S(1)}, u32[]{:S(2)}, u32[]{:S(2)}) collective-permute-start(bf16[136,512]{1,0:T(8,128)(2,1)S(1)} %maximum_maximum_fusion), channel_id=1, source_target_pairs={{0,24},{4,28},{8,16},{12,20},{16,8},{20,12},{24,0},{28,4},{1,25},{... | collective-permute-start | bytes 417800 | tf_op jit(solution)/shard_map/ppermute | solution.py:244
  13.8 7.1 %collective-permute-start.4 = (bf16[1024,128]{1,0:T(8,128)(2,1)S(1)}, bf16[1024,128]{1,0:T(8,128)(2,1)S(1)}, u32[]{:S(2)}, u32[]{:S(2)}) collective-permute-start(bf16[1024,128]{1,0:T(8,128)(2,1)S(1)} %slice_dynamic-update-slice_fusion), channel_id=1, source_target_pairs={{0,4},{4,0},{8,12},{12,8},{16,20},{20,16},{24,28},{28,24},{1,5},{5... | collective-permute-start | bytes 786440 | tf_op jit(solution)/shard_map/ppermute | solution.py:244
  21.1 5.7 %collective-permute-start.6 = (bf16[768,128]{1,0:T(8,128)(2,1)S(1)}, bf16[768,128]{1,0:T(8,128)(2,1)S(1)}, u32[]{:S(2)}, u32[]{:S(2)}) collective-permute-start(bf16[768,128]{1,0:T(8,128)(2,1)S(1)} %constant_dynamic-update-slice_fusion.4), channel_id=1, source_target_pairs={{0,8},{4,12},{8,0},{12,4},{16,24},{20,28},{24,16},{28,20},{1,9},{5... | collective-permute-start | bytes 589832 | tf_op jit(solution)/shard_map/ppermute | solution.py:244
  22.6 15.7 %collective-permute-start.9 = (bf16[4,136,512]{2,1,0:T(8,128)(2,1)S(1)}, bf16[4,136,512]{2,1,0:T(8,128)(2,1)S(1)}, u32[]{:S(2)}, u32[]{:S(2)}) collective-permute-start(bf16[4,136,512]{2,1,0:T(8,128)(2,1)S(1)} %pad_maximum_fusion.refs_1_), channel_id=1, source_target_pairs={{0,2},{1,3},{2,0},{3,1},{4,6},{5,7},{6,4},{7,5},{8,10},{9,11},{10,... | collective-permute-start | bytes 1671176 | tf_op jit(solution)/shard_map/ppermute | solution.py:244
  27.0 6.6 %collective-permute-start.7 = (bf16[384,128]{1,0:T(8,128)(2,1)S(1)}, bf16[384,128]{1,0:T(8,128)(2,1)S(1)}, u32[]{:S(2)}, u32[]{:S(2)}) collective-permute-start(bf16[384,128]{1,0:T(8,128)(2,1)S(1)} %select_dynamic-update-slice_fusion), channel_id=1, source_target_pairs={{0,16},{4,20},{8,24},{12,28},{16,0},{20,4},{24,8},{28,12},{1,17},{... | collective-permute-start | bytes 294920 | tf_op jit(solution)/shard_map/ppermute | solution.py:244
  29.4 8.9 %collective-permute-start.5 = (bf16[3,136,512]{2,1,0:T(8,128)(2,1)S(1)}, bf16[3,136,512]{2,1,0:T(8,128)(2,1)S(1)}, u32[]{:S(2)}, u32[]{:S(2)}) collective-permute-start(bf16[3,136,512]{2,1,0:T(8,128)(2,1)S(1)} %pad_maximum_fusion.1.refs_1_), channel_id=1, source_target_pairs={{0,4},{4,0},{8,12},{12,8},{16,20},{20,16},{24,28},{28,24},{1,5},{5... | collective-permute-start | bytes 1253384 | tf_op jit(solution)/shard_map/ppermute | solution.py:244
  38.3 3.7 %collective-permute-start.13 = (f32[32,128]{1,0:T(8,128)S(1)}, f32[32,128]{1,0:T(8,128)S(1)}, u32[]{:S(2)}, u32[]{:S(2)}) collective-permute-start(f32[32,128]{1,0:T(8,128)S(1)} %add.155), channel_id=1, source_target_pairs={{0,2},{1,3},{2,0},{3,1},{4,6},{5,7},{6,4},{7,5},{8,10},{9,11},{10,... | collective-permute-start | bytes 49160 | tf_op jit(solution)/shard_map/ppermute | solution.py:244
  39.9 10.5 %collective-permute-start.10 = (bf16[4,136,512]{2,1,0:T(8,128)(2,1)S(1)}, bf16[4,136,512]{2,1,0:T(8,128)(2,1)S(1)}, u32[]{:S(2)}, u32[]{:S(2)}) collective-permute-start(bf16[4,136,512]{2,1,0:T(8,128)(2,1)S(1)} %pad_maximum_fusion.refs_1_), channel_id=1, source_target_pairs={{0,1},{1,0},{2,3},{3,2},{4,5},{5,4},{6,7},{7,6},{8,9},{9,8},{10,11... | collective-permute-start | bytes 1671176 | tf_op jit(solution)/shard_map/ppermute | solution.py:244
  39.9 10.5 %collective-permute-start.11 = (bf16[3,136,512]{2,1,0:T(8,128)(2,1)S(1)}, bf16[3,136,512]{2,1,0:T(8,128)(2,1)S(1)}, u32[]{:S(2)}, u32[]{:S(2)}) collective-permute-start(bf16[3,136,512]{2,1,0:T(8,128)(2,1)S(1)} %collective-permute-done.5.refs_3_.refs_2_), channel_id=1, source_target_pairs={{0,1},{1,0},{2,3},{3,2},{4,5},{5,4},{6,7},{7,6},{8,9},{9,8},{10,11... | collective-permute-start | bytes 1253384 | tf_op jit(solution)/shard_map/ppermute | solution.py:244
  40.4 17.7 %collective-permute-start.12 = (bf16[3,136,512]{2,1,0:T(8,128)(2,1)S(1)}, bf16[3,136,512]{2,1,0:T(8,128)(2,1)S(1)}, u32[]{:S(2)}, u32[]{:S(2)}) collective-permute-start(bf16[3,136,512]{2,1,0:T(8,128)(2,1)S(1)} %collective-permute-done.5.refs_3_.refs_2_), channel_id=1, source_target_pairs={{0,2},{1,3},{2,0},{3,1},{4,6},{5,7},{6,4},{7,5},{8,10},{9,11},{10,... | collective-permute-start | bytes 1253384 | tf_op jit(solution)/shard_map/ppermute | solution.py:244
  40.9 21.2 %collective-permute-start.16 = (bf16[4,136,512]{2,1,0:T(8,128)(2,1)S(1)}, bf16[4,136,512]{2,1,0:T(8,128)(2,1)S(1)}, u32[]{:S(2)}, u32[]{:S(2)}) collective-permute-start(bf16[4,136,512]{2,1,0:T(8,128)(2,1)S(1)} %collective-permute-done.9.refs_1_), channel_id=1, source_target_pairs={{0,1},{1,0},{2,3},{3,2},{4,5},{5,4},{6,7},{7,6},{8,9},{9,8},{10,11... | collective-permute-start | bytes 1671176 | tf_op jit(solution)/shard_map/ppermute | solution.py:244
  42.1 4.5 %collective-permute-start.14 = (bf16[1,32,128]{2,1,0:T(8,128)(2,1)S(1)}, bf16[1,32,128]{2,1,0:T(8,128)(2,1)S(1)}, u32[]{:S(2)}, u32[]{:S(2)}) collective-permute-start(bf16[1,32,128]{2,1,0:T(8,128)(2,1)S(1)} %fusion.27), channel_id=1, source_target_pairs={{0,16},{4,20},{8,24},{12,28},{16,0},{20,4},{24,8},{28,12},{1,17},{... | collective-permute-start | bytes 24584 | tf_op jit(solution)/shard_map/ppermute | solution.py:244
  46.6 3.7 %collective-permute-start.15 = (bf16[2,32,128]{2,1,0:T(8,128)(2,1)S(1)}, bf16[2,32,128]{2,1,0:T(8,128)(2,1)S(1)}, u32[]{:S(2)}, u32[]{:S(2)}) collective-permute-start(bf16[2,32,128]{2,1,0:T(8,128)(2,1)S(1)} %pad_maximum_fusion.5), channel_id=1, source_target_pairs={{0,8},{4,12},{8,0},{12,4},{16,24},{20,28},{24,16},{28,20},{1,9},{5... | collective-permute-start | bytes 49160 | tf_op jit(solution)/shard_map/ppermute | solution.py:244
  58.1 4.0 %collective-permute-start.18 = (bf16[4,32,128]{2,1,0:T(8,128)(2,1)S(1)}, bf16[4,32,128]{2,1,0:T(8,128)(2,1)S(1)}, u32[]{:S(2)}, u32[]{:S(2)}) collective-permute-start(bf16[4,32,128]{2,1,0:T(8,128)(2,1)S(1)} %pad_maximum_fusion.4), channel_id=1, source_target_pairs={{0,4},{4,0},{8,12},{12,8},{16,20},{20,16},{24,28},{28,24},{1,5},{5... | collective-permute-start | bytes 98312 | tf_op jit(solution)/shard_map/ppermute | solution.py:244
  58.7 3.4 %collective-permute-start.17 = (bf16[3,136,512]{2,1,0:T(8,128)(2,1)S(1)}, bf16[3,136,512]{2,1,0:T(8,128)(2,1)S(1)}, u32[]{:S(2)}, u32[]{:S(2)}) collective-permute-start(bf16[3,136,512]{2,1,0:T(8,128)(2,1)S(1)} %collective-permute-done.12.refs_2_), channel_id=1, source_target_pairs={{0,1},{1,0},{2,3},{3,2},{4,5},{5,4},{6,7},{7,6},{8,9},{9,8},{10,11... | collective-permute-start | bytes 1253384 | tf_op jit(solution)/shard_map/ppermute | solution.py:244
  77.8 2.6 %collective-permute-start.19 = (bf16[8,128,256]{2,1,0:T(8,128)(2,1)S(1)}, bf16[8,128,256]{2,1,0:T(8,128)(2,1)S(1)}, u32[]{:S(2)}, u32[]{:S(2)}) collective-permute-start(bf16[8,128,256]{2,1,0:T(8,128)(2,1)S(1)} %get-tuple-element.57), channel_id=1, source_target_pairs={{0,1},{1,0},{2,3},{3,2},{4,5},{5,4},{6,7},{7,6},{8,9},{9,8},{10,11... | collective-permute-start | bytes 1572872 | tf_op jit(solution)/shard_map/ppermute | solution.py:244
  80.6 8.5 %collective-permute-start.21 = (bf16[4,128,256]{2,1,0:T(8,128)(2,1)S(1)}, bf16[4,128,256]{2,1,0:T(8,128)(2,1)S(1)}, u32[]{:S(2)}, u32[]{:S(2)}) collective-permute-start(bf16[4,128,256]{2,1,0:T(8,128)(2,1)S(1)} %get-tuple-element.78), channel_id=1, source_target_pairs={{0,2},{1,3},{2,0},{3,1},{4,6},{5,7},{6,4},{7,5},{8,10},{9,11},{10,... | collective-permute-start | bytes 786440 | tf_op jit(solution)/shard_map/ppermute | solution.py:244
  82.2 8.1 %collective-permute-start.22 = (bf16[4,128,256]{2,1,0:T(8,128)(2,1)S(1)}, bf16[4,128,256]{2,1,0:T(8,128)(2,1)S(1)}, u32[]{:S(2)}, u32[]{:S(2)}) collective-permute-start(bf16[4,128,256]{2,1,0:T(8,128)(2,1)S(1)} %slice.387), channel_id=1, source_target_pairs={{0,4},{4,0},{8,12},{12,8},{16,20},{20,16},{24,28},{28,24},{1,5},{5... | collective-permute-start | bytes 786440 | tf_op jit(solution)/shard_map/ppermute | solution.py:244
  90.3 9.1 %collective-permute-start.24 = (bf16[4,128,256]{2,1,0:T(8,128)(2,1)S(1)}, bf16[4,128,256]{2,1,0:T(8,128)(2,1)S(1)}, u32[]{:S(2)}, u32[]{:S(2)}) collective-permute-start(bf16[4,128,256]{2,1,0:T(8,128)(2,1)S(1)} %get-tuple-element.77), channel_id=1, source_target_pairs={{0,2},{1,3},{2,0},{3,1},{4,6},{5,7},{6,4},{7,5},{8,10},{9,11},{10,... | collective-permute-start | bytes 786440 | tf_op jit(solution)/shard_map/ppermute | solution.py:244
  90.9 2.6 %collective-permute-start.29 = (bf16[8,128,256]{2,1,0:T(8,128)(2,1)S(1)}, bf16[8,128,256]{2,1,0:T(8,128)(2,1)S(1)}, u32[]{:S(2)}, u32[]{:S(2)}) collective-permute-start(bf16[8,128,256]{2,1,0:T(8,128)(2,1)S(1)} %get-tuple-element.71), channel_id=1, source_target_pairs={{0,1},{1,0},{2,3},{3,2},{4,5},{5,4},{6,7},{7,6},{8,9},{9,8},{10,11... | collective-permute-start | bytes 1572872 | tf_op jit(solution)/shard_map/ppermute | solution.py:244
  91.2 15.6 %collective-permute-start.31 = (bf16[4,128,256]{2,1,0:T(8,128)(2,1)S(1)}, bf16[4,128,256]{2,1,0:T(8,128)(2,1)S(1)}, u32[]{:S(2)}, u32[]{:S(2)}) collective-permute-start(bf16[4,128,256]{2,1,0:T(8,128)(2,1)S(1)} %add_convert_fusion.1), channel_id=1, source_target_pairs={{0,2},{1,3},{2,0},{3,1},{4,6},{5,7},{6,4},{7,5},{8,10},{9,11},{10,... | collective-permute-start | bytes 786440 | tf_op jit(solution)/shard_map/ppermute | solution.py:244
  92.9 9.2 %collective-permute-start.25 = (bf16[4,128,256]{2,1,0:T(8,128)(2,1)S(1)}, bf16[4,128,256]{2,1,0:T(8,128)(2,1)S(1)}, u32[]{:S(2)}, u32[]{:S(2)}) collective-permute-start(bf16[4,128,256]{2,1,0:T(8,128)(2,1)S(1)} %fusion.1), channel_id=1, source_target_pairs={{0,4},{4,0},{8,12},{12,8},{16,20},{20,16},{24,28},{28,24},{1,5},{5... | collective-permute-start | bytes 786440 | tf_op jit(solution)/shard_map/ppermute | solution.py:244
  93.7 13.2 %collective-permute-start.30 = (bf16[4,128,256]{2,1,0:T(8,128)(2,1)S(1)}, bf16[4,128,256]{2,1,0:T(8,128)(2,1)S(1)}, u32[]{:S(2)}, u32[]{:S(2)}) collective-permute-start(bf16[4,128,256]{2,1,0:T(8,128)(2,1)S(1)} %slice.386), channel_id=1, source_target_pairs={{0,4},{4,0},{8,12},{12,8},{16,20},{20,16},{24,28},{28,24},{1,5},{5... | collective-permute-start | bytes 786440 | tf_op jit(solution)/shard_map/ppermute | solution.py:244
  102.3 6.5 %collective-permute-start.26 = (bf16[128,256]{1,0:T(8,128)(2,1)S(1)}, bf16[128,256]{1,0:T(8,128)(2,1)S(1)}, u32[]{:S(2)}, u32[]{:S(2)}) collective-permute-start(bf16[128,256]{1,0:T(8,128)(2,1)S(1)} %get-tuple-element.81), channel_id=1, source_target_pairs={{0,8},{4,12},{8,0},{12,4},{16,24},{20,28},{24,16},{28,20},{1,9},{5... | collective-permute-start | bytes 196616 | tf_op jit(solution)/shard_map/ppermute | solution.py:244
  103.3 8.1 %collective-permute-start.27 = (bf16[128,256]{1,0:T(8,128)(2,1)S(1)}, bf16[128,256]{1,0:T(8,128)(2,1)S(1)}, u32[]{:S(2)}, u32[]{:S(2)}) collective-permute-start(bf16[128,256]{1,0:T(8,128)(2,1)S(1)} %get-tuple-element.83), channel_id=1, source_target_pairs={{0,16},{4,20},{8,24},{12,28},{16,0},{20,4},{24,8},{28,12},{1,17},{... | collective-permute-start | bytes 196616 | tf_op jit(solution)/shard_map/ppermute | solution.py:244
  104.1 7.3 %collective-permute-start.28 = (bf16[128,256]{1,0:T(8,128)(2,1)S(1)}, bf16[128,256]{1,0:T(8,128)(2,1)S(1)}, u32[]{:S(2)}, u32[]{:S(2)}) collective-permute-start(bf16[128,256]{1,0:T(8,128)(2,1)S(1)} %get-tuple-element.82), channel_id=1, source_target_pairs={{0,24},{4,28},{8,16},{12,20},{16,8},{20,12},{24,0},{28,4},{1,25},{... | collective-permute-start | bytes 196616 | tf_op jit(solution)/shard_map/ppermute | solution.py:244
  106.9 4.9 %collective-permute-start.32 = (bf16[128,256]{1,0:T(8,128)(2,1)S(1)}, bf16[128,256]{1,0:T(8,128)(2,1)S(1)}, u32[]{:S(2)}, u32[]{:S(2)}) collective-permute-start(bf16[128,256]{1,0:T(8,128)(2,1)S(1)} %get-tuple-element.84), channel_id=1, source_target_pairs={{0,8},{4,12},{8,0},{12,4},{16,24},{20,28},{24,16},{28,20},{1,9},{5... | collective-permute-start | bytes 196616 | tf_op jit(solution)/shard_map/ppermute | solution.py:244
  108.0 7.5 %collective-permute-start.33 = (bf16[128,256]{1,0:T(8,128)(2,1)S(1)}, bf16[128,256]{1,0:T(8,128)(2,1)S(1)}, u32[]{:S(2)}, u32[]{:S(2)}) collective-permute-start(bf16[128,256]{1,0:T(8,128)(2,1)S(1)} %get-tuple-element.86), channel_id=1, source_target_pairs={{0,16},{4,20},{8,24},{12,28},{16,0},{20,4},{24,8},{28,12},{1,17},{... | collective-permute-start | bytes 196616 | tf_op jit(solution)/shard_map/ppermute | solution.py:244
  108.8 6.7 %collective-permute-start.34 = (bf16[128,256]{1,0:T(8,128)(2,1)S(1)}, bf16[128,256]{1,0:T(8,128)(2,1)S(1)}, u32[]{:S(2)}, u32[]{:S(2)}) collective-permute-start(bf16[128,256]{1,0:T(8,128)(2,1)S(1)} %get-tuple-element.85), channel_id=1, source_target_pairs={{0,24},{4,28},{8,16},{12,20},{16,8},{20,12},{24,0},{28,4},{1,25},{... | collective-permute-start | bytes 196616 | tf_op jit(solution)/shard_map/ppermute | solution.py:244
  (5 other events, 68.1 us)

commit v5 on v4

--- a/solution.py
+++ b/solution.py
@@ -19,7 +19,6 @@
 UNROLL = 16
 COST = pl.CostEstimate(flops=1_000_000, bytes_accessed=1_000, transcendentals=0)
 ORDER = (0, 2, 4, 6, 1, 3, 5, 7)
-HALVING = (0, 4, 2, 6, 1, 5, 3, 7)
 GATHERED = (0, 4, 2, 6, 1, 5, 3, 7)
 
 
@@ -301,17 +300,12 @@
     ahead = [xor_move(block, "dp", n) for n in (1, 2, 4, 6)]
     layout = ((0,), (4, 1, 2, 3), (5, 6, 7))
 
-    natural = i ^ jnp.array(HALVING, jnp.int32)
-    adapters = jnp.sum(
-        jnp.where(natural[:, None] == jnp.arange(dp_count)[None, :], request_adapter[None, :], 0), axis=1
-    )
-    columns = nt_dot(select_adapters(adapters, adapter_input_maps.shape[1], i), adapter_input_maps)
+    chosen = select_adapters(request_adapter, adapter_input_maps.shape[1], i)
+    columns = nt_dot(chosen, adapter_input_maps)
     columns = columns.astype(BF16)
 
     halves = adapter_output_maps.reshape(adapter_output_maps.shape[0], -1)
-    tables = jnp.dot(
-        select_adapters(request_adapter, halves.shape[0], i), halves, preferred_element_type=F32
-    ).astype(BF16)
+    tables = jnp.dot(chosen, halves, preferred_element_type=F32).astype(BF16)
     share = halves.shape[1] // 2
     upper = i >= dp_count // 2
     first_expert = (i * units) % experts_all
@@ -326,11 +320,15 @@
 
     def halve(columns, given, bits):
         kept = columns.shape[0] // 2
-        got = xor_move(jnp.concatenate(strip(columns[kept:]) + given, axis=0), "dp", bits)
+        pairs = columns.reshape((-1, 2, DOUBLE_RANK, quarter))
+        side = (i // bits) % 2
+        mine_half = lax.dynamic_index_in_dim(pairs, side, 1, keepdims=False).reshape(kept, quarter)
+        sent_half = lax.dynamic_index_in_dim(pairs, 1 - side, 1, keepdims=False).reshape(kept, quarter)
+        got = xor_move(jnp.concatenate(strip(sent_half) + given, axis=0), "dp", bits)
         more = jnp.concatenate([got[n * kept : (n + 1) * kept] for n in range(strips)], axis=1)
         got = got[strips * kept :]
         size = given[0].shape[0]
-        return columns[:kept] + more, [got[n * size : (n + 1) * size] for n in range(len(given))]
+        return mine_half + more, [got[n * size : (n + 1) * size] for n in range(len(given))]
 
     tables = strip(tables)
     columns, came = halve(columns, tables, 1)

time: 116 us -> 116 us (level)
  other arithmetic: 7.42 us -> 5.86 us
  transfers between devices with their start and end apart: 35 -> 35, of which waited for: 17 -> 18; matrix products, arithmetic and copies ran while one was open for 6% -> 5% of each run, Pallas kernels for 13% -> 13%
where the time goes in v5:
time: 116 us
  waiting for transfers between devices  40.6 us (35%)
  starting transfers between devices  35 us (30%)
  Pallas kernels  31.1 us (27%)
  other arithmetic  5.86 us (5%)
  matrix products  1.55 us (1%)
  local copies, waits for them, and re-layouts  1.41 us (1%)
    ppermute x35, waiting for transfers between devices, xor_move(): return lax.ppermute(value, axis, [(i, i ^ bits) for i in range(size)])  40.6 us
    ppermute x35, starting transfers between devices, xor_move(): return lax.ppermute(value, axis, [(i, i ^ bits) for i in range(size)])  35 us
    pallas_call x2, Pallas kernels, expand(): pl.pallas_call(functools.partial(expand_kernel, units, quarters, first, l...  16.9 us
    pallas_call x2, Pallas kernels, contract(): pl.pallas_call(functools.partial(contract_kernel, units, jobs, parts), in...  12.7 us
  transfers between devices with their start and end apart: 35, of which 18 were waited for; matrix products, arithmetic and copies ran while one was open for 5% of the time, Pallas kernels for 13%

profile of v5, /device:TPU:0, one launch (start us, length us, event | category | flops | bytes accessed | tf_op | source)
XLA Modules:
  0.0 115.9 jit_solution(14372675296380049743)
XLA Ops:
  2.4 3.0 %collective-permute-start = (bf16[136,512]{1,0:T(8,128)(2,1)S(1)}, bf16[136,512]{1,0:T(8,128)(2,1)S(1)}, u32[]{:S(2)}, u32[]{:S(2)}) collective-permute-start(bf16[136,512]{1,0:T(8,128)(2,1)S(1)} %maximum_maximum_fusion), channel_id=1, source_target_pairs={{0,4},{4,0},{8,12},{12,8},{16,20},{20,16},{24,28},{28,24},{1,5},{5... | collective-permute-start | bytes 417800 | tf_op jit(solution)/shard_map/ppermute | solution.py:243
  5.4 1.6 %collective-permute-start.1 = (bf16[136,512]{1,0:T(8,128)(2,1)S(1)}, bf16[136,512]{1,0:T(8,128)(2,1)S(1)}, u32[]{:S(2)}, u32[]{:S(2)}) collective-permute-start(bf16[136,512]{1,0:T(8,128)(2,1)S(1)} %maximum_maximum_fusion), channel_id=1, source_target_pairs={{0,8},{4,12},{8,0},{12,4},{16,24},{20,28},{24,16},{28,20},{1,9},{5... | collective-permute-start | bytes 417800 | tf_op jit(solution)/shard_map/ppermute | solution.py:243
  7.0 2.6 %collective-permute-start.2 = (bf16[136,512]{1,0:T(8,128)(2,1)S(1)}, bf16[136,512]{1,0:T(8,128)(2,1)S(1)}, u32[]{:S(2)}, u32[]{:S(2)}) collective-permute-start(bf16[136,512]{1,0:T(8,128)(2,1)S(1)} %maximum_maximum_fusion), channel_id=1, source_target_pairs={{0,16},{4,20},{8,24},{12,28},{16,0},{20,4},{24,8},{28,12},{1,17},{... | collective-permute-start | bytes 417800 | tf_op jit(solution)/shard_map/ppermute | solution.py:243
  14.1 5.2 %collective-permute-done.4 = bf16[1024,128]{1,0:T(8,128)(2,1)S(1)} collective-permute-done((bf16[1024,128]{1,0:T(8,128)(2,1)S(1)}, bf16[1024,128]{1,0:T(8,128)(2,1)S(1)}, u32[]{:S(2)}, u32[]{:S(2)}) %collective-permute-start.4) | collective-permute-done | bytes 262176 | tf_op jit(solution)/shard_map/ppermute | solution.py:243
  20.4 2.1 %collective-permute-start.6 = (bf16[768,128]{1,0:T(8,128)(2,1)S(1)}, bf16[768,128]{1,0:T(8,128)(2,1)S(1)}, u32[]{:S(2)}, u32[]{:S(2)}) collective-permute-start(bf16[768,128]{1,0:T(8,128)(2,1)S(1)} %constant_dynamic-update-slice_fusion.4), channel_id=1, source_target_pairs={{0,8},{4,12},{8,0},{12,4},{16,24},{20,28},{24,16},{28,20},{1,9},{5... | collective-permute-start | bytes 589832 | tf_op jit(solution)/shard_map/ppermute | solution.py:243
  22.6 1.6 %collective-permute-start.9 = (bf16[4,136,512]{2,1,0:T(8,128)(2,1)S(1)}, bf16[4,136,512]{2,1,0:T(8,128)(2,1)S(1)}, u32[]{:S(2)}, u32[]{:S(2)}) collective-permute-start(bf16[4,136,512]{2,1,0:T(8,128)(2,1)S(1)} %pad_maximum_fusion.refs_1_), channel_id=1, source_target_pairs={{0,2},{1,3},{2,0},{3,1},{4,6},{5,7},{6,4},{7,5},{8,10},{9,11},{10,... | collective-permute-start | bytes 1671176 | tf_op jit(solution)/shard_map/ppermute | solution.py:243
  24.2 1.9 %collective-permute-done.6 = bf16[768,128]{1,0:T(8,128)(2,1)S(1)} collective-permute-done((bf16[768,128]{1,0:T(8,128)(2,1)S(1)}, bf16[768,128]{1,0:T(8,128)(2,1)S(1)}, u32[]{:S(2)}, u32[]{:S(2)}) %collective-permute-start.6) | collective-permute-done | bytes 196640 | tf_op jit(solution)/shard_map/ppermute | solution.py:243
  26.3 3.2 %collective-permute-start.7 = (bf16[384,128]{1,0:T(8,128)(2,1)S(1)}, bf16[384,128]{1,0:T(8,128)(2,1)S(1)}, u32[]{:S(2)}, u32[]{:S(2)}) collective-permute-start(bf16[384,128]{1,0:T(8,128)(2,1)S(1)} %select_dynamic-update-slice_fusion), channel_id=1, source_target_pairs={{0,16},{4,20},{8,24},{12,28},{16,0},{20,4},{24,8},{28,12},{1,17},{... | collective-permute-start | bytes 294920 | tf_op jit(solution)/shard_map/ppermute | solution.py:243
  30.1 2.0 %collective-permute-done.7 = bf16[384,128]{1,0:T(8,128)(2,1)S(1)} collective-permute-done((bf16[384,128]{1,0:T(8,128)(2,1)S(1)}, bf16[384,128]{1,0:T(8,128)(2,1)S(1)}, u32[]{:S(2)}, u32[]{:S(2)}) %collective-permute-start.7) | collective-permute-done | bytes 98336 | tf_op jit(solution)/shard_map/ppermute | solution.py:243
  32.3 1.2 collective-permute-done.8
  33.4 4.9 %collective-permute-done.5.refs_3_.refs_2_ = bf16[3,136,512]{2,1,0:T(8,128)(2,1)S(1)} collective-permute-done((bf16[3,136,512]{2,1,0:T(8,128)(2,1)S(1)}, bf16[3,136,512]{2,1,0:T(8,128)(2,1)S(1)}, u32[]{:S(2)}, u32[]{:S(2)}) %collective-permute-start.5) | collective-permute-done | bytes 417824 | tf_op jit(solution)/shard_map/ppermute | solution.py:243
  38.4 1.5 %collective-permute-start.13 = (f32[32,128]{1,0:T(8,128)S(1)}, f32[32,128]{1,0:T(8,128)S(1)}, u32[]{:S(2)}, u32[]{:S(2)}) collective-permute-start(f32[32,128]{1,0:T(8,128)S(1)} %add.181), channel_id=1, source_target_pairs={{0,2},{1,3},{2,0},{3,1},{4,6},{5,7},{6,4},{7,5},{8,10},{9,11},{10,... | collective-permute-start | bytes 49160 | tf_op jit(solution)/shard_map/ppermute | solution.py:243
  42.5 4.2 %collective-permute-done.14 = bf16[1,32,128]{2,1,0:T(8,128)(2,1)S(1)} collective-permute-done((bf16[1,32,128]{2,1,0:T(8,128)(2,1)S(1)}, bf16[1,32,128]{2,1,0:T(8,128)(2,1)S(1)}, u32[]{:S(2)}, u32[]{:S(2)}) %collective-permute-start.14) | collective-permute-done | bytes 8224 | tf_op jit(solution)/shard_map/ppermute | solution.py:243
  47.0 1.6 %shard_map.109 = (bf16[8,512,128]{2,1,0:T(8,128)(2,1)S(1)}, bf16[8,128,512]{2,1,0:T(8,128)(2,1)S(1)}, f32[16,256,128]{2,1,0:T(8,128)S(1)}) custom-call(s32[9]{0:T(128)S(1)} %pad_add_fusion.1.scalar_ref, bf16[1,136,512]{2,1,0:T(8,128)(2,1)S(1)} %fusion.43.refs_0_, bf16[3,136,512]{2,1,0:T(8,128)(2,1)S(1)} %pad_maximum_fusion.1.refs_1_, ...), custom_call_target="tpu_custom_call" | custom-call | flops 1000000 | bytes 1000 | tf_op jit(solution)/shard_map/pallas_call | solution.py:75
  48.6 1.8 %collective-permute-done.15 = bf16[2,32,128]{2,1,0:T(8,128)(2,1)S(1)} collective-permute-done((bf16[2,32,128]{2,1,0:T(8,128)(2,1)S(1)}, bf16[2,32,128]{2,1,0:T(8,128)(2,1)S(1)}, u32[]{:S(2)}, u32[]{:S(2)}) %collective-permute-start.15) | collective-permute-done | bytes 16416 | tf_op jit(solution)/shard_map/ppermute | solution.py:243
  50.4 7.7 %shard_map.110.refs_9_ = f32[16,256,256]{2,1,0:T(8,128)S(1)} custom-call(s32[9]{0:T(128)S(1)} %pad_add_fusion.scalar_ref, bf16[128,2048]{1,0:T(8,128)(2,1)S(1)} %copy-done.1, bf16[4,136,512]{2,1,0:T(8,128)(2,1)S(1)} %pad_maximum_fusion.refs_1_, bf16[3,136,512]{2,1,0:T(8,128)(2,1)S(1)} %collective-permute-done.5.refs_3_.refs_2_, ...), custom_call_target="tpu_custom_call" | custom-call | flops 1000000 | bytes 1000 | tf_op jit(solution)/shard_map/pallas_call | solution.py:186
  58.8 3.3 %collective-permute-done.18 = bf16[4,32,128]{2,1,0:T(8,128)(2,1)S(1)} collective-permute-done((bf16[4,32,128]{2,1,0:T(8,128)(2,1)S(1)}, bf16[4,32,128]{2,1,0:T(8,128)(2,1)S(1)}, u32[]{:S(2)}, u32[]{:S(2)}) %collective-permute-start.18) | collective-permute-done | bytes 32800 | tf_op jit(solution)/shard_map/ppermute | solution.py:243
  62.2 9.1 %shard_map.111.hidden_ref = bf16[16,256,128]{2,1,0:T(8,128)(2,1)S(1)} custom-call(s32[9]{0:T(128)S(1)} %pad_add_fusion.scalar_ref, bf16[128,2048]{1,0:T(8,128)(2,1)S(1)} %copy-done.1, bf16[4,136,512]{2,1,0:T(8,128)(2,1)S(1)} %collective-permute-done.9.refs_1_, bf16[3,136,512]{2,1,0:T(8,128)(2,1)S(1)} %collective-permute-done.12.refs_2_, ...), custom_call_target="tpu_custom_call" | custom-call | flops 1000000 | bytes 1000 | tf_op jit(solution)/shard_map/pallas_call | solution.py:186
  71.4 6.3 %shard_map.112 = (bf16[8,128,256]{2,1,0:T(8,128)(2,1)S(1)}, f32[8,128,256]{2,1,0:T(8,128)S(1)}, bf16[8,128,256]{2,1,0:T(8,128)(2,1)S(1)}, f32[8,128,256]{2,1,0:T(8,128)S(1)}) custom-call(s32[9]{0:T(128)S(1)} %pad_add_fusion.scalar_ref, bf16[16,2048,128]{2,1,0:T(8,128)(2,1)} %down_hbm.3, bf16[16,256,128]{2,1,0:T(8,128)(2,1)S(1)} %shard_map.111.hidden_ref, ...), custom_call_target="tpu_custom_call" | custom-call | flops 1000000 | bytes 1000 | tf_op jit(solution)/shard_map/pallas_call | solution.py:226
  78.3 1.4 %collective-permute-done.20 = bf16[8,128,256]{2,1,0:T(8,128)(2,1)S(1)} collective-permute-done((bf16[8,128,256]{2,1,0:T(8,128)(2,1)S(1)}, bf16[8,128,256]{2,1,0:T(8,128)(2,1)S(1)}, u32[]{:S(2)}, u32[]{:S(2)}) %collective-permute-start.20) | collective-permute-done | bytes 524320 | tf_op jit(solution)/shard_map/ppermute | solution.py:243
  80.6 1.6 %collective-permute-start.21 = (bf16[4,128,256]{2,1,0:T(8,128)(2,1)S(1)}, bf16[4,128,256]{2,1,0:T(8,128)(2,1)S(1)}, u32[]{:S(2)}, u32[]{:S(2)}) collective-permute-start(bf16[4,128,256]{2,1,0:T(8,128)(2,1)S(1)} %get-tuple-element.78), channel_id=1, source_target_pairs={{0,2},{1,3},{2,0},{3,1},{4,6},{5,7},{6,4},{7,5},{8,10},{9,11},{10,... | collective-permute-start | bytes 786440 | tf_op jit(solution)/shard_map/ppermute | solution.py:243
  82.8 6.3 %shard_map.113 = (bf16[8,128,256]{2,1,0:T(8,128)(2,1)S(1)}, f32[8,128,256]{2,1,0:T(8,128)S(1)}, bf16[8,128,256]{2,1,0:T(8,128)(2,1)S(1)}, f32[8,128,256]{2,1,0:T(8,128)S(1)}) custom-call(s32[9]{0:T(128)S(1)} %pad_add_fusion.scalar_ref, bf16[16,2048,128]{2,1,0:T(8,128)(2,1)} %down_hbm.3, bf16[16,256,128]{2,1,0:T(8,128)(2,1)S(1)} %shard_map.111.hidden_ref, ...), custom_call_target="tpu_custom_call" | custom-call | flops 1000000 | bytes 1000 | tf_op jit(solution)/shard_map/pallas_call | solution.py:226
  89.1 1.2 %collective-permute-done.22 = bf16[4,128,256]{2,1,0:T(8,128)(2,1)S(1)} collective-permute-done((bf16[4,128,256]{2,1,0:T(8,128)(2,1)S(1)}, bf16[4,128,256]{2,1,0:T(8,128)(2,1)S(1)}, u32[]{:S(2)}, u32[]{:S(2)}) %collective-permute-start.22) | collective-permute-done | bytes 262176 | tf_op jit(solution)/shard_map/ppermute | solution.py:243
  91.2 1.6 %collective-permute-start.31 = (bf16[4,128,256]{2,1,0:T(8,128)(2,1)S(1)}, bf16[4,128,256]{2,1,0:T(8,128)(2,1)S(1)}, u32[]{:S(2)}, u32[]{:S(2)}) collective-permute-start(bf16[4,128,256]{2,1,0:T(8,128)(2,1)S(1)} %add_convert_fusion.1), channel_id=1, source_target_pairs={{0,2},{1,3},{2,0},{3,1},{4,6},{5,7},{6,4},{7,5},{8,10},{9,11},{10,... | collective-permute-start | bytes 786440 | tf_op jit(solution)/shard_map/ppermute | solution.py:243
  93.7 1.6 %collective-permute-start.30 = (bf16[4,128,256]{2,1,0:T(8,128)(2,1)S(1)}, bf16[4,128,256]{2,1,0:T(8,128)(2,1)S(1)}, u32[]{:S(2)}, u32[]{:S(2)}) collective-permute-start(bf16[4,128,256]{2,1,0:T(8,128)(2,1)S(1)} %slice.357), channel_id=1, source_target_pairs={{0,4},{4,0},{8,12},{12,8},{16,20},{20,16},{24,28},{28,24},{1,5},{5... | collective-permute-start | bytes 786440 | tf_op jit(solution)/shard_map/ppermute | solution.py:243
  95.3 4.2 %collective-permute-done.24 = bf16[4,128,256]{2,1,0:T(8,128)(2,1)S(1)} collective-permute-done((bf16[4,128,256]{2,1,0:T(8,128)(2,1)S(1)}, bf16[4,128,256]{2,1,0:T(8,128)(2,1)S(1)}, u32[]{:S(2)}, u32[]{:S(2)}) %collective-permute-start.24) | collective-permute-done | bytes 262176 | tf_op jit(solution)/shard_map/ppermute | solution.py:243
  99.5 2.7 %collective-permute-done.25 = bf16[4,128,256]{2,1,0:T(8,128)(2,1)S(1)} collective-permute-done((bf16[4,128,256]{2,1,0:T(8,128)(2,1)S(1)}, bf16[4,128,256]{2,1,0:T(8,128)(2,1)S(1)}, u32[]{:S(2)}, u32[]{:S(2)}) %collective-permute-start.25) | collective-permute-done | bytes 262176 | tf_op jit(solution)/shard_map/ppermute | solution.py:243
  102.7 1.2 %collective-permute-start.27 = (bf16[128,256]{1,0:T(8,128)(2,1)S(1)}, bf16[128,256]{1,0:T(8,128)(2,1)S(1)}, u32[]{:S(2)}, u32[]{:S(2)}) collective-permute-start(bf16[128,256]{1,0:T(8,128)(2,1)S(1)} %get-tuple-element.83), channel_id=1, source_target_pairs={{0,16},{4,20},{8,24},{12,28},{16,0},{20,4},{24,8},{28,12},{1,17},{... | collective-permute-start | bytes 196616 | tf_op jit(solution)/shard_map/ppermute | solution.py:243
  103.8 2.9 %collective-permute-start.28 = (bf16[128,256]{1,0:T(8,128)(2,1)S(1)}, bf16[128,256]{1,0:T(8,128)(2,1)S(1)}, u32[]{:S(2)}, u32[]{:S(2)}) collective-permute-start(bf16[128,256]{1,0:T(8,128)(2,1)S(1)} %get-tuple-element.82), channel_id=1, source_target_pairs={{0,24},{4,28},{8,16},{12,20},{16,8},{20,12},{24,0},{28,4},{1,25},{... | collective-permute-start | bytes 196616 | tf_op jit(solution)/shard_map/ppermute | solution.py:243
  107.3 1.2 %collective-permute-start.33 = (bf16[128,256]{1,0:T(8,128)(2,1)S(1)}, bf16[128,256]{1,0:T(8,128)(2,1)S(1)}, u32[]{:S(2)}, u32[]{:S(2)}) collective-permute-start(bf16[128,256]{1,0:T(8,128)(2,1)S(1)} %get-tuple-element.86), channel_id=1, source_target_pairs={{0,16},{4,20},{8,24},{12,28},{16,0},{20,4},{24,8},{28,12},{1,17},{... | collective-permute-start | bytes 196616 | tf_op jit(solution)/shard_map/ppermute | solution.py:243
  108.5 2.9 %collective-permute-start.34 = (bf16[128,256]{1,0:T(8,128)(2,1)S(1)}, bf16[128,256]{1,0:T(8,128)(2,1)S(1)}, u32[]{:S(2)}, u32[]{:S(2)}) collective-permute-start(bf16[128,256]{1,0:T(8,128)(2,1)S(1)} %get-tuple-element.85), channel_id=1, source_target_pairs={{0,24},{4,28},{8,16},{12,20},{16,8},{20,12},{24,0},{28,4},{1,25},{... | collective-permute-start | bytes 196616 | tf_op jit(solution)/shard_map/ppermute | solution.py:243
  111.7 3.5 %collective-permute-done.33 = bf16[128,256]{1,0:T(8,128)(2,1)S(1)} collective-permute-done((bf16[128,256]{1,0:T(8,128)(2,1)S(1)}, bf16[128,256]{1,0:T(8,128)(2,1)S(1)}, u32[]{:S(2)}, u32[]{:S(2)}) %collective-permute-start.33) | collective-permute-done | bytes 65568 | tf_op jit(solution)/shard_map/ppermute | solution.py:243
  (123 shorter events, 18.4 us)
Async XLA Ops:
  2.4 16.9 %collective-permute-start = (bf16[136,512]{1,0:T(8,128)(2,1)S(1)}, bf16[136,512]{1,0:T(8,128)(2,1)S(1)}, u32[]{:S(2)}, u32[]{:S(2)}) collective-permute-start(bf16[136,512]{1,0:T(8,128)(2,1)S(1)} %maximum_maximum_fusion), channel_id=1, source_target_pairs={{0,4},{4,0},{8,12},{12,8},{16,20},{20,16},{24,28},{28,24},{1,5},{5... | collective-permute-start | bytes 417800 | tf_op jit(solution)/shard_map/ppermute | solution.py:243
  5.4 13.9 %collective-permute-start.1 = (bf16[136,512]{1,0:T(8,128)(2,1)S(1)}, bf16[136,512]{1,0:T(8,128)(2,1)S(1)}, u32[]{:S(2)}, u32[]{:S(2)}) collective-permute-start(bf16[136,512]{1,0:T(8,128)(2,1)S(1)} %maximum_maximum_fusion), channel_id=1, source_target_pairs={{0,8},{4,12},{8,0},{12,4},{16,24},{20,28},{24,16},{28,20},{1,9},{5... | collective-permute-start | bytes 417800 | tf_op jit(solution)/shard_map/ppermute | solution.py:243
  7.0 13.3 %collective-permute-start.2 = (bf16[136,512]{1,0:T(8,128)(2,1)S(1)}, bf16[136,512]{1,0:T(8,128)(2,1)S(1)}, u32[]{:S(2)}, u32[]{:S(2)}) collective-permute-start(bf16[136,512]{1,0:T(8,128)(2,1)S(1)} %maximum_maximum_fusion), channel_id=1, source_target_pairs={{0,16},{4,20},{8,24},{12,28},{16,0},{20,4},{24,8},{28,12},{1,17},{... | collective-permute-start | bytes 417800 | tf_op jit(solution)/shard_map/ppermute | solution.py:243
  9.6 10.7 %collective-permute-start.3 = (bf16[136,512]{1,0:T(8,128)(2,1)S(1)}, bf16[136,512]{1,0:T(8,128)(2,1)S(1)}, u32[]{:S(2)}, u32[]{:S(2)}) collective-permute-start(bf16[136,512]{1,0:T(8,128)(2,1)S(1)} %maximum_maximum_fusion), channel_id=1, source_target_pairs={{0,24},{4,28},{8,16},{12,20},{16,8},{20,12},{24,0},{28,4},{1,25},{... | collective-permute-start | bytes 417800 | tf_op jit(solution)/shard_map/ppermute | solution.py:243
  12.2 7.1 %collective-permute-start.4 = (bf16[1024,128]{1,0:T(8,128)(2,1)S(1)}, bf16[1024,128]{1,0:T(8,128)(2,1)S(1)}, u32[]{:S(2)}, u32[]{:S(2)}) collective-permute-start(bf16[1024,128]{1,0:T(8,128)(2,1)S(1)} %slice_dynamic-update-slice_fusion), channel_id=1, source_target_pairs={{0,4},{4,0},{8,12},{12,8},{16,20},{20,16},{24,28},{28,24},{1,5},{5... | collective-permute-start | bytes 786440 | tf_op jit(solution)/shard_map/ppermute | solution.py:243
  20.4 5.8 %collective-permute-start.6 = (bf16[768,128]{1,0:T(8,128)(2,1)S(1)}, bf16[768,128]{1,0:T(8,128)(2,1)S(1)}, u32[]{:S(2)}, u32[]{:S(2)}) collective-permute-start(bf16[768,128]{1,0:T(8,128)(2,1)S(1)} %constant_dynamic-update-slice_fusion.4), channel_id=1, source_target_pairs={{0,8},{4,12},{8,0},{12,4},{16,24},{20,28},{24,16},{28,20},{1,9},{5... | collective-permute-start | bytes 589832 | tf_op jit(solution)/shard_map/ppermute | solution.py:243
  22.6 15.7 %collective-permute-start.9 = (bf16[4,136,512]{2,1,0:T(8,128)(2,1)S(1)}, bf16[4,136,512]{2,1,0:T(8,128)(2,1)S(1)}, u32[]{:S(2)}, u32[]{:S(2)}) collective-permute-start(bf16[4,136,512]{2,1,0:T(8,128)(2,1)S(1)} %pad_maximum_fusion.refs_1_), channel_id=1, source_target_pairs={{0,2},{1,3},{2,0},{3,1},{4,6},{5,7},{6,4},{7,5},{8,10},{9,11},{10,... | collective-permute-start | bytes 1671176 | tf_op jit(solution)/shard_map/ppermute | solution.py:243
  26.3 5.8 %collective-permute-start.7 = (bf16[384,128]{1,0:T(8,128)(2,1)S(1)}, bf16[384,128]{1,0:T(8,128)(2,1)S(1)}, u32[]{:S(2)}, u32[]{:S(2)}) collective-permute-start(bf16[384,128]{1,0:T(8,128)(2,1)S(1)} %select_dynamic-update-slice_fusion), channel_id=1, source_target_pairs={{0,16},{4,20},{8,24},{12,28},{16,0},{20,4},{24,8},{28,12},{1,17},{... | collective-permute-start | bytes 294920 | tf_op jit(solution)/shard_map/ppermute | solution.py:243
  29.5 8.8 %collective-permute-start.5 = (bf16[3,136,512]{2,1,0:T(8,128)(2,1)S(1)}, bf16[3,136,512]{2,1,0:T(8,128)(2,1)S(1)}, u32[]{:S(2)}, u32[]{:S(2)}) collective-permute-start(bf16[3,136,512]{2,1,0:T(8,128)(2,1)S(1)} %pad_maximum_fusion.1.refs_1_), channel_id=1, source_target_pairs={{0,4},{4,0},{8,12},{12,8},{16,20},{20,16},{24,28},{28,24},{1,5},{5... | collective-permute-start | bytes 1253384 | tf_op jit(solution)/shard_map/ppermute | solution.py:243
  38.4 3.7 %collective-permute-start.13 = (f32[32,128]{1,0:T(8,128)S(1)}, f32[32,128]{1,0:T(8,128)S(1)}, u32[]{:S(2)}, u32[]{:S(2)}) collective-permute-start(f32[32,128]{1,0:T(8,128)S(1)} %add.181), channel_id=1, source_target_pairs={{0,2},{1,3},{2,0},{3,1},{4,6},{5,7},{6,4},{7,5},{8,10},{9,11},{10,... | collective-permute-start | bytes 49160 | tf_op jit(solution)/shard_map/ppermute | solution.py:243
  39.9 10.5 %collective-permute-start.10 = (bf16[4,136,512]{2,1,0:T(8,128)(2,1)S(1)}, bf16[4,136,512]{2,1,0:T(8,128)(2,1)S(1)}, u32[]{:S(2)}, u32[]{:S(2)}) collective-permute-start(bf16[4,136,512]{2,1,0:T(8,128)(2,1)S(1)} %pad_maximum_fusion.refs_1_), channel_id=1, source_target_pairs={{0,1},{1,0},{2,3},{3,2},{4,5},{5,4},{6,7},{7,6},{8,9},{9,8},{10,11... | collective-permute-start | bytes 1671176 | tf_op jit(solution)/shard_map/ppermute | solution.py:243
  39.9 10.5 %collective-permute-start.11 = (bf16[3,136,512]{2,1,0:T(8,128)(2,1)S(1)}, bf16[3,136,512]{2,1,0:T(8,128)(2,1)S(1)}, u32[]{:S(2)}, u32[]{:S(2)}) collective-permute-start(bf16[3,136,512]{2,1,0:T(8,128)(2,1)S(1)} %collective-permute-done.5.refs_3_.refs_2_), channel_id=1, source_target_pairs={{0,1},{1,0},{2,3},{3,2},{4,5},{5,4},{6,7},{7,6},{8,9},{9,8},{10,11... | collective-permute-start | bytes 1253384 | tf_op jit(solution)/shard_map/ppermute | solution.py:243
  40.4 17.7 %collective-permute-start.12 = (bf16[3,136,512]{2,1,0:T(8,128)(2,1)S(1)}, bf16[3,136,512]{2,1,0:T(8,128)(2,1)S(1)}, u32[]{:S(2)}, u32[]{:S(2)}) collective-permute-start(bf16[3,136,512]{2,1,0:T(8,128)(2,1)S(1)} %collective-permute-done.5.refs_3_.refs_2_), channel_id=1, source_target_pairs={{0,2},{1,3},{2,0},{3,1},{4,6},{5,7},{6,4},{7,5},{8,10},{9,11},{10,... | collective-permute-start | bytes 1253384 | tf_op jit(solution)/shard_map/ppermute | solution.py:243
  41.0 21.2 %collective-permute-start.16 = (bf16[4,136,512]{2,1,0:T(8,128)(2,1)S(1)}, bf16[4,136,512]{2,1,0:T(8,128)(2,1)S(1)}, u32[]{:S(2)}, u32[]{:S(2)}) collective-permute-start(bf16[4,136,512]{2,1,0:T(8,128)(2,1)S(1)} %collective-permute-done.9.refs_1_), channel_id=1, source_target_pairs={{0,1},{1,0},{2,3},{3,2},{4,5},{5,4},{6,7},{7,6},{8,9},{9,8},{10,11... | collective-permute-start | bytes 1671176 | tf_op jit(solution)/shard_map/ppermute | solution.py:243
  42.1 4.5 %collective-permute-start.14 = (bf16[1,32,128]{2,1,0:T(8,128)(2,1)S(1)}, bf16[1,32,128]{2,1,0:T(8,128)(2,1)S(1)}, u32[]{:S(2)}, u32[]{:S(2)}) collective-permute-start(bf16[1,32,128]{2,1,0:T(8,128)(2,1)S(1)} %fusion.28), channel_id=1, source_target_pairs={{0,16},{4,20},{8,24},{12,28},{16,0},{20,4},{24,8},{28,12},{1,17},{... | collective-permute-start | bytes 24584 | tf_op jit(solution)/shard_map/ppermute | solution.py:243
  46.7 3.7 %collective-permute-start.15 = (bf16[2,32,128]{2,1,0:T(8,128)(2,1)S(1)}, bf16[2,32,128]{2,1,0:T(8,128)(2,1)S(1)}, u32[]{:S(2)}, u32[]{:S(2)}) collective-permute-start(bf16[2,32,128]{2,1,0:T(8,128)(2,1)S(1)} %pad_maximum_fusion.5), channel_id=1, source_target_pairs={{0,8},{4,12},{8,0},{12,4},{16,24},{20,28},{24,16},{28,20},{1,9},{5... | collective-permute-start | bytes 49160 | tf_op jit(solution)/shard_map/ppermute | solution.py:243
  58.2 4.0 %collective-permute-start.18 = (bf16[4,32,128]{2,1,0:T(8,128)(2,1)S(1)}, bf16[4,32,128]{2,1,0:T(8,128)(2,1)S(1)}, u32[]{:S(2)}, u32[]{:S(2)}) collective-permute-start(bf16[4,32,128]{2,1,0:T(8,128)(2,1)S(1)} %pad_maximum_fusion.4), channel_id=1, source_target_pairs={{0,4},{4,0},{8,12},{12,8},{16,20},{20,16},{24,28},{28,24},{1,5},{5... | collective-permute-start | bytes 98312 | tf_op jit(solution)/shard_map/ppermute | solution.py:243
  58.8 3.4 %collective-permute-start.17 = (bf16[3,136,512]{2,1,0:T(8,128)(2,1)S(1)}, bf16[3,136,512]{2,1,0:T(8,128)(2,1)S(1)}, u32[]{:S(2)}, u32[]{:S(2)}) collective-permute-start(bf16[3,136,512]{2,1,0:T(8,128)(2,1)S(1)} %collective-permute-done.12.refs_2_), channel_id=1, source_target_pairs={{0,1},{1,0},{2,3},{3,2},{4,5},{5,4},{6,7},{7,6},{8,9},{9,8},{10,11... | collective-permute-start | bytes 1253384 | tf_op jit(solution)/shard_map/ppermute | solution.py:243
  77.8 2.6 %collective-permute-start.19 = (bf16[8,128,256]{2,1,0:T(8,128)(2,1)S(1)}, bf16[8,128,256]{2,1,0:T(8,128)(2,1)S(1)}, u32[]{:S(2)}, u32[]{:S(2)}) collective-permute-start(bf16[8,128,256]{2,1,0:T(8,128)(2,1)S(1)} %get-tuple-element.57), channel_id=1, source_target_pairs={{0,1},{1,0},{2,3},{3,2},{4,5},{5,4},{6,7},{7,6},{8,9},{9,8},{10,11... | collective-permute-start | bytes 1572872 | tf_op jit(solution)/shard_map/ppermute | solution.py:243
  80.6 8.5 %collective-permute-start.21 = (bf16[4,128,256]{2,1,0:T(8,128)(2,1)S(1)}, bf16[4,128,256]{2,1,0:T(8,128)(2,1)S(1)}, u32[]{:S(2)}, u32[]{:S(2)}) collective-permute-start(bf16[4,128,256]{2,1,0:T(8,128)(2,1)S(1)} %get-tuple-element.78), channel_id=1, source_target_pairs={{0,2},{1,3},{2,0},{3,1},{4,6},{5,7},{6,4},{7,5},{8,10},{9,11},{10,... | collective-permute-start | bytes 786440 | tf_op jit(solution)/shard_map/ppermute | solution.py:243
  82.2 8.1 %collective-permute-start.22 = (bf16[4,128,256]{2,1,0:T(8,128)(2,1)S(1)}, bf16[4,128,256]{2,1,0:T(8,128)(2,1)S(1)}, u32[]{:S(2)}, u32[]{:S(2)}) collective-permute-start(bf16[4,128,256]{2,1,0:T(8,128)(2,1)S(1)} %slice.358), channel_id=1, source_target_pairs={{0,4},{4,0},{8,12},{12,8},{16,20},{20,16},{24,28},{28,24},{1,5},{5... | collective-permute-start | bytes 786440 | tf_op jit(solution)/shard_map/ppermute | solution.py:243
  90.4 9.1 %collective-permute-start.24 = (bf16[4,128,256]{2,1,0:T(8,128)(2,1)S(1)}, bf16[4,128,256]{2,1,0:T(8,128)(2,1)S(1)}, u32[]{:S(2)}, u32[]{:S(2)}) collective-permute-start(bf16[4,128,256]{2,1,0:T(8,128)(2,1)S(1)} %get-tuple-element.77), channel_id=1, source_target_pairs={{0,2},{1,3},{2,0},{3,1},{4,6},{5,7},{6,4},{7,5},{8,10},{9,11},{10,... | collective-permute-start | bytes 786440 | tf_op jit(solution)/shard_map/ppermute | solution.py:243
  90.9 2.6 %collective-permute-start.29 = (bf16[8,128,256]{2,1,0:T(8,128)(2,1)S(1)}, bf16[8,128,256]{2,1,0:T(8,128)(2,1)S(1)}, u32[]{:S(2)}, u32[]{:S(2)}) collective-permute-start(bf16[8,128,256]{2,1,0:T(8,128)(2,1)S(1)} %get-tuple-element.71), channel_id=1, source_target_pairs={{0,1},{1,0},{2,3},{3,2},{4,5},{5,4},{6,7},{7,6},{8,9},{9,8},{10,11... | collective-permute-start | bytes 1572872 | tf_op jit(solution)/shard_map/ppermute | solution.py:243
  91.2 15.6 %collective-permute-start.31 = (bf16[4,128,256]{2,1,0:T(8,128)(2,1)S(1)}, bf16[4,128,256]{2,1,0:T(8,128)(2,1)S(1)}, u32[]{:S(2)}, u32[]{:S(2)}) collective-permute-start(bf16[4,128,256]{2,1,0:T(8,128)(2,1)S(1)} %add_convert_fusion.1), channel_id=1, source_target_pairs={{0,2},{1,3},{2,0},{3,1},{4,6},{5,7},{6,4},{7,5},{8,10},{9,11},{10,... | collective-permute-start | bytes 786440 | tf_op jit(solution)/shard_map/ppermute | solution.py:243
  92.9 9.2 %collective-permute-start.25 = (bf16[4,128,256]{2,1,0:T(8,128)(2,1)S(1)}, bf16[4,128,256]{2,1,0:T(8,128)(2,1)S(1)}, u32[]{:S(2)}, u32[]{:S(2)}) collective-permute-start(bf16[4,128,256]{2,1,0:T(8,128)(2,1)S(1)} %fusion.1), channel_id=1, source_target_pairs={{0,4},{4,0},{8,12},{12,8},{16,20},{20,16},{24,28},{28,24},{1,5},{5... | collective-permute-start | bytes 786440 | tf_op jit(solution)/shard_map/ppermute | solution.py:243
  93.7 13.2 %collective-permute-start.30 = (bf16[4,128,256]{2,1,0:T(8,128)(2,1)S(1)}, bf16[4,128,256]{2,1,0:T(8,128)(2,1)S(1)}, u32[]{:S(2)}, u32[]{:S(2)}) collective-permute-start(bf16[4,128,256]{2,1,0:T(8,128)(2,1)S(1)} %slice.357), channel_id=1, source_target_pairs={{0,4},{4,0},{8,12},{12,8},{16,20},{20,16},{24,28},{28,24},{1,5},{5... | collective-permute-start | bytes 786440 | tf_op jit(solution)/shard_map/ppermute | solution.py:243
  102.3 6.2 %collective-permute-start.26 = (bf16[128,256]{1,0:T(8,128)(2,1)S(1)}, bf16[128,256]{1,0:T(8,128)(2,1)S(1)}, u32[]{:S(2)}, u32[]{:S(2)}) collective-permute-start(bf16[128,256]{1,0:T(8,128)(2,1)S(1)} %get-tuple-element.81), channel_id=1, source_target_pairs={{0,8},{4,12},{8,0},{12,4},{16,24},{20,28},{24,16},{28,20},{1,9},{5... | collective-permute-start | bytes 196616 | tf_op jit(solution)/shard_map/ppermute | solution.py:243
  102.7 8.8 %collective-permute-start.27 = (bf16[128,256]{1,0:T(8,128)(2,1)S(1)}, bf16[128,256]{1,0:T(8,128)(2,1)S(1)}, u32[]{:S(2)}, u32[]{:S(2)}) collective-permute-start(bf16[128,256]{1,0:T(8,128)(2,1)S(1)} %get-tuple-element.83), channel_id=1, source_target_pairs={{0,16},{4,20},{8,24},{12,28},{16,0},{20,4},{24,8},{28,12},{1,17},{... | collective-permute-start | bytes 196616 | tf_op jit(solution)/shard_map/ppermute | solution.py:243
  103.8 7.6 %collective-permute-start.28 = (bf16[128,256]{1,0:T(8,128)(2,1)S(1)}, bf16[128,256]{1,0:T(8,128)(2,1)S(1)}, u32[]{:S(2)}, u32[]{:S(2)}) collective-permute-start(bf16[128,256]{1,0:T(8,128)(2,1)S(1)} %get-tuple-element.82), channel_id=1, source_target_pairs={{0,24},{4,28},{8,16},{12,20},{16,8},{20,12},{24,0},{28,4},{1,25},{... | collective-permute-start | bytes 196616 | tf_op jit(solution)/shard_map/ppermute | solution.py:243
  107.0 4.8 %collective-permute-start.32 = (bf16[128,256]{1,0:T(8,128)(2,1)S(1)}, bf16[128,256]{1,0:T(8,128)(2,1)S(1)}, u32[]{:S(2)}, u32[]{:S(2)}) collective-permute-start(bf16[128,256]{1,0:T(8,128)(2,1)S(1)} %get-tuple-element.84), channel_id=1, source_target_pairs={{0,8},{4,12},{8,0},{12,4},{16,24},{20,28},{24,16},{28,20},{1,9},{5... | collective-permute-start | bytes 196616 | tf_op jit(solution)/shard_map/ppermute | solution.py:243
  107.3 7.9 %collective-permute-start.33 = (bf16[128,256]{1,0:T(8,128)(2,1)S(1)}, bf16[128,256]{1,0:T(8,128)(2,1)S(1)}, u32[]{:S(2)}, u32[]{:S(2)}) collective-permute-start(bf16[128,256]{1,0:T(8,128)(2,1)S(1)} %get-tuple-element.86), channel_id=1, source_target_pairs={{0,16},{4,20},{8,24},{12,28},{16,0},{20,4},{24,8},{28,12},{1,17},{... | collective-permute-start | bytes 196616 | tf_op jit(solution)/shard_map/ppermute | solution.py:243
  108.5 6.8 %collective-permute-start.34 = (bf16[128,256]{1,0:T(8,128)(2,1)S(1)}, bf16[128,256]{1,0:T(8,128)(2,1)S(1)}, u32[]{:S(2)}, u32[]{:S(2)}) collective-permute-start(bf16[128,256]{1,0:T(8,128)(2,1)S(1)} %get-tuple-element.85), channel_id=1, source_target_pairs={{0,24},{4,28},{8,16},{12,20},{16,8},{20,12},{24,0},{28,4},{1,25},{... | collective-permute-start | bytes 196616 | tf_op jit(solution)/shard_map/ppermute | solution.py:243
  (5 other events, 66.6 us)
